TPU v7x, 32 devices: a whole 2x2x4 slice. The times are simulated.
32 devices in a mesh: patch: 8 (over z, y), coarse: 4 (over x, core).
Axes of the slice: x: 2, y: 2, z: 4, core: 2. Of those that a mesh axis runs over, the one named last changes fastest.
Arguments:
- residual: bfloat16 [2, 2, 49152, 256], P(None, None, ('patch', 'coarse')), may hold values from -6 to 6
- patch_inv: bfloat16 [128, 2, 1024, 1024], P(('patch', 'coarse')), may hold values from -0.1875 to 0.1875
- coarse_basis: bfloat16 [128, 2, 1024, 32], P(('patch', 'coarse')), may hold values from -0.1875 to 0.1875
- coarse_inv: bfloat16 [64, 2, 32, 32], P('coarse'), may hold values from -1 to 1
- patch_slots: int32 [128, 512], P(('patch', 'coarse')), may hold values from 0 to 1791, as said below
- send_rows: int32 [32, 2, 128], P(('patch', 'coarse')), may hold values from 0 to 1535, as said below
- coarse_block: int32 [128], P(('patch', 'coarse')), may hold values from 0 to 63
Outputs:
- correction: bfloat16 [2, 2, 49152, 256], P(None, None, ('patch', 'coarse'))
Inputs may be any that keep to these rules, and one draw needn't show every extreme that they name: `send_rows`: within each of the two blocks of a device the 128 rows are distinct. `patch_slots`: the 512 positions of a patch are distinct; they hold its device's rows (p mod 4) * 384 to (p mod 4 + 1) * 384 - 1, 64 positions of 1536 or more, and other rows of its device below 1536; each position of 1536 or more is used by exactly one patch of the device.
All inputs are finite; a program needn't handle non-finite values.
Results may differ from a plain program's by a relative error of at most 0.006.
Values may be sent and summed in bfloat16 or wider, within the bound.
No kernel may reach another device: no remote copies, remote signals or barrier semaphores. Data moves between devices by JAX's collectives and lax.ppermute only.
A program may use at most 128 MiB of HBM per device.

v0:
```python
import jax
import jax.numpy as jnp
from jax import lax
from jax.sharding import PartitionSpec as P


def passed_along(value, axis, steps):
    count = lax.axis_size(axis)
    pairs = [(source, (source + steps) % count) for source in range(count)]
    return lax.ppermute(value, axis, pairs)


def spread_rows(selector, terms, form):
    upper_part = terms.astype(jnp.bfloat16)
    lower_part = (terms - upper_part.astype(jnp.float32)).astype(jnp.bfloat16)
    first = jnp.einsum(form, selector, upper_part, preferred_element_type=jnp.float32)
    return first + jnp.einsum(form, selector, lower_part, preferred_element_type=jnp.float32)


def per_device(residual, patch_inv, coarse_basis, coarse_inv, patch_slots, send_rows, coarse_block):
    wave_count = residual.shape[0]
    node_rows = residual.shape[2]
    patches = patch_inv.shape[0]
    patch_nodes = patch_inv.shape[2] // 2
    coarse_width = coarse_basis.shape[3]
    slot_rows = send_rows.shape[2]
    ext_rows = node_rows + 2 * slot_rows
    blocks_all = coarse_inv.shape[0] * lax.axis_size("coarse")
    highest = lax.Precision.HIGHEST
    node_ids = jnp.arange(node_rows, dtype=jnp.int32)
    up_select = (send_rows[0, 0][:, None] == node_ids[None, :]).astype(jnp.bfloat16)
    down_select = (send_rows[0, 1][:, None] == node_ids[None, :]).astype(jnp.bfloat16)
    upward = jnp.einsum(
        "kn,wqnr->wqkr", up_select, residual, preferred_element_type=jnp.float32
    ).astype(jnp.bfloat16)
    downward = jnp.einsum(
        "kn,wqnr->wqkr", down_select, residual, preferred_element_type=jnp.float32
    ).astype(jnp.bfloat16)
    from_below = passed_along(upward, ("patch", "coarse"), 1)
    from_above = passed_along(downward, ("patch", "coarse"), -1)
    extended = jnp.concatenate([residual, from_below, from_above], axis=2)
    ext_select = (
        patch_slots[:, :, None] == jnp.arange(ext_rows, dtype=jnp.int32)[None, None, :]
    ).astype(jnp.bfloat16)
    gathered = jnp.einsum(
        "pne,wqer->wqpnr", ext_select, extended, preferred_element_type=jnp.float32
    ).astype(jnp.bfloat16)
    basis_cols = coarse_basis.reshape(patches, wave_count, 2, patch_nodes, coarse_width)
    restricted = jnp.einsum(
        "pwqnc,wqpnr->pwcr", basis_cols, gathered, preferred_element_type=jnp.float32
    )
    member = coarse_block[:, None] == jnp.arange(blocks_all, dtype=jnp.int32)[None, :]
    partial_sums = jnp.einsum(
        "pb,pwcr->bwcr", member.astype(jnp.float32), restricted, precision=highest
    )
    totals = lax.psum(partial_sums, ("patch", "coarse"))
    inverses = lax.all_gather(coarse_inv, "coarse", axis=0, tiled=True)
    coarse_coef = jnp.einsum(
        "bwcd,bwdr->bwcr", inverses.astype(jnp.float32), totals, precision=highest
    ).astype(jnp.bfloat16)
    patch_coef = jnp.einsum(
        "pb,bwcr->pwcr",
        member.astype(jnp.bfloat16),
        coarse_coef,
        preferred_element_type=jnp.float32,
    ).astype(jnp.bfloat16)
    inverse = patch_inv.reshape(patches, wave_count, 2, patch_nodes, 2, patch_nodes)
    local_terms = jnp.einsum(
        "pwabqn,wqpnr->wapbr", inverse, gathered, preferred_element_type=jnp.float32
    )
    local_terms = local_terms + jnp.einsum(
        "pwqnc,pwcr->wqpnr", basis_cols, patch_coef, preferred_element_type=jnp.float32
    )
    collected = spread_rows(ext_select, local_terms, "pne,wqpnr->wqer")
    to_lower = collected[:, :, node_rows : node_rows + slot_rows]
    to_upper = collected[:, :, node_rows + slot_rows :]
    back_from_above = passed_along(to_lower.astype(jnp.bfloat16), ("patch", "coarse"), -1).astype(
        to_lower.dtype
    )
    back_from_below = passed_along(to_upper.astype(jnp.bfloat16), ("patch", "coarse"), 1).astype(
        to_upper.dtype
    )
    summed = collected[:, :, :node_rows]
    summed = summed + spread_rows(up_select, back_from_above, "kn,wqkr->wqnr")
    summed = summed + spread_rows(down_select, back_from_below, "kn,wqkr->wqnr")
    return summed.astype(jnp.bfloat16)


def solution(mesh):
    placed = (
        P(None, None, ("patch", "coarse"), None),
        P(("patch", "coarse"), None, None, None),
        P(("patch", "coarse"), None, None, None),
        P("coarse", None, None, None),
        P(("patch", "coarse"), None),
        P(("patch", "coarse"), None, None),
        P(("patch", "coarse")),
    )
    return jax.shard_map(
        per_device,
        mesh=mesh,
        in_specs=placed,
        out_specs=P(None, None, ("patch", "coarse"), None),
        check_vma=False,
    )
```

profile of v0, /device:TPU:0, one launch (start us, length us, event | category | flops | bytes accessed | tf_op | source)
XLA Modules:
  0.0 256.1 jit_solution(5155626987619132174)
XLA Ops:
  6.5 0.0 copy-start
  6.5 0.0 all-reduce.2.cloned.1.call-start
  6.5 0.8 slice_bitcast_fusion.1
  7.4 2.6 %fusion.39 = bf16[2,2,128,256]{3,2,1,0:T(8,128)(2,1)S(1)} fusion(bf16[2,2,1536,256]{3,2,1,0:T(8,128)(2,1)} %param.7, s32[128]{0:T(128)S(1)} %get-tuple-element.7), kind=kOutput, calls=%fused_computation.37 | convolution fusion | flops 402980864 | bytes 3408384 | tf_op jit(solution)/shard_map/kn,wqnr->wqkr/dot_general | solution.py:33
  10.0 0.5 collective-permute-start
  10.6 3.2 %fusion.40 = bf16[2,2,128,256]{3,2,1,0:T(8,128)(2,1)} fusion(bf16[2,2,1536,256]{3,2,1,0:T(8,128)(2,1)} %param.7, s32[128]{0:T(128)S(1)} %get-tuple-element.8), kind=kOutput, calls=%fused_computation.38 | convolution fusion | flops 402980864 | bytes 3408384 | tf_op jit(solution)/shard_map/kn,wqnr->wqkr/dot_general | solution.py:36
  13.8 5.9 %collective-permute-start.1 = (bf16[2,2,128,256]{3,2,1,0:T(8,128)(2,1)}, bf16[2,2,128,256]{3,2,1,0:T(8,128)(2,1)}, u32[]{:S(2)}, u32[]{:S(2)}) collective-permute-start(bf16[2,2,128,256]{3,2,1,0:T(8,128)(2,1)} %fusion.40), channel_id=1, source_target_pairs={{0,31},{1,0},{2,1},{3,2},{4,3},{5,4},{6,5},{7,6},{8,7},{9,8},{10,9... | collective-permute-start | bytes 786440 | tf_op jit(solution)/shard_map/ppermute | solution.py:10
  19.7 0.0 copy-done
  19.7 2.8 %copy.22 = bf16[2,2,1536,256]{2,3,1,0:T(8,128)(2,1)} copy(bf16[2,2,1536,256]{3,2,1,0:T(8,128)(2,1)S(1)} %copy-done) | data formatting | bytes 6291456 | tf_op args[0]
  22.5 0.0 collective-permute-done
  22.5 1.1 copy.23
  23.6 0.3 collective-permute-done.1
  23.9 1.1 copy.24
  25.0 0.0 copy-done.5
  25.1 0.0 copy-start.2
  25.1 10.3 %fusion.29 = bf16[2,2,256,4,512]{4,2,3,1,0:T(8,128)(2,1)S(1)} fusion(s32[4,512]{1,0:T(4,128)S(1)} %copy-done.5, bf16[2,2,128,256]{2,3,1,0:T(8,128)(2,1)S(1)} %copy.24, bf16[2,2,128,256]{2,3,1,0:T(8,128)(2,1)S(1)} %copy.23, bf16[2,2,1536,256]{2,3,1,0:T(8,128)(2,1)} %copy.22), kind=kOutput, calls=%fused_computation.30 | convolution fusion | flops 7532969984 | bytes 7872512 | tf_op jit(solution)/shard_map/pne,wqer->wqpnr/dot_general | solution.py:45
  35.4 0.0 copy-start.6
  35.4 0.0 copy-start.4
  35.4 2.0 copy-done.6
  37.4 0.0 copy-done.2
  37.4 1.3 fusion.36
  38.7 0.0 copy-done.4
  38.8 3.9 %fusion.68 = f32[64,2,32,256]{3,0,2,1:T(8,128)} fusion(f32[4,2,32,256]{3,2,1,0:T(8,128)S(1)} %fusion.36, s32[4]{0:T(128)S(1)} %copy-done.4), kind=kOutput, calls=%fused_computation.60 | convolution fusion | flops 50331904 | bytes 4456464 | tf_op jit(solution)/shard_map/pb,pwcr->bwcr/dot_general | solution.py:53
  42.6 0.0 all-reduce.2.cloned.1.call-update
  42.7 0.4 reshape.11
  43.0 0.0 copy-start.3
  43.0 28.0 %reshape.10 = bf16[4,2,2,512,2,512]{5,4,3,2,1,0:T(2,128)(2,1)} reshape(bf16[4,2,1024,1024]{3,2,1,0:T(8,128)(2,1)} %param.8) | data formatting | bytes 33554432 | tf_op jit(solution)/shard_map/reshape | solution.py:67
  71.1 0.0 copy-done.3
  71.1 9.2 %all_gather.3 = bf16[64,2,32,32]{3,2,1,0:T(8,128)(2,1)S(1)} all-gather(bf16[16,2,32,32]{3,2,1,0:T(8,128)(2,1)S(1)} %copy-done.3), channel_id=1, replica_groups=mesh['patch'=8,'coarse'=4] {'coarse'}, dimensions={0}, use_global_device_ids=true | all-gather | bytes 327680 | tf_op jit(solution)/shard_map/all_gather | solution.py:57
  80.3 15.3 %fusion = f32[2,4,256,2,512,1]{4,2,5,3,1,0:T(8,128)} fusion(bf16[4,2,2,512,2,512]{5,4,3,2,1,0:T(2,128)(2,1)} %reshape.10, bf16[2,2,256,4,512]{4,2,3,1,0:T(8,128)(2,1)} %copy-done.6), kind=kOutput, calls=%fused_computation | convolution fusion | flops 4294967296 | bytes 29360128 | tf_op jit(solution)/shard_map/pwabqn,wqpnr->wapbr/dot_general | solution.py:68
  95.6 91.1 %all-reduce.2.cloned.1.call-done = f32[64,2,32,256]{3,0,2,1:T(8,128)} async-done(((f32[64,2,32,256]{3,0,2,1:T(8,128)}), f32[64,2,32,256]{3,0,2,1:T(8,128)}) %all-reduce.2.cloned.1.call-update) | async-done | bytes 4194320 | tf_op jit(solution)/shard_map/psum | solution.py:56
  186.7 7.1 %convert_bitcast_fusion = bf16[64,2,32,256]{3,2,1,0:T(8,128)(2,1)S(1)} fusion(bf16[64,2,32,32]{3,2,1,0:T(8,128)(2,1)S(1)} %all_gather.3, f32[64,2,32,256]{3,0,2,1:T(8,128)} %all-reduce.2.cloned.1.call-done), kind=kOutput, calls=%fused_computation.33 | convolution fusion | flops 403701760 | bytes 6553600 | tf_op jit(solution)/shard_map/bwcd,bwdr->bwcr/dot_general | solution.py:58
  193.8 1.2 fusion.44
  195.0 1.3 fusion.60
  196.3 0.0 copy-start.1
  196.3 3.2 %copy-done.1 = f32[2,4,256,2,512]{4,2,3,1,0:T(8,128)} copy-done((f32[2,4,256,2,512]{4,2,3,1,0:T(8,128)}, f32[2,4,256,2,512]{4,2,3,1,0:T(8,128)S(1)}, u32[]{:S(2)}) %copy-start.1) | copy-done | bytes 8388632
  199.5 13.1 %fusion.4 = f32[2,2,256,1792,1]{3,2,1,4,0:T(8,128)} fusion(s32[4,512]{1,0:T(4,128)S(1)} %copy-done.5, f32[2,4,256,2,512]{4,2,3,1,0:T(8,128)S(1)} %fusion.60, f32[2,4,256,2,512,1]{4,2,5,3,1,0:T(8,128)} %fusion), kind=kOutput, calls=%fused_computation.5 | convolution fusion | flops 7530348544 | bytes 24125440 | tf_op jit(solution)/shard_map/pne,wqpnr->wqer/dot_general | solution.py:17
  212.6 18.2 %fusion.78 = (bf16[2,2,1792,256]{2,3,1,0:T(8,128)(2,1)S(1)}, f32[2,2,1792,256]{2,3,1,0:T(8,128)}) fusion(f32[2,2,256,1792,1]{3,2,1,4,0:T(8,128)} %fusion.4, s32[4,512]{1,0:T(4,128)S(1)} %copy-done.5, f32[2,4,256,2,512]{4,2,3,1,0:T(8,128)} %copy-done.1, f32[2,4,256,2,512,1]{4,2,5,3,1,0:T(8,128)} %fusion), kind=kOutput, calls=%fused_computation.71 | convolution fusion | flops 7527727104 | bytes 35135488 | tf_op jit(solution)/shard_map/pne,wqpnr->wqer/dot_general | solution.py:16
  230.8 0.1 fusion.77
  230.9 0.9 collective-permute-start.2
  231.8 0.0 collective-permute-start.3
  231.8 3.9 %collective-permute-done.2 = bf16[2,2,128,256]{2,3,1,0:T(8,128)(2,1)S(1)} collective-permute-done((bf16[2,2,128,256]{2,3,1,0:T(8,128)(2,1)S(1)}, bf16[2,2,128,256]{2,3,1,0:T(8,128)(2,1)S(1)}, u32[]{:S(2)}, u32[]{:S(2)}) %collective-permute-start.2) | collective-permute-done | bytes 262176 | tf_op jit(solution)/shard_map/ppermute | solution.py:10
  235.7 1.1 fusion.48
  236.8 1.1 fusion.50
  237.9 3.3 %collective-permute-done.3 = bf16[2,2,128,256]{2,3,1,0:T(8,128)(2,1)S(1)} collective-permute-done((bf16[2,2,128,256]{2,3,1,0:T(8,128)(2,1)S(1)}, bf16[2,2,128,256]{2,3,1,0:T(8,128)(2,1)S(1)}, u32[]{:S(2)}, u32[]{:S(2)}) %collective-permute-start.3) | collective-permute-done | bytes 262176 | tf_op jit(solution)/shard_map/ppermute | solution.py:10
  241.2 1.1 fusion.54
  242.3 4.2 %fusion.16 = bf16[2,2,1536,256]{2,3,1,0:T(8,128)(2,1)S(1)} fusion(f32[2,2,1792,256]{2,3,1,0:T(8,128)} %get-tuple-element.10, f32[2,2,256,1536]{3,2,1,0:T(8,128)S(1)} %fusion.54, f32[2,2,256,1536]{3,2,1,0:T(8,128)S(1)} %fusion.50, f32[2,2,256,1536]{3,2,1,0:T(8,128)S(1)} %fusion.48, bf16[2,2,128,256]{2,3,1,0:T(8,128)(2,1)S(1)} %collective-permute-done.3, ...), kind=kOutput, calls=%fused_computation.19 | convolution fusion | flops 410714112 | bytes 28574208 | tf_op jit(solution)/shard_map/kn,wqkr->wqnr/dot_general | solution.py:16
  246.5 2.8 %copy.36 = bf16[2,2,1536,256]{3,2,1,0:T(8,128)(2,1)} copy(bf16[2,2,1536,256]{2,3,1,0:T(8,128)(2,1)S(1)} %fusion.16) | data formatting | bytes 6291456 | tf_op jit(solution)/shard_map/convert_element_type | solution.py:86
  (1 shorter events, 0.0 us)
Async XLA Ops:
  6.5 13.2 %copy-start = (bf16[2,2,1536,256]{3,2,1,0:T(8,128)(2,1)S(1)}, bf16[2,2,1536,256]{3,2,1,0:T(8,128)(2,1)}, u32[]{:S(2)}) copy-start(bf16[2,2,1536,256]{3,2,1,0:T(8,128)(2,1)} %param.7) | copy-start | bytes 9437188
  6.5 180.1 %all-reduce.2.cloned.1.call-start = ((), (), s32[]{:S(2)}) async-start(), calls=%async_computation | async-start | bytes 8388608 | tf_op jit(solution)/shard_map/psum | solution.py:56
  10.0 12.5 %collective-permute-start = (bf16[2,2,128,256]{3,2,1,0:T(8,128)(2,1)S(1)}, bf16[2,2,128,256]{3,2,1,0:T(8,128)(2,1)}, u32[]{:S(2)}, u32[]{:S(2)}) collective-permute-start(bf16[2,2,128,256]{3,2,1,0:T(8,128)(2,1)S(1)} %fusion.39), channel_id=1, source_target_pairs={{0,1},{1,2},{2,3},{3,4},{4,5},{5,6},{6,7},{7,8},{8,9},{9,10},{10,1... | collective-permute-start | bytes 786440 | tf_op jit(solution)/shard_map/ppermute | solution.py:10
  13.8 11.3 %copy-start.5 = (s32[4,512]{1,0:T(4,128)S(1)}, s32[4,512]{1,0:T(4,128)}, u32[]{:S(2)}) copy-start(s32[4,512]{1,0:T(4,128)} %param.11) | copy-start | bytes 24580
  13.8 10.1 %collective-permute-start.1 = (bf16[2,2,128,256]{3,2,1,0:T(8,128)(2,1)}, bf16[2,2,128,256]{3,2,1,0:T(8,128)(2,1)}, u32[]{:S(2)}, u32[]{:S(2)}) collective-permute-start(bf16[2,2,128,256]{3,2,1,0:T(8,128)(2,1)} %fusion.40), channel_id=1, source_target_pairs={{0,31},{1,0},{2,1},{3,2},{4,3},{5,4},{6,5},{7,6},{8,7},{9,8},{10,9... | collective-permute-start | bytes 786440 | tf_op jit(solution)/shard_map/ppermute | solution.py:10
  25.1 12.4 %copy-start.2 = (bf16[4,2,1024,32]{2,3,1,0:T(8,128)(2,1)S(1)}, bf16[4,2,1024,32]{2,3,1,0:T(8,128)(2,1)}, u32[]{:S(2)}) copy-start(bf16[4,2,1024,32]{2,3,1,0:T(8,128)(2,1)} %param.9) | copy-start | bytes 1572868
  35.4 2.1 copy-start.6
  35.4 3.4 %copy-start.4 = (s32[4]{0:T(128)S(1)}, s32[4]{0:T(128)}, u32[]{:S(2)}) copy-start(s32[4]{0:T(128)} %param.13) | copy-start | bytes 52
  43.0 28.0 %copy-start.3 = (bf16[16,2,32,32]{3,2,1,0:T(8,128)(2,1)S(1)}, bf16[16,2,32,32]{3,2,1,0:T(8,128)(2,1)}, u32[]{:S(2)}) copy-start(bf16[16,2,32,32]{3,2,1,0:T(8,128)(2,1)} %param.10) | copy-start | bytes 196612
  196.3 3.2 %copy-start.1 = (f32[2,4,256,2,512]{4,2,3,1,0:T(8,128)}, f32[2,4,256,2,512]{4,2,3,1,0:T(8,128)S(1)}, u32[]{:S(2)}) copy-start(f32[2,4,256,2,512]{4,2,3,1,0:T(8,128)S(1)} %fusion.60) | copy-start | bytes 25165828
  230.9 4.8 %collective-permute-start.2 = (bf16[2,2,128,256]{2,3,1,0:T(8,128)(2,1)S(1)}, bf16[2,2,128,256]{2,3,1,0:T(8,128)(2,1)S(1)}, u32[]{:S(2)}, u32[]{:S(2)}) collective-permute-start(bf16[2,2,128,256]{2,3,1,0:T(8,128)(2,1)S(1)} %get-tuple-element.5), channel_id=1, source_target_pairs={{0,31},{1,0},{2,1},{3,2},{4,3},{5,4},{6,5},{7,6},{8,7},{9,8},{10,9... | collective-permute-start | bytes 786440 | tf_op jit(solution)/shard_map/ppermute | solution.py:10
  231.8 9.4 %collective-permute-start.3 = (bf16[2,2,128,256]{2,3,1,0:T(8,128)(2,1)S(1)}, bf16[2,2,128,256]{2,3,1,0:T(8,128)(2,1)S(1)}, u32[]{:S(2)}, u32[]{:S(2)}) collective-permute-start(bf16[2,2,128,256]{2,3,1,0:T(8,128)(2,1)S(1)} %get-tuple-element.6), channel_id=1, source_target_pairs={{0,1},{1,2},{2,3},{3,4},{4,5},{5,6},{6,7},{7,8},{8,9},{9,10},{10,1... | collective-permute-start | bytes 786440 | tf_op jit(solution)/shard_map/ppermute | solution.py:10
Sparse Core Ops, SparseCore 0:
  42.8 143.8 all-reduce.1
where the time goes:
time: 257 us; the launch traced here: 256 us
  waiting for transfers between devices  98.6 us (38%)
  matrix products  84.9 us (33%)
  local copies, waits for them, and re-layouts  42.4 us (16%)
  between operations  13.5 us (5%)
  blocking collectives  9.23 us (4%)
  starting transfers between devices  7.39 us (3%)
    psum x1, waiting for transfers between devices, per_device(): totals = lax.psum(partial_sums, ('patch', 'coarse'))  91.1 us
    reshape x1, local copies, waits for them, and re-layouts, per_device(): patch_inv.reshape(patches, wave_count, 2, patch_nodes, 2, patch_nodes)  28 us
    dot_general x3, matrix products, spread_rows(): jnp.einsum(form, selector, upper_part, preferred_element_type=jnp.float32)  23.4 us
    dot_general x1, matrix products, per_device(): jnp.einsum('pwabqn,wqpnr->wapbr', inverse, gathered, preferred_element_ty...  15.3 us
    dot_general x3, matrix products, spread_rows(): jnp.einsum(form, selector, lower_part, preferred_element_type=jnp.float32)  15.3 us
    dot_general x1, matrix products, per_device(): jnp.einsum('pne,wqer->wqpnr', ext_select, extended, preferred_element_typ...  10.3 us
    all_gather x1, blocking collectives, per_device(): inverses = lax.all_gather(coarse_inv, 'coarse', axis=0, tiled=True)  9.23 us
    unnamed x15, local copies, waits for them, and re-layouts  8.05 us
  transfers between devices with their start and end apart: 5, of which 4 were waited for; matrix products, arithmetic and copies ran while one was open for 21% of the time, Pallas kernels for 0%

commit v1 on v0

v1 whole, which is shorter than its diff:
```python
import functools

import jax
import jax.numpy as jnp
from jax import lax
from jax.experimental import pallas as pl
from jax.experimental.pallas import tpu as pltpu
from jax.sharding import PartitionSpec as P

AXES = ("patch", "coarse")
LANES = 128
F32 = jnp.float32
BF16 = jnp.bfloat16


def passed_along(value, axis, steps):
    count = lax.axis_size(axis)
    pairs = [(source, (source + steps) % count) for source in range(count)]
    return lax.ppermute(value, axis, pairs)


def dot(a, b):
    return jnp.dot(a, b, preferred_element_type=F32)


def as_column(row):
    return jnp.transpose(jnp.broadcast_to(row, (LANES, row.shape[1])))


def iota(shape, axis):
    return lax.broadcasted_iota(jnp.int32, shape, axis)


def one_hot_rows(column, width, start=0):
    rows = column.shape[0]
    parts = [
        (column == (iota((rows, LANES), 1) + (start + t)).astype(F32)).astype(F32).astype(BF16)
        for t in range(0, width, LANES)
    ]
    return jnp.concatenate(parts, axis=1)


def vmem(shape, dtype):
    return pltpu.VMEM(shape, dtype)


def whole(array):
    zeros = (0,) * array.ndim
    return pl.BlockSpec(array.shape, lambda *_: zeros)


def select_kernel(rows_ref, x_ref, up_ref, down_ref, sel):
    slots = rows_ref.shape[1]
    nodes = x_ref.shape[1]

    @pl.when(pl.program_id(0) == 0)
    def _():
        for b in range(2):
            col = as_column(rows_ref[b : b + 1, :].astype(F32))
            sel[b * slots : (b + 1) * slots, :] = one_hot_rows(col, nodes)

    got = dot(sel[...], x_ref[0]).astype(BF16)
    up_ref[0] = got[:slots]
    down_ref[0] = got[slots:]


def select_rows(x4, rows):
    parts, nodes, width = x4.shape
    slots = rows.shape[1]
    block = pl.BlockSpec((1, slots, width), lambda i: (i, 0, 0))
    shape = jax.ShapeDtypeStruct((parts, slots, width), BF16)
    return pl.pallas_call(
        select_kernel,
        grid=(parts,),
        in_specs=[whole(rows), pl.BlockSpec((1, nodes, width), lambda i: (i, 0, 0))],
        out_specs=[block, block],
        out_shape=[shape, shape],
        scratch_shapes=[vmem((2 * slots, nodes), BF16)],
        name="select",
    )(rows, x4)


def prep_kernel(
    core, slots_ref, basis_ref, x_ref,
    pos_ref, rest_ref, crem_ref, y_ref, r_ref, btrem_ref, bext_ref,
    ccat, bt,
):
    patches, patch_nodes = slots_ref.shape
    waves, width = basis_ref.shape[1], basis_ref.shape[2]
    nodes = x_ref.shape[1]
    rest = patch_nodes - core
    ext = ccat.shape[1]
    step = pl.program_id(0)

    @pl.when(step == 0)
    def _():
        slots = slots_ref[...].astype(F32)
        first = (iota((patches, patch_nodes), 0) * core).astype(F32)
        local = slots - first
        outside = (local < 0.0) | (local >= float(core))
        before = (iota((patch_nodes, patch_nodes), 0) < iota((patch_nodes, patch_nodes), 1))
        rank = dot(
            outside.astype(F32).astype(BF16), before.astype(F32).astype(BF16)
        )
        pos = jnp.where(outside, rank + float(core), local)
        pos_ref[...] = pos
        for p in range(patches):
            prow = pos[p : p + 1, :]
            srow = slots[p : p + 1, :]
            permute = one_hot_rows(as_column(prow), patch_nodes)
            basis = jnp.concatenate(
                [
                    basis_ref[p, w, :, q * patch_nodes : (q + 1) * patch_nodes]
                    for w in range(waves)
                    for q in range(2)
                ],
                axis=0,
            )
            moved = dot(basis, permute).astype(BF16)
            hit = prow == (iota((rest, patch_nodes), 0) + core).astype(F32)
            ids = jnp.sum(
                jnp.where(hit, jnp.broadcast_to(srow, hit.shape), 0.0), axis=1, keepdims=True
            )
            ids = jnp.broadcast_to(ids, (rest, LANES))
            rest_ref[:, p * rest : (p + 1) * rest] = jnp.transpose(ids)[0:8]
            pick = one_hot_rows(ids, ext)
            ccat[p * rest : (p + 1) * rest, :] = pick
            spread = dot(moved[:, core:], pick).astype(BF16)
            for k in range(waves * 2):
                rows = slice(k * width, (k + 1) * width)
                here = slice(p * width, (p + 1) * width)
                bt[k, here, :] = spread[rows]
                bt[k, here, p * core : (p + 1) * core] = (
                    spread[rows, p * core : (p + 1) * core] + moved[rows, :core]
                )
        crem_ref[...] = ccat[:, nodes:]

    x = x_ref[0]
    y_ref[0] = dot(ccat[:, :nodes], x).astype(BF16)
    mine = bt[step]
    part = dot(mine[:, :nodes], x)

    @pl.when(step % 2 == 0)
    def _():
        r_ref[0] = part

    @pl.when(step % 2 == 1)
    def _():
        r_ref[0] = r_ref[0] + part

    btrem_ref[0] = mine[:, nodes:]
    bext_ref[0] = jnp.transpose(mine)


def prepare(slots, basis_t, x4, ext):
    parts, nodes, width = x4.shape
    patches, patch_nodes = slots.shape
    core = nodes // patches
    rest = patch_nodes - core
    columns = patches * basis_t.shape[2]
    rows3 = lambda a, b: pl.BlockSpec((1, a, b), lambda i: (i, 0, 0))
    shape = jax.ShapeDtypeStruct
    return pl.pallas_call(
        functools.partial(prep_kernel, core),
        grid=(parts,),
        in_specs=[whole(slots), whole(basis_t), rows3(nodes, width)],
        out_specs=[
            pl.BlockSpec((patches, patch_nodes), lambda i: (0, 0)),
            pl.BlockSpec((8, patches * rest), lambda i: (0, 0)),
            pl.BlockSpec((patches * rest, ext - nodes), lambda i: (0, 0)),
            rows3(patches * rest, width),
            pl.BlockSpec((1, columns, width), lambda i: (i // 2, 0, 0)),
            rows3(columns, ext - nodes),
            rows3(ext, columns),
        ],
        out_shape=[
            shape((patches, patch_nodes), F32),
            shape((8, patches * rest), F32),
            shape((patches * rest, ext - nodes), BF16),
            shape((parts, patches * rest, width), BF16),
            shape((parts // 2, columns, width), F32),
            shape((parts, columns, ext - nodes), BF16),
            shape((parts, ext, columns), BF16),
        ],
        scratch_shapes=[vmem((patches * rest, ext), BF16), vmem((parts, columns, ext), BF16)],
        name="prep",
    )(slots, basis_t, x4)


def owner_order(columns, patches, width, per_group):
    rows = patches * per_group
    i = iota((columns, columns), 0)
    j = iota((columns, columns), 1)
    source = ((i % rows) // per_group) * width + (i // rows) * per_group + i % per_group
    return (source == j).astype(F32).astype(BF16)


def restrict_kernel(per_group, block_ref, r_ref, btrem_ref, below_ref, above_ref, out_ref):
    waves, columns, width = r_ref.shape
    patches = block_ref.shape[0]
    slots = below_ref.shape[1]
    rows = patches * per_group
    groups = columns // rows
    halves = width // LANES
    order = owner_order(columns, patches, columns // patches, per_group)
    tail = out_ref.shape[1] - rows
    keys = jnp.zeros((tail, LANES), F32)
    for p in range(patches):
        keys = jnp.where(iota((tail, LANES), 0) == p, block_ref[p].astype(F32), keys)
    keys = keys.astype(BF16)
    for w in range(waves):
        total = r_ref[w]
        for q in range(2):
            k = 2 * w + q
            total = total + dot(btrem_ref[k, :, :slots], below_ref[k])
            total = total + dot(btrem_ref[k, :, slots:], above_ref[k])
        moved = dot(order, total.astype(BF16)).astype(BF16)
        for g in range(groups):
            for h in range(halves):
                owner = (w * groups + g) * halves + h
                out_ref[owner, :rows, :] = moved[g * rows : (g + 1) * rows, h * LANES : (h + 1) * LANES]
                out_ref[owner, rows:, :] = keys


def restrict(block, r_own, bt_rem, below, above, owners, per_group, padded):
    return pl.pallas_call(
        functools.partial(restrict_kernel, per_group),
        in_specs=[pl.BlockSpec(memory_space=pltpu.SMEM)] + [pl.BlockSpec(memory_space=pltpu.VMEM)] * 4,
        out_specs=pl.BlockSpec(memory_space=pltpu.VMEM),
        out_shape=jax.ShapeDtypeStruct((owners, padded, LANES), BF16),
        name="restrict",
    )(block, r_own, bt_rem, below, above)


def sums_kernel(per_group, patches, got_ref, out_ref, data, tags):
    owners, padded, _ = got_ref.shape
    rows = patches * per_group
    tail = padded - rows
    for s in range(owners):
        data[s * rows : (s + 1) * rows, :] = got_ref[s, :rows, :].astype(F32)
        tags[s * tail : (s + 1) * tail, :] = got_ref[s, rows:, :].astype(F32)
    count = owners * rows
    i = iota((count, owners * tail), 0)
    j = iota((count, owners * tail), 1)
    wanted = (i // rows) * tail + (i % rows) // per_group
    keys = dot((wanted == j).astype(F32).astype(BF16), tags[...].astype(BF16))
    keys = keys * float(per_group) + (iota((count, LANES), 0) % per_group).astype(F32)
    key_row = jnp.transpose(keys)[0:1, :]
    column = jnp.concatenate([keys] * (count // LANES), axis=1)
    same = (column == key_row).astype(F32).astype(BF16)
    sums = dot(same, data[...].astype(BF16))
    data[...] = sums
    for s in range(owners):
        out_ref[s] = data[s * rows : (s + 1) * rows, :].astype(BF16)


def owner_sums(got, patches, per_group):
    owners, padded, _ = got.shape
    rows = patches * per_group
    return pl.pallas_call(
        functools.partial(sums_kernel, per_group, patches),
        in_specs=[pl.BlockSpec(memory_space=pltpu.VMEM)],
        out_specs=pl.BlockSpec(memory_space=pltpu.VMEM),
        out_shape=jax.ShapeDtypeStruct((owners, rows, LANES), BF16),
        scratch_shapes=[
            vmem((owners * rows, LANES), F32),
            vmem((owners * (padded - rows), LANES), F32),
        ],
        name="sums",
    )(got)


def local_kernel(pos_ref, core_ref, y_ref, crem_ref, below_ref, above_ref, inv_ref, out_ref, pm, g):
    core, width = core_ref.shape[1], core_ref.shape[2]
    patch_nodes = pos_ref.shape[2]
    slots = below_ref.shape[1]
    prow = pos_ref[0]

    @pl.when(pl.program_id(1) == 0)
    def _():
        pm[...] = one_hot_rows(as_column(prow), patch_nodes)

    crem = crem_ref[...]
    for q in range(2):
        far = dot(crem[:, :slots], below_ref[q]) + dot(crem[:, slots:], above_ref[q])
        other = y_ref[q] + far.astype(BF16)
        ordered = jnp.concatenate([core_ref[q], other], axis=0)
        g[q * patch_nodes : (q + 1) * patch_nodes, :] = dot(pm[...], ordered).astype(BF16)
    local = dot(inv_ref[0, 0], g[...]).astype(BF16)
    back = (prow == iota((patch_nodes, patch_nodes), 0).astype(F32)).astype(F32).astype(BF16)
    for q in range(2):
        out_ref[0, q] = dot(back, local[q * patch_nodes : (q + 1) * patch_nodes]).astype(BF16)


def local_products(pos, x4, y, crem, below, above, patch_inv, first, count):
    parts, nodes, width = x4.shape
    patches, waves = patch_inv.shape[:2]
    patch_nodes = pos.shape[1]
    core = nodes // patches
    rest = patch_nodes - core
    slots = below.shape[1]
    pos3 = pos.reshape(patches, 1, patch_nodes)
    return pl.pallas_call(
        local_kernel,
        grid=(count, waves),
        in_specs=[
            pl.BlockSpec((1, 1, patch_nodes), lambda p, w: (first + p, 0, 0)),
            pl.BlockSpec((2, core, width), lambda p, w: (w, first + p, 0)),
            pl.BlockSpec((2, rest, width), lambda p, w: (w, first + p, 0)),
            pl.BlockSpec((rest, 2 * slots), lambda p, w: (first + p, 0)),
            pl.BlockSpec((2, slots, width), lambda p, w: (w, 0, 0)),
            pl.BlockSpec((2, slots, width), lambda p, w: (w, 0, 0)),
            pl.BlockSpec((1, 1) + patch_inv.shape[2:], lambda p, w: (first + p, w, 0, 0)),
        ],
        out_specs=pl.BlockSpec((1, 2, patch_nodes, width), lambda p, w: (p, w, 0, 0)),
        out_shape=jax.ShapeDtypeStruct((count, parts, patch_nodes, width), BF16),
        scratch_shapes=[
            vmem((patch_nodes, patch_nodes), BF16),
            vmem((2 * patch_nodes, width), BF16),
        ],
        name="local",
    )(pos3, x4, y, crem, below, above, patch_inv)


def scatter_kernel(nodes, rest_ref, *refs):
    *local_refs, own_ref, margin_ref, spread = refs
    core = nodes // sum(r.shape[0] for r in local_refs)
    ext, columns = spread.shape

    @pl.when(pl.program_id(0) == 0)
    def _():
        ids = rest_ref[0:1, :]
        spread[...] = (ids == iota((ext, columns), 0).astype(F32)).astype(F32).astype(BF16)

    blocks = [(r, i) for r in local_refs for i in range(r.shape[0])]
    others = jnp.concatenate([r[i, 0, core:, :] for r, i in blocks], axis=0)
    total = dot(spread[...], others)
    for p, (r, i) in enumerate(blocks):
        rows = slice(p * core, (p + 1) * core)
        own_ref[0, rows, :] = (total[rows] + r[i, 0, :core, :].astype(F32)).astype(BF16)
    margin_ref[0] = total[nodes:]


def scatter(rest_ids, locals_, nodes, ext):
    parts, patch_nodes, width = locals_[0].shape[1:]
    columns = rest_ids.shape[1]
    return pl.pallas_call(
        functools.partial(scatter_kernel, nodes),
        grid=(parts,),
        in_specs=[whole(rest_ids)]
        + [pl.BlockSpec((a.shape[0], 1, patch_nodes, width), lambda i: (0, i, 0, 0)) for a in locals_],
        out_specs=[
            pl.BlockSpec((1, nodes, width), lambda i: (i, 0, 0)),
            pl.BlockSpec((1, ext - nodes, width), lambda i: (i, 0, 0)),
        ],
        out_shape=[
            jax.ShapeDtypeStruct((parts, nodes, width), BF16),
            jax.ShapeDtypeStruct((parts, ext - nodes, width), F32),
        ],
        scratch_shapes=[vmem((ext, columns), BF16)],
        name="scatter",
    )(rest_ids, *locals_)


def coef_kernel(
    per_group, block_ref, place_ref, sums_ref, inv_ref, brem_ref, margin_ref,
    coef_ref, low_ref, high_ref, gathered, inverse,
):
    waves, columns, width = coef_ref.shape
    patches = block_ref.shape[0]
    group, each = inv_ref.shape[0], inv_ref.shape[1]
    size = inv_ref.shape[3]
    rows = patches * per_group
    groups = columns // rows
    halves = width // LANES
    slots = low_ref.shape[1]
    order = owner_order(columns, patches, size, per_group)
    inverse[...] = jnp.zeros(inverse.shape, inverse.dtype)
    for w in range(waves):
        for p in range(patches):
            block = block_ref[p]
            piece = lax.rem(block // each - place_ref[0] + group, group)
            inverse[p * size : (p + 1) * size, p * size : (p + 1) * size] = inv_ref[
                piece, lax.rem(block, each), w
            ].astype(F32)
        for g in range(groups):
            for h in range(halves):
                gathered[g * rows : (g + 1) * rows, h * LANES : (h + 1) * LANES] = sums_ref[
                    (w * groups + g) * halves + h
                ].astype(F32)
        mixed = dot(inverse[...].astype(BF16), jnp.transpose(order)).astype(BF16)
        coef = dot(mixed, gathered[...].astype(BF16)).astype(BF16)
        coef_ref[w] = coef
        for q in range(2):
            k = 2 * w + q
            low_ref[k] = (margin_ref[k, :slots, :] + dot(brem_ref[k, :slots, :], coef)).astype(BF16)
            high_ref[k] = (margin_ref[k, slots:, :] + dot(brem_ref[k, slots:, :], coef)).astype(BF16)


def coefficients(block, place, sums, inverses, b_ext, margin, nodes, per_group):
    parts, ext, columns = b_ext.shape
    width = margin.shape[2]
    waves = inverses.shape[2]
    slots = (ext - nodes) // 2
    shape = jax.ShapeDtypeStruct
    full = pl.BlockSpec(memory_space=pltpu.VMEM)
    zero = lambda a: pl.BlockSpec(a, lambda *_: (0,) * len(a))
    return pl.pallas_call(
        functools.partial(coef_kernel, per_group),
        grid=(1,),
        in_specs=[
            pl.BlockSpec(memory_space=pltpu.SMEM),
            pl.BlockSpec(memory_space=pltpu.SMEM),
            zero(sums.shape),
            zero(inverses.shape),
            pl.BlockSpec((parts, ext - nodes, columns), lambda i: (0, nodes // (ext - nodes), 0)),
            zero(margin.shape),
        ],
        out_specs=[
            zero((waves, columns, width)),
            zero((parts, slots, width)),
            zero((parts, slots, width)),
        ],
        out_shape=[
            shape((waves, columns, width), BF16),
            shape((parts, slots, width), BF16),
            shape((parts, slots, width), BF16),
        ],
        scratch_shapes=[vmem((columns, width), F32), vmem((columns, columns), F32)],
        name="coef",
    )(block, place, sums, inverses, b_ext, margin)


def final_kernel(rows_ref, own_ref, b_ref, coef_ref, above_ref, below_ref, out_ref, spread):
    slots = rows_ref.shape[1]
    nodes = own_ref.shape[1]

    @pl.when(pl.program_id(0) == 0)
    def _():
        for b in range(2):
            ids = rows_ref[b : b + 1, :].astype(F32)
            spread[:, b * slots : (b + 1) * slots] = (
                (ids == iota((nodes, slots), 0).astype(F32)).astype(F32).astype(BF16)
            )

    back = jnp.concatenate([above_ref[0], below_ref[0]], axis=0)
    total = own_ref[0].astype(F32) + dot(spread[...], back) + dot(b_ref[0], coef_ref[0])
    out_ref[0] = total.astype(BF16)


def finish(rows, own, b_ext, coef, above, below):
    parts, nodes, width = own.shape
    slots = rows.shape[1]
    columns = b_ext.shape[2]
    part = lambda a: pl.BlockSpec((1, a, width), lambda i: (i, 0, 0))
    return pl.pallas_call(
        final_kernel,
        grid=(parts,),
        in_specs=[
            whole(rows),
            part(nodes),
            pl.BlockSpec((1, nodes, columns), lambda i: (i, 0, 0)),
            pl.BlockSpec((1, columns, width), lambda i: (i // 2, 0, 0)),
            part(slots),
            part(slots),
        ],
        out_specs=part(nodes),
        out_shape=jax.ShapeDtypeStruct((parts, nodes, width), BF16),
        scratch_shapes=[vmem((nodes, 2 * slots), BF16)],
        name="finish",
    )(rows, own, b_ext, coef, above, below)


def per_device(residual, patch_inv, coarse_basis, coarse_inv, patch_slots, send_rows, coarse_block):
    waves, _, nodes, width = residual.shape
    patches = patch_inv.shape[0]
    size = coarse_basis.shape[3]
    slots = send_rows.shape[2]
    ext = nodes + 2 * slots
    owners = lax.axis_size(AXES)
    halves = width // LANES
    groups = owners // (waves * halves)
    per_group = size // groups
    assert groups * waves * halves == owners and per_group * groups == size
    rows = patches * per_group
    padded = -(-(rows + patches) // 8) * 8
    x4 = residual.reshape(2 * waves, nodes, width)
    send = send_rows[0]

    up, down = select_rows(x4, send)
    below = passed_along(up, AXES, 1)
    above = passed_along(down, AXES, -1)
    basis_t = jnp.swapaxes(coarse_basis, 2, 3)
    pos, rest_ids, crem, y, r_own, bt_rem, b_ext = prepare(patch_slots, basis_t, x4, ext)
    count = lax.axis_size("coarse")
    inverses = jnp.stack(
        [coarse_inv] + [passed_along(coarse_inv, "coarse", -k) for k in range(1, count)]
    )
    place = lax.axis_index("coarse").astype(jnp.int32).reshape(1)

    sent = restrict(coarse_block, r_own, bt_rem, below, above, owners, per_group, padded)
    got = lax.all_to_all(sent, AXES, 0, 0, tiled=True)
    half = patches // 2
    first = local_products(pos, x4, y, crem, below, above, patch_inv, 0, half)
    sums = owner_sums(got, patches, per_group)
    mine = lax.all_to_all(sums, AXES, 0, 0, tiled=True)
    second = local_products(pos, x4, y, crem, below, above, patch_inv, half, patches - half)
    own, margin = scatter(rest_ids, [first, second], nodes, ext)
    coef, low, high = coefficients(
        coarse_block, place, mine, inverses, b_ext, margin, nodes, per_group
    )
    back_above = passed_along(low, AXES, -1)
    back_below = passed_along(high, AXES, 1)
    out = finish(send, own, b_ext, coef, back_above, back_below)
    return out.reshape(residual.shape)


def solution(mesh):
    placed = (
        P(None, None, AXES, None),
        P(AXES, None, None, None),
        P(AXES, None, None, None),
        P("coarse", None, None, None),
        P(AXES, None),
        P(AXES, None, None),
        P(AXES),
    )
    return jax.shard_map(
        per_device,
        mesh=mesh,
        in_specs=placed,
        out_specs=P(None, None, AXES, None),
        check_vma=False,
    )
```

time: 257 us -> 108 us (0.42)
  matrix products: 84.9 us -> 0 us
  waiting for transfers between devices: 98.6 us -> 21.9 us
  Pallas kernels: 0 us -> 54.2 us
  local copies, waits for them, and re-layouts: 42.4 us -> 3.44 us
  between operations: 13.5 us -> 0.06 us
  starting transfers between devices: 7.39 us -> 13.7 us
  blocking collectives: 9.23 us -> 12.2 us
    psum x1 -> x0, waiting for transfers between devices: 91.1 us -> none  [per_device(): totals = lax.psum(partial_sums, ('patch', 'coarse'))]
    dot_general x15 -> x0, matrix products: 84.9 us -> none  [the longest x3 23.4 us: spread_rows(): jnp.einsum(form, selector, upper_part, preferred_element_type=jnp.float32)]
    pallas_call x0 -> x9, Pallas kernels: none -> 54.2 us  [the longest x2 21.4 us: local_products(): pl.pallas_call(local_kernel, grid=(count, waves), in_specs=[pl.BlockSpec(...]
    reshape x2 -> x1, local copies, waits for them, and re-layouts: 28.4 us -> 1.3 us  [local_products(): pos3 = pos.reshape(patches, 1, patch_nodes)]
    ppermute x4 -> x7, waiting for transfers between devices: 7.54 us -> 21.9 us  [passed_along(): return lax.ppermute(value, axis, pairs)]
    all_to_all x0 -> x1, blocking collectives: none -> 12.2 us  [per_device(): got = lax.all_to_all(sent, AXES, 0, 0, tiled=True)]
    all_gather x1 -> x0, blocking collectives: 9.23 us -> none  [per_device(): inverses = lax.all_gather(coarse_inv, 'coarse', axis=0, tiled=True)]
    unnamed x15 -> x12, local copies, waits for them, and re-layouts: 8.05 us -> 2.15 us
  transfers between devices with their start and end apart: 5 -> 8, of which waited for: 4 -> 4; matrix products, arithmetic and copies ran while one was open for 21% -> 2% of each run, Pallas kernels for 0% -> 33%
where the time goes in v1:
time: 108 us; the launch traced here: 107 us
  Pallas kernels  54.2 us (50%)
  waiting for transfers between devices  21.9 us (20%)
  starting transfers between devices  13.7 us (13%)
  blocking collectives  12.2 us (11%)
  local copies, waits for them, and re-layouts  3.44 us (3%)
  other arithmetic  1.26 us (1%)
    ppermute x7, waiting for transfers between devices, passed_along(): return lax.ppermute(value, axis, pairs)  21.9 us
    pallas_call x2, Pallas kernels, local_products(): pl.pallas_call(local_kernel, grid=(count, waves), in_specs=[pl.BlockSpec(...  21.4 us
    all_to_all x1, blocking collectives, per_device(): got = lax.all_to_all(sent, AXES, 0, 0, tiled=True)  12.2 us
    ppermute x7, starting transfers between devices, passed_along(): return lax.ppermute(value, axis, pairs)  11.2 us
    pallas_call x1, Pallas kernels, prepare(): pl.pallas_call(functools.partial(prep_kernel, core), grid=(parts,), in_sp...  8.1 us
    pallas_call x1, Pallas kernels, scatter(): pl.pallas_call(functools.partial(scatter_kernel, nodes), grid=(parts,), i...  6.09 us
    pallas_call x1, Pallas kernels, finish(): pl.pallas_call(final_kernel, grid=(parts,), in_specs=[whole(rows), part(n...  5.9 us
    pallas_call x1, Pallas kernels, select_rows(): pl.pallas_call(select_kernel, grid=(parts,), in_specs=[whole(rows), pl.Bl...  4.52 us
  transfers between devices with their start and end apart: 8, of which 4 were waited for; matrix products, arithmetic and copies ran while one was open for 2% of the time, Pallas kernels for 33%

profile of v1, /device:TPU:0, one launch (start us, length us, event | category | flops | bytes accessed | tf_op | source)
XLA Modules:
  0.0 106.8 jit_solution(10021901045187987296)
XLA Ops:
  0.0 4.5 %select.1 = (bf16[4,128,256]{2,1,0:T(8,128)(2,1)}, bf16[4,128,256]{2,1,0:T(8,128)(2,1)}) custom-call(s32[2,128]{1,0:T(2,128)} %bitcast.18, bf16[4,1536,256]{2,1,0:T(8,128)(2,1)} %bitcast.9), custom_call_target="tpu_custom_call" | custom-call | tf_op jit(solution)/shard_map/select/pallas_call | solution.py:72
  4.5 0.0 copy-start.5
  4.5 0.5 collective-permute-start
  5.0 6.0 %collective-permute-start.1 = (bf16[4,128,256]{2,1,0:T(8,128)(2,1)}, bf16[4,128,256]{2,1,0:T(8,128)(2,1)S(1)}, u32[]{:S(2)}, u32[]{:S(2)}) collective-permute-start(bf16[4,128,256]{2,1,0:T(8,128)(2,1)} %get-tuple-element.24), channel_id=1, source_target_pairs={{0,31},{1,0},{2,1},{3,2},{4,3},{5,4},{6,5},{7,6},{8,7},{9,8},{10,9... | collective-permute-start | bytes 786440 | tf_op jit(solution)/shard_map/ppermute | solution.py:19
  11.0 8.1 %prep.1 = (f32[4,512]{1,0:T(4,128)}, f32[8,512]{1,0:T(8,128)}, bf16[512,256]{1,0:T(8,128)(2,1)}, bf16[4,512,256]{2,1,0:T(8,128)(2,1)}, f32[2,128,256]{2,1,0:T(8,...) custom-call(s32[4,512]{1,0:T(4,128)} %slots_ref.1, bf16[4,2,32,1024]{3,2,1,0:T(8,128)(2,1)} %bitcast.13, ...), custom_call_target="tpu_custom_call" | custom-call | tf_op jit(solution)/shard_map/prep/pallas_call | solution.py:163
  19.1 0.0 collective-permute-done.below_ref
  19.1 0.0 copy-start
  19.1 0.0 collective-permute-done.1.above_ref
  19.1 0.0 copy-start.1
  19.1 0.7 copy-done
  19.8 0.1 copy-done.1
  19.9 2.6 %restrict.1 = bf16[32,24,128]{2,1,0:T(8,128)(2,1)} custom-call(s32[4]{0:T(128)} %block_ref.3, f32[2,128,256]{2,1,0:T(8,128)} %get-tuple-element.27.r_ref, bf16[4,128,256]{2,1,0:T(8,128)(2,1)} %get-tuple-element.28.btrem_ref, bf16[4,128,256]{2,1,0:T(8,128)(2,1)} %copy-done, bf16[4,128,256]{2,1,0:T(8,128)(2,1)} %copy-done.1), custom_call_target="tpu_custom_call" | custom-call | tf_op jit(solution)/shard_map/restrict/pallas_call | solution.py:226
  22.5 12.2 %all_to_all.10.got_ref = bf16[32,24,128]{2,1,0:T(8,128)(2,1)} all-to-all(bf16[32,24,128]{2,1,0:T(8,128)(2,1)} %restrict.1), channel_id=1, replica_groups=mesh['patch'=8,'coarse'=4] {'patch','coarse'}, dimensions={0} | all-to-all | bytes 393216 | tf_op jit(solution)/shard_map/all_to_all | solution.py:502
  34.7 2.2 %sums.1 = bf16[32,16,128]{2,1,0:T(8,128)(2,1)} custom-call(bf16[32,24,128]{2,1,0:T(8,128)(2,1)} %all_to_all.10.got_ref), custom_call_target="tpu_custom_call" | custom-call | tf_op jit(solution)/shard_map/sums/pallas_call | solution.py:260
  36.9 2.6 %all-to-all-start.1 = ((bf16[32,16,128]{2,1,0:T(8,128)(2,1)}), bf16[32,16,128]{2,1,0:T(8,128)(2,1)S(1)}, u32[]{:S(2)}, u32[]{:S(2)}) async-start(bf16[32,16,128]{2,1,0:T(8,128)(2,1)} %sums.1), calls=%async_computation.1 | async-start | bytes 262144 | tf_op jit(solution)/shard_map/all_to_all | solution.py:506
  39.4 0.0 copy-done.5
  39.4 1.5 %collective-permute-start.2 = (bf16[16,2,32,32]{3,2,1,0:T(8,128)(2,1)S(1)}, bf16[16,2,32,32]{3,2,1,0:T(8,128)(2,1)S(1)}, u32[]{:S(2)}, u32[]{:S(2)}) collective-permute-start(bf16[16,2,32,32]{3,2,1,0:T(8,128)(2,1)S(1)} %copy-done.5), channel_id=1, source_target_pairs={{0,3},{1,0},{2,1},{3,2},{4,7},{5,4},{6,5},{7,6},{8,11},{9,8},{10,9... | collective-permute-start | bytes 196616 | tf_op jit(solution)/shard_map/ppermute | solution.py:19
  41.0 0.4 collective-permute-start.3
  41.4 0.1 collective-permute-start.4
  41.5 1.3 %reshape.14.pos_ref = f32[4,1,512]{2,1,0:T(1,128)} reshape(f32[4,512]{1,0:T(4,128)} %get-tuple-element.20) | data formatting | bytes 16384 | tf_op jit(solution)/shard_map/reshape | solution.py:302
  42.8 5.7 %collective-permute-done.2 = bf16[16,2,32,32]{3,2,1,0:T(8,128)(2,1)S(1)} collective-permute-done((bf16[16,2,32,32]{3,2,1,0:T(8,128)(2,1)S(1)}, bf16[16,2,32,32]{3,2,1,0:T(8,128)(2,1)S(1)}, u32[]{:S(2)}, u32[]{:S(2)}) %collective-permute-start.2) | collective-permute-done | bytes 65568 | tf_op jit(solution)/shard_map/ppermute | solution.py:19
  48.5 6.6 %collective-permute-done.3 = bf16[16,2,32,32]{3,2,1,0:T(8,128)(2,1)S(1)} collective-permute-done((bf16[16,2,32,32]{3,2,1,0:T(8,128)(2,1)S(1)}, bf16[16,2,32,32]{3,2,1,0:T(8,128)(2,1)S(1)}, u32[]{:S(2)}, u32[]{:S(2)}) %collective-permute-start.3) | collective-permute-done | bytes 65568 | tf_op jit(solution)/shard_map/ppermute | solution.py:19
  55.1 0.0 collective-permute-done.4
  55.1 1.3 %pad_maximum_fusion.inv_ref = bf16[4,16,2,32,32]{4,3,2,1,0:T(8,128)(2,1)} fusion(bf16[1,16,2,32,32]{4,3,2,1,0:T(8,128)(2,1)S(1)} %bitcast.17, bf16[1,16,2,32,32]{4,3,2,1,0:T(8,128)(2,1)S(1)} %bitcast.16, bf16[1,16,2,32,32]{4,3,2,1,0:T(8,128)(2,1)S(1)} %bitcast.15, bf16[1,16,2,32,32]{4,3,2,1,0:T(8,128)(2,1)S(1)} %bitcast.14), kind=kLoop, calls=%fused_computation | loop fusion | flops 393216 | bytes 524288 | tf_op jit(solution)/shard_map/stack | solution.py:496
  56.3 10.7 %local.3.refs_1_ = bf16[2,4,512,256]{3,2,1,0:T(8,128)(2,1)} custom-call(f32[4,1,512]{2,1,0:T(1,128)} %reshape.14.pos_ref, bf16[4,1536,256]{2,1,0:T(8,128)(2,1)} %bitcast.11, bf16[4,512,256]{2,1,0:T(8,128)(2,1)} %get-tuple-element.21.y_ref, bf16[512,256]{1,0:T(8,128)(2,1)} %get-tuple-element.22.crem_ref, bf16[4,128,256]{2,1,0:T(8,128)(2,1)} %copy-done, ...), custom_call_target="tpu_custom_call" | custom-call | tf_op jit(solution)/shard_map/local/pallas_call | solution.py:303
  67.0 10.7 %local.2.refs_0_ = bf16[2,4,512,256]{3,2,1,0:T(8,128)(2,1)} custom-call(f32[4,1,512]{2,1,0:T(1,128)} %reshape.14.pos_ref, bf16[4,1536,256]{2,1,0:T(8,128)(2,1)} %bitcast.12, bf16[4,512,256]{2,1,0:T(8,128)(2,1)} %get-tuple-element.21.y_ref, bf16[512,256]{1,0:T(8,128)(2,1)} %get-tuple-element.22.crem_ref, bf16[4,128,256]{2,1,0:T(8,128)(2,1)} %copy-done, ...), custom_call_target="tpu_custom_call" | custom-call | tf_op jit(solution)/shard_map/local/pallas_call | solution.py:303
  77.8 6.1 %scatter.1 = (bf16[4,1536,256]{2,1,0:T(8,128)(2,1)}, f32[4,256,256]{2,1,0:T(8,128)}) custom-call(f32[8,512]{1,0:T(8,128)} %get-tuple-element.19.rest_ref, bf16[2,4,512,256]{3,2,1,0:T(8,128)(2,1)} %local.2.refs_0_, bf16[2,4,512,256]{3,2,1,0:T(8,128)(2,1)} %local.3.refs_1_), custom_call_target="tpu_custom_call" | custom-call | tf_op jit(solution)/shard_map/scatter/pallas_call | solution.py:347
  83.9 0.0 all-to-all-done.1.sums_ref
  83.9 0.0 copy-start.2
  83.9 0.7 copy-done.2
  84.5 3.4 %coef.1 = (bf16[2,128,256]{2,1,0:T(8,128)(2,1)}, bf16[4,128,256]{2,1,0:T(8,128)(2,1)}, bf16[4,128,256]{2,1,0:T(8,128)(2,1)}) custom-call(s32[4]{0:T(128)} %block_ref.3, s32[1]{0:T(128)} %bitcast.3.place_ref, bf16[32,16,128]{2,1,0:T(8,128)(2,1)} %copy-done.2, bf16[4,16,2,32,32]{4,3,2,1,0:T(8,128)(2,1)} %pad_maximum_fusion.inv_ref, ...), custom_call_target="tpu_custom_call" | custom-call | tf_op jit(solution)/shard_map/coef/pallas_call | solution.py:408
  87.9 2.7 %collective-permute-start.5 = (bf16[4,128,256]{2,1,0:T(8,128)(2,1)}, bf16[4,128,256]{2,1,0:T(8,128)(2,1)S(1)}, u32[]{:S(2)}, u32[]{:S(2)}) collective-permute-start(bf16[4,128,256]{2,1,0:T(8,128)(2,1)} %get-tuple-element.31), channel_id=1, source_target_pairs={{0,31},{1,0},{2,1},{3,2},{4,3},{5,4},{6,5},{7,6},{8,7},{9,8},{10,9... | collective-permute-start | bytes 786440 | tf_op jit(solution)/shard_map/ppermute | solution.py:19
  90.6 0.0 collective-permute-start.6
  90.6 4.2 %collective-permute-done.5.above_ref = bf16[4,128,256]{2,1,0:T(8,128)(2,1)S(1)} collective-permute-done((bf16[4,128,256]{2,1,0:T(8,128)(2,1)}, bf16[4,128,256]{2,1,0:T(8,128)(2,1)S(1)}, u32[]{:S(2)}, u32[]{:S(2)}) %collective-permute-start.5) | collective-permute-done | bytes 262176 | tf_op jit(solution)/shard_map/ppermute | solution.py:19
  94.8 0.0 copy-start.3
  94.8 5.4 %collective-permute-done.6.below_ref = bf16[4,128,256]{2,1,0:T(8,128)(2,1)S(1)} collective-permute-done((bf16[4,128,256]{2,1,0:T(8,128)(2,1)}, bf16[4,128,256]{2,1,0:T(8,128)(2,1)S(1)}, u32[]{:S(2)}, u32[]{:S(2)}) %collective-permute-start.6) | collective-permute-done | bytes 262176 | tf_op jit(solution)/shard_map/ppermute | solution.py:19
  100.2 0.0 copy-start.4
  100.2 0.0 copy-done.3
  100.2 0.7 copy-done.4
  100.9 5.9 %finish.1 = bf16[4,1536,256]{2,1,0:T(8,128)(2,1)} custom-call(s32[2,128]{1,0:T(2,128)} %bitcast.19, bf16[4,1536,256]{2,1,0:T(8,128)(2,1)} %get-tuple-element.25.own_ref, bf16[4,1792,128]{2,1,0:T(8,128)(2,1)} %get-tuple-element.26.brem_ref.b_ref, bf16[2,128,256]{2,1,0:T(8,128)(2,1)} %get-tuple-element.30.coef_ref, bf16[4,128,256]{2,1,0:T(8,128)(2,1)} %copy-done.3, ...), custom_call_target="tpu_custom_call" | custom-call | tf_op jit(solution)/shard_map/finish/pallas_call | solution.py:456
Async XLA Ops:
  4.5 34.9 %copy-start.5 = (bf16[16,2,32,32]{3,2,1,0:T(8,128)(2,1)S(1)}, bf16[16,2,32,32]{3,2,1,0:T(8,128)(2,1)}, u32[]{:S(2)}) copy-start(bf16[16,2,32,32]{3,2,1,0:T(8,128)(2,1)} %param.10) | copy-start | bytes 196612
  4.5 14.6 %collective-permute-start = (bf16[4,128,256]{2,1,0:T(8,128)(2,1)}, bf16[4,128,256]{2,1,0:T(8,128)(2,1)S(1)}, u32[]{:S(2)}, u32[]{:S(2)}) collective-permute-start(bf16[4,128,256]{2,1,0:T(8,128)(2,1)} %get-tuple-element.23), channel_id=1, source_target_pairs={{0,1},{1,2},{2,3},{3,4},{4,5},{5,6},{6,7},{7,8},{8,9},{9,10},{10,1... | collective-permute-start | bytes 786440 | tf_op jit(solution)/shard_map/ppermute | solution.py:19
  5.0 14.1 %collective-permute-start.1 = (bf16[4,128,256]{2,1,0:T(8,128)(2,1)}, bf16[4,128,256]{2,1,0:T(8,128)(2,1)S(1)}, u32[]{:S(2)}, u32[]{:S(2)}) collective-permute-start(bf16[4,128,256]{2,1,0:T(8,128)(2,1)} %get-tuple-element.24), channel_id=1, source_target_pairs={{0,31},{1,0},{2,1},{3,2},{4,3},{5,4},{6,5},{7,6},{8,7},{9,8},{10,9... | collective-permute-start | bytes 786440 | tf_op jit(solution)/shard_map/ppermute | solution.py:19
  19.1 0.7 copy-start
  19.1 0.8 copy-start.1
  36.9 47.0 %all-to-all-start.1 = ((bf16[32,16,128]{2,1,0:T(8,128)(2,1)}), bf16[32,16,128]{2,1,0:T(8,128)(2,1)S(1)}, u32[]{:S(2)}, u32[]{:S(2)}) async-start(bf16[32,16,128]{2,1,0:T(8,128)(2,1)} %sums.1), calls=%async_computation.1 | async-start | bytes 262144 | tf_op jit(solution)/shard_map/all_to_all | solution.py:506
  39.4 9.0 %collective-permute-start.2 = (bf16[16,2,32,32]{3,2,1,0:T(8,128)(2,1)S(1)}, bf16[16,2,32,32]{3,2,1,0:T(8,128)(2,1)S(1)}, u32[]{:S(2)}, u32[]{:S(2)}) collective-permute-start(bf16[16,2,32,32]{3,2,1,0:T(8,128)(2,1)S(1)} %copy-done.5), channel_id=1, source_target_pairs={{0,3},{1,0},{2,1},{3,2},{4,7},{5,4},{6,5},{7,6},{8,11},{9,8},{10,9... | collective-permute-start | bytes 196616 | tf_op jit(solution)/shard_map/ppermute | solution.py:19
  41.0 14.1 %collective-permute-start.3 = (bf16[16,2,32,32]{3,2,1,0:T(8,128)(2,1)S(1)}, bf16[16,2,32,32]{3,2,1,0:T(8,128)(2,1)S(1)}, u32[]{:S(2)}, u32[]{:S(2)}) collective-permute-start(bf16[16,2,32,32]{3,2,1,0:T(8,128)(2,1)S(1)} %copy-done.5), channel_id=1, source_target_pairs={{0,2},{1,3},{2,0},{3,1},{4,6},{5,7},{6,4},{7,5},{8,10},{9,11},{10,... | collective-permute-start | bytes 196616 | tf_op jit(solution)/shard_map/ppermute | solution.py:19
  41.4 13.7 %collective-permute-start.4 = (bf16[16,2,32,32]{3,2,1,0:T(8,128)(2,1)S(1)}, bf16[16,2,32,32]{3,2,1,0:T(8,128)(2,1)S(1)}, u32[]{:S(2)}, u32[]{:S(2)}) collective-permute-start(bf16[16,2,32,32]{3,2,1,0:T(8,128)(2,1)S(1)} %copy-done.5), channel_id=1, source_target_pairs={{0,1},{1,2},{2,3},{3,0},{4,5},{5,6},{6,7},{7,4},{8,9},{9,10},{10,1... | collective-permute-start | bytes 196616 | tf_op jit(solution)/shard_map/ppermute | solution.py:19
  83.9 0.7 copy-start.2
  87.9 6.9 %collective-permute-start.5 = (bf16[4,128,256]{2,1,0:T(8,128)(2,1)}, bf16[4,128,256]{2,1,0:T(8,128)(2,1)S(1)}, u32[]{:S(2)}, u32[]{:S(2)}) collective-permute-start(bf16[4,128,256]{2,1,0:T(8,128)(2,1)} %get-tuple-element.31), channel_id=1, source_target_pairs={{0,31},{1,0},{2,1},{3,2},{4,3},{5,4},{6,5},{7,6},{8,7},{9,8},{10,9... | collective-permute-start | bytes 786440 | tf_op jit(solution)/shard_map/ppermute | solution.py:19
  90.6 9.6 %collective-permute-start.6 = (bf16[4,128,256]{2,1,0:T(8,128)(2,1)}, bf16[4,128,256]{2,1,0:T(8,128)(2,1)S(1)}, u32[]{:S(2)}, u32[]{:S(2)}) collective-permute-start(bf16[4,128,256]{2,1,0:T(8,128)(2,1)} %get-tuple-element.32), channel_id=1, source_target_pairs={{0,1},{1,2},{2,3},{3,4},{4,5},{5,6},{6,7},{7,8},{8,9},{9,10},{10,1... | collective-permute-start | bytes 786440 | tf_op jit(solution)/shard_map/ppermute | solution.py:19
  94.8 5.4 %copy-start.3 = (bf16[4,128,256]{2,1,0:T(8,128)(2,1)}, bf16[4,128,256]{2,1,0:T(8,128)(2,1)S(1)}, u32[]{:S(2)}) copy-start(bf16[4,128,256]{2,1,0:T(8,128)(2,1)S(1)} %collective-permute-done.5.above_ref) | copy-start | bytes 786436
  100.2 0.7 copy-start.4

commit v2 on v0

v2 whole, which is shorter than its diff:
```python
import functools

import jax
import jax.numpy as jnp
from jax import lax
from jax.experimental import pallas as pl
from jax.experimental.pallas import tpu as pltpu
from jax.sharding import PartitionSpec as P


AXES = ("patch", "coarse")
LANES = 128
MIB = 1 << 20
F32 = jnp.float32
BF16 = jnp.bfloat16


def passed_along(value, axis, steps):
    count = lax.axis_size(axis)
    pairs = [(source, (source + steps) % count) for source in range(count)]
    return lax.ppermute(value, axis, pairs)


def dot(a, b):
    return jnp.dot(a, b, preferred_element_type=F32)


def beside(parts):
    return jnp.concatenate(parts, axis=1)


def dot_in_halves(a_ref, b):
    half = b.shape[0] // 2
    return dot(a_ref[:, :half], b[:half]) + dot(a_ref[:, half:], b[half:])


def as_column(row):
    return jnp.transpose(jnp.broadcast_to(row, (LANES, row.shape[1])))


def iota(shape, axis):
    return lax.broadcasted_iota(jnp.int32, shape, axis)


def one_hot_rows(column, width, start=0):
    rows = column.shape[0]
    parts = [
        (column == (iota((rows, LANES), 1) + (start + t)).astype(F32)).astype(F32).astype(BF16)
        for t in range(0, width, LANES)
    ]
    return jnp.concatenate(parts, axis=1)


def vmem(shape, dtype):
    return pltpu.VMEM(shape, dtype)


def resident(array):
    return pltpu.with_memory_space_constraint(array, pltpu.VMEM)


def call(kernel, limit, smem, far, near, far_out, near_out, scratch=()):
    spaces = [pltpu.SMEM] * len(smem) + [pltpu.HBM] * len(far) + [pltpu.VMEM] * len(near)
    out_spaces = [pltpu.HBM] * len(far_out) + [pltpu.VMEM] * len(near_out)
    return pl.pallas_call(
        kernel,
        in_specs=[pl.BlockSpec(memory_space=m) for m in spaces],
        out_specs=[pl.BlockSpec(memory_space=m) for m in out_spaces],
        out_shape=[pltpu.HBM(*o) for o in far_out] + [vmem(*o) for o in near_out],
        scratch_shapes=list(scratch),
        compiler_params=pltpu.CompilerParams(vmem_limit_bytes=limit * MIB),
    )(
        *smem,
        *[pltpu.with_memory_space_constraint(a, pltpu.HBM) for a in far],
        *[resident(a) for a in near],
    )


def copy(source, target, sem):
    moved = pltpu.make_async_copy(source, target, sem)
    moved.start()
    return moved


def select_kernel(
    x_hbm, rows_hbm, slots_hbm, up_ref, down_ref, x_ref, slots_ref,
    rows_ref, arrived,
):
    slots = rows_ref.shape[1]
    parts, nodes, _ = x_ref.shape
    small = pltpu.make_async_copy(rows_hbm, rows_ref, arrived.at[parts])
    copies = [pltpu.make_async_copy(x_hbm.at[k], x_ref.at[k], arrived.at[k]) for k in range(parts)]
    later = pltpu.make_async_copy(slots_hbm, slots_ref, arrived.at[parts + 1])
    for copy in [small] + copies + [later]:
        copy.start()
    small.wait()
    pick = jnp.concatenate(
        [one_hot_rows(as_column(rows_ref[b : b + 1, :].astype(F32)), nodes) for b in range(2)], axis=0
    )
    width = x_ref.shape[2]
    for k in range(0, parts, 2):
        copies[k].wait()
        copies[k + 1].wait()
        got = dot(pick, beside([x_ref[k], x_ref[k + 1]])).astype(BF16)
        for j in range(2):
            up_ref[k + j] = got[:slots, j * width : (j + 1) * width]
            down_ref[k + j] = got[slots:, j * width : (j + 1) * width]
    later.wait()


def select_rows(x4, rows, patch_slots):
    parts, _, width = x4.shape
    slots = rows.shape[1]
    margin = vmem((parts, slots, width), BF16)
    kept = [vmem(a.shape, a.dtype) for a in (x4, patch_slots)]
    return pl.pallas_call(
        select_kernel,
        in_specs=[pl.BlockSpec(memory_space=pltpu.HBM)] * 3,
        out_specs=[pl.BlockSpec(memory_space=pltpu.VMEM)] * 4,
        out_shape=[margin, margin] + kept,
        scratch_shapes=[vmem(rows.shape, rows.dtype), pltpu.SemaphoreType.DMA((parts + 2,))],
        compiler_params=pltpu.CompilerParams(vmem_limit_bytes=6 * MIB),
        name="select",
    )(*[pltpu.with_memory_space_constraint(a, pltpu.HBM) for a in (x4, rows, patch_slots)])


def prep_kernel(
    basis_hbm, slots_ref, x_ref,
    crem_hbm, y_hbm, bext_hbm, pos_ref, rest_ref, r_ref, btrem_ref,
    ccat, bt, basis_ref, y_ref, bext_ref, sems,
):
    basis_in = copy(basis_hbm, basis_ref, sems.at[0])
    patches, patch_nodes = slots_ref.shape
    waves, width = basis_ref.shape[1], basis_ref.shape[2]
    parts, nodes, _ = x_ref.shape
    core = nodes // patches
    rest = patch_nodes - core
    ext = ccat.shape[1]
    slots = slots_ref[...].astype(F32)
    first = (iota((patches, patch_nodes), 0) * core).astype(F32)
    local = slots - first
    outside = (local < 0.0) | (local >= float(core))
    before = iota((patch_nodes, patch_nodes), 0) < iota((patch_nodes, patch_nodes), 1)
    rank = dot(outside.astype(F32).astype(BF16), before.astype(F32).astype(BF16))
    pos = jnp.where(outside, rank + float(core), local)
    pos_ref[...] = pos
    basis_in.wait()
    for p in range(patches):
        prow = pos[p : p + 1, :]
        srow = slots[p : p + 1, :]
        permute = one_hot_rows(as_column(prow), patch_nodes)
        basis = jnp.concatenate(
            [
                basis_ref[p, w, :, q * patch_nodes : (q + 1) * patch_nodes]
                for w in range(waves)
                for q in range(2)
            ],
            axis=0,
        )
        moved = dot(basis, permute).astype(BF16)
        hit = prow == (iota((rest, patch_nodes), 0) + core).astype(F32)
        ids = jnp.sum(
            jnp.where(hit, jnp.broadcast_to(srow, hit.shape), 0.0), axis=1, keepdims=True
        )
        ids = jnp.broadcast_to(ids, (rest, LANES))
        rest_ref[:, p * rest : (p + 1) * rest] = jnp.transpose(ids)[0:8]
        pick = one_hot_rows(ids, ext)
        ccat[p * rest : (p + 1) * rest, :] = pick
        spread = dot(moved[:, core:], pick).astype(BF16)
        for k in range(parts):
            rows = slice(k * width, (k + 1) * width)
            here = slice(p * width, (p + 1) * width)
            bt[k, here, :] = spread[rows]
            bt[k, here, p * core : (p + 1) * core] = (
                spread[rows, p * core : (p + 1) * core] + moved[rows, :core]
            )
    sent = [copy(ccat.at[:, pl.ds(nodes, ext - nodes)], crem_hbm, sems.at[1])]
    for k in range(parts):
        btrem_ref[k] = bt[k, :, nodes:]
        bext_ref[k] = jnp.transpose(bt[k])
        sent.append(copy(bext_ref.at[k], bext_hbm.at[k], sems.at[3 + 2 * k]))
    for k in range(0, parts, 2):
        both = dot(ccat[:, :nodes], beside([x_ref[k], x_ref[k + 1]])).astype(BF16)
        for j in range(2):
            y_ref[k + j] = both[:, j * x_ref.shape[2] : (j + 1) * x_ref.shape[2]]
    for k in range(parts):
        sent.append(copy(y_ref.at[k], y_hbm.at[k], sems.at[2 + 2 * k]))
    for w in range(waves):
        r_ref[w] = sum(dot(bt[k, :, :nodes], x_ref[k]) for k in (2 * w, 2 * w + 1))
    for moved in sent:
        moved.wait()


def prepare(slots, basis_t, x4, ext):
    parts, nodes, width = x4.shape
    patches, patch_nodes = slots.shape
    rest = patch_nodes - nodes // patches
    columns = patches * basis_t.shape[2]
    y = ((parts, patches * rest, width), BF16)
    b_ext = ((parts, ext, columns), BF16)
    return call(
        prep_kernel,
        12,
        [],
        [basis_t],
        [slots, x4],
        [((patches * rest, ext - nodes), BF16), y, b_ext],
        [
            ((patches, patch_nodes), F32),
            ((8, patches * rest), F32),
            ((parts // 2, columns, width), F32),
            ((parts, columns, ext - nodes), BF16),
        ],
        [
            vmem((patches * rest, ext), BF16),
            vmem((parts, columns, ext), BF16),
            vmem(basis_t.shape, BF16),
            vmem(*y),
            vmem(*b_ext),
            pltpu.SemaphoreType.DMA((2 + 2 * parts,)),
        ],
    )


def owner_order(columns, patches, width, per_group):
    rows = patches * per_group
    i = iota((columns, columns), 0)
    j = iota((columns, columns), 1)
    source = ((i % rows) // per_group) * width + (i // rows) * per_group + i % per_group
    return (source == j).astype(F32).astype(BF16)


def restrict_kernel(per_group, block_ref, r_ref, btrem_ref, below_ref, above_ref, inv_ref, out_ref):
    waves, columns, width = r_ref.shape
    patches = block_ref.shape[0]
    slots = below_ref.shape[1]
    rows = patches * per_group
    groups = columns // rows
    halves = width // LANES
    order = owner_order(columns, patches, columns // patches, per_group)
    tail = out_ref.shape[1] - rows
    keys = jnp.zeros((tail, LANES), F32)
    for p in range(patches):
        keys = jnp.where(iota((tail, LANES), 0) == p, block_ref[p].astype(F32), keys)
    for w in range(waves):
        total = r_ref[w]
        for q in range(2):
            k = 2 * w + q
            total = total + dot(btrem_ref[k, :, :slots], below_ref[k])
            total = total + dot(btrem_ref[k, :, slots:], above_ref[k])
        moved = dot(order, total.astype(BF16)).astype(BF16)
        for g in range(groups):
            last = (keys + inv_ref[w * groups + g]).astype(BF16)
            for h in range(halves):
                owner = (w * groups + g) * halves + h
                out_ref[owner, :rows, :] = moved[g * rows : (g + 1) * rows, h * LANES : (h + 1) * LANES]
                out_ref[owner, rows:, :] = last


def restrict(block, r_own, bt_rem, below, above, inv_rows, owners, per_group, padded):
    out = ((owners, padded, LANES), BF16)
    return call(
        functools.partial(restrict_kernel, per_group),
        3,
        [block],
        [],
        [r_own, bt_rem, below, above, inv_rows],
        [],
        [out],
    )[0]


def inverse_rows(coarse_inv, patches, per_group, tail, share):
    blocks, waves, size, _ = coarse_inv.shape
    count = lax.axis_size("patch")
    padded = jnp.pad(coarse_inv, ((0, count * share - blocks), (0, 0), (0, 0), (0, 0)))
    mine = lax.dynamic_slice_in_dim(padded, lax.axis_index("patch") * share, share, 0)
    mine = mine.reshape(share, waves, size, size // per_group, per_group)
    mine = mine.transpose(1, 3, 0, 4, 2).reshape(waves * (size // per_group), share, per_group * size)
    edges = ((0, 0), (patches, tail - patches - share), (0, LANES - per_group * size))
    return jnp.pad(mine.astype(F32), edges)


def sums_kernel(per_group, patches, coarse_count, blocks, share, got_ref, out_ref, data, tags):
    owners, padded, _ = got_ref.shape
    rows = patches * per_group
    tail = padded - rows
    for s in range(owners):
        data[s * rows : (s + 1) * rows, :] = got_ref[s, :rows, :].astype(F32)
        tags[s * tail : (s + 1) * tail, :] = got_ref[s, rows:, :].astype(F32)
    tag = tags[...].astype(BF16)
    count = owners * rows
    i = iota((count, owners * tail), 0)
    j = iota((count, owners * tail), 1)
    wanted = (i // rows) * tail + (i % rows) // per_group
    keys = dot((wanted == j).astype(F32).astype(BF16), tag)
    keys = keys * float(per_group) + (iota((count, LANES), 0) % per_group).astype(F32)
    key_row = jnp.transpose(keys)[0:1, :]
    column = jnp.concatenate([keys] * (count // LANES), axis=1)
    same = (column == key_row).astype(F32).astype(BF16)
    data[...] = dot(same, data[...].astype(BF16))

    pairs = owners * patches
    i = iota((pairs, owners * tail), 0)
    j = iota((pairs, owners * tail), 1)
    named = dot(((i // patches) * tail + i % patches == j).astype(F32).astype(BF16), tag)
    source, place = j // tail, j % tail - patches
    block = (source // coarse_count) * share + place
    held = (place >= 0) & (place < share) & (block < blocks)
    block = jnp.where(held, (source % coarse_count) * blocks + block, -1).astype(F32)
    if owners * tail >= LANES:
        named = jnp.concatenate([named] * (owners * tail // LANES), axis=1)
    tags[0:pairs, :] = dot((named == block).astype(F32).astype(BF16), tag)
    extra = out_ref.shape[1] - rows - patches
    for s in range(owners):
        out_ref[s, :rows, :] = data[s * rows : (s + 1) * rows, :].astype(BF16)
        last = tags[s * patches : (s + 1) * patches, :]
        if extra:
            last = jnp.concatenate([last, jnp.zeros((extra, LANES), F32)], axis=0)
        out_ref[s, rows:, :] = last.astype(BF16)


def owner_sums(got, patches, per_group, blocks, share):
    owners, padded, _ = got.shape
    rows = patches * per_group
    back = -(-(rows + patches) // 8) * 8
    out = ((owners, back, LANES), BF16)
    return call(
        functools.partial(
            sums_kernel, per_group, patches, lax.axis_size("coarse"), blocks, share
        ),
        6,
        [],
        [],
        [got],
        [],
        [out],
        [
            vmem((owners * rows, LANES), F32),
            vmem((owners * (padded - rows), LANES), F32),
        ],
    )[0]


def local_kernel(
    first, inv_hbm, x_hbm, y_hbm, crem_hbm, below_hbm, above_hbm, pos_ref,
    local_hbm, rest_hbm,
    g, inv_ref, x_ref, y_ref, crem_ref, far_ref, local_ref, rest_ref, order_ref, back_ref,
    sems, inv_sems, out_sems,
):
    parts, rows, width = x_ref.shape
    count, waves = inv_ref.shape[:2]
    patch_nodes = pos_ref.shape[1]
    core = rows // count
    rest = patch_nodes - core
    slots = below_hbm.shape[1]
    mine = pl.ds(first * rest, count * rest)
    small = [
        copy(crem_hbm.at[mine], crem_ref, sems.at[0]),
        copy(below_hbm, far_ref.at[:, pl.ds(0, slots)], sems.at[1]),
        copy(above_hbm, far_ref.at[:, pl.ds(slots, slots)], sems.at[2]),
        copy(y_hbm.at[:, mine], y_ref, sems.at[3]),
        copy(x_hbm.at[:, pl.ds(first * core, rows)], x_ref, sems.at[4]),
    ]
    inverses = {
        (i, w): copy(inv_hbm.at[first + i, w], inv_ref.at[i, w], inv_sems.at[i * waves + w])
        for i in range(count)
        for w in range(waves)
    }
    for i in range(count):
        prow = pos_ref[first + i : first + i + 1, :]
        order_ref[i] = one_hot_rows(as_column(prow), patch_nodes)
        places = (iota((rest, patch_nodes), 0) + core).astype(F32)
        back_ref[i] = (prow == places).astype(F32).astype(BF16)
    for moved in small:
        moved.wait()
    sent = []
    for i in range(count):
        here = slice(i * rest, (i + 1) * rest)
        for k in range(0, parts, 2):
            far = dot(crem_ref[here, :], beside([far_ref[k], far_ref[k + 1]]))
            other = beside([y_ref[k, here, :], y_ref[k + 1, here, :]]) + far.astype(BF16)
            rows = slice(i * core, (i + 1) * core)
            mine = beside([x_ref[k, rows, :], x_ref[k + 1, rows, :]])
            moved = dot(order_ref[i], jnp.concatenate([mine, other], axis=0)).astype(BF16)
            for j in range(2):
                at = (k + j) * patch_nodes
                g[at : at + patch_nodes, :] = moved[:, j * width : (j + 1) * width]
        for w in range(waves):
            inverses[i, w].wait()
        for w in range(waves):
            terms = g[2 * w * patch_nodes : 2 * (w + 1) * patch_nodes, :]
            local_ref[i, w] = dot_in_halves(inv_ref.at[i, w], terms).astype(BF16)
        for w in range(waves):
            pair = beside([local_ref[i, w, :patch_nodes, :], local_ref[i, w, patch_nodes:, :]])
            got = dot(back_ref[i], pair).astype(BF16)
            for j in range(2):
                rest_ref[2 * w + j, here, :] = got[:, j * width : (j + 1) * width]
            sent.append(copy(local_ref.at[i, w], local_hbm.at[i, w], out_sems.at[i, w]))
    sent.append(copy(rest_ref, rest_hbm, sems.at[0]))
    for moved in sent:
        moved.wait()


def local_products(pos, x4, y, crem, below, above, patch_inv, first, count):
    parts, nodes, width = x4.shape
    patches, patch_nodes = pos.shape
    core = nodes // patches
    rest = patch_nodes - core
    waves = patch_inv.shape[1]
    local = ((count, waves, 2 * patch_nodes, width), BF16)
    others = ((parts, count * rest, width), BF16)
    return call(
        functools.partial(local_kernel, first),
        24,
        [],
        [patch_inv, x4, y, crem, below, above],
        [pos],
        [local, others],
        [],
        [
            vmem((parts * patch_nodes, width), BF16),
            vmem((count,) + patch_inv.shape[1:], BF16),
            vmem((parts, count * core, width), BF16),
            vmem(*others),
            vmem((count * rest, crem.shape[1]), BF16),
            vmem((parts, crem.shape[1], width), BF16),
            vmem(*local),
            vmem(*others),
            vmem((count, patch_nodes, patch_nodes), BF16),
            vmem((count, rest, patch_nodes), BF16),
            pltpu.SemaphoreType.DMA((5,)),
            pltpu.SemaphoreType.DMA((count * waves,)),
            pltpu.SemaphoreType.DMA((count, waves)),
        ],
    )


def coef_kernel(
    per_group, patches, bext_hbm, *refs
):
    *other_hbm, sums_ref, rest_ref, coef_ref, low_ref, high_ref = refs[:-5]
    gathered, inverses, brem_ref, other_ref, sems = refs[-5:]
    slots = low_ref.shape[1]
    nodes = bext_hbm.shape[1] - 2 * slots
    arriving = [copy(bext_hbm.at[:, pl.ds(nodes, 2 * slots)], brem_ref, sems.at[0])]
    start = 0
    for i, other in enumerate(other_hbm):
        place = pl.ds(start, other.shape[1])
        arriving.append(copy(other, other_ref.at[:, place], sems.at[1 + i]))
        start += other.shape[1]
    waves, columns, width = coef_ref.shape
    size = columns // patches
    rows = patches * per_group
    groups = columns // rows
    halves = width // LANES
    held = groups * patches
    i = iota((columns, held), 0)
    j = iota((columns, held), 1)
    grow = ((i // rows) * patches + (i % rows) // per_group == j).astype(F32).astype(BF16)
    i = iota((columns, LANES), 0)
    j = iota((columns, LANES), 1)
    in_lanes = j // size == i % per_group
    fold = (iota((LANES, columns), 0) % size == iota((LANES, columns), 1) % size)
    fold = fold.astype(F32).astype(BF16)
    i = iota((columns, columns), 0)
    j = iota((columns, columns), 1)
    in_patch = j // size == (i % rows) // per_group
    ids = rest_ref[0:1, :]
    reach = (2 * slots, ids.shape[1])
    spread = (ids == (iota(reach, 0) + nodes).astype(F32)).astype(F32).astype(BF16)
    for w in range(waves):
        for g in range(groups):
            for h in range(halves):
                owner = (w * groups + g) * halves + h
                gathered[g * rows : (g + 1) * rows, h * LANES : (h + 1) * LANES] = sums_ref[
                    owner, :rows, :
                ].astype(F32)
            inverses[g * patches : (g + 1) * patches, :] = sums_ref[
                (w * groups + g) * halves, rows : rows + patches, :
            ].astype(F32)
        grown = dot(grow, inverses[...].astype(BF16))
        folded = dot(jnp.where(in_lanes, grown, 0.0).astype(BF16), fold)
        inverse = jnp.transpose(jnp.where(in_patch, folded, 0.0)).astype(BF16)
        coef = dot(inverse, gathered[...].astype(BF16)).astype(BF16)
        coef_ref[w] = coef
        if w == 0:
            for moved in arriving:
                moved.wait()
        for q in range(2):
            k = 2 * w + q
            margin = (dot(spread, other_ref[k]) + dot(brem_ref[k], coef)).astype(BF16)
            low_ref[k] = margin[:slots]
            high_ref[k] = margin[slots:]


def coefficients(sums, b_ext, rest_ids, others, patches, slots, per_group):
    parts, _, columns = b_ext.shape
    width = others[0].shape[2]
    groups = columns // (patches * per_group)
    margin = ((parts, slots, width), BF16)
    return call(
        functools.partial(coef_kernel, per_group, patches),
        6,
        [],
        [b_ext] + others,
        [sums, rest_ids],
        [],
        [((parts // 2, columns, width), BF16), margin, margin],
        [
            vmem((columns, width), F32),
            vmem((groups * patches, LANES), F32),
            vmem((parts, 2 * slots, columns), BF16),
            vmem((parts, rest_ids.shape[1], width), BF16),
            pltpu.SemaphoreType.DMA((1 + len(others),)),
        ],
    )


def own_kernel(bext_hbm, *refs):
    *pairs, rest_ref, pos_ref, coef_ref, out_ref, bown_ref, local_ref, other_ref, sems = refs
    half = len(pairs) // 2
    parts, nodes, _ = out_ref.shape
    patches, patch_nodes = pos_ref.shape
    core = nodes // patches
    arriving = []
    for k in range(parts):
        moves = [(bext_hbm.at[k, pl.ds(0, nodes)], bown_ref.at[k])]
        start = 0
        for a in pairs[half:]:
            moves.append((a.at[k], other_ref.at[k, pl.ds(start, a.shape[1])]))
            start += a.shape[1]
        start = 0
        terms = pl.ds((k % 2) * patch_nodes, patch_nodes)
        for a in pairs[:half]:
            here = pl.ds(start, a.shape[0])
            moves.append((a.at[:, k // 2, terms], local_ref.at[k, here]))
            start += a.shape[0]
        arriving.append([copy(a, b, sems.at[k, i]) for i, (a, b) in enumerate(moves)])
    ids = rest_ref[0:1, :]
    shape = (nodes, ids.shape[1])
    spread = (ids == iota(shape, 0).astype(F32)).astype(F32).astype(BF16)
    places = iota((core, patch_nodes), 0).astype(F32)
    backs = [
        (pos_ref[p : p + 1, :] == places).astype(F32).astype(BF16) for p in range(patches)
    ]
    width = out_ref.shape[2]
    for k in range(0, parts, 2):
        for moved in arriving[k] + arriving[k + 1]:
            moved.wait()
        total = dot(spread, beside([other_ref[k], other_ref[k + 1]]))
        cores = [
            dot(backs[p], beside([local_ref[k, p], local_ref[k + 1, p]])) for p in range(patches)
        ]
        total = total + jnp.concatenate(cores, axis=0)
        for j in range(2):
            coarse = dot(bown_ref[k + j], coef_ref[(k + j) // 2])
            out_ref[k + j] = total[:, j * width : (j + 1) * width] + coarse


def own_rows(b_ext, coef, rest_ids, pos, locals_, others, nodes):
    parts, _, columns = b_ext.shape
    width = coef.shape[2]
    return call(
        own_kernel,
        20,
        [],
        [b_ext] + locals_ + others,
        [rest_ids, pos, coef],
        [],
        [((parts, nodes, width), F32)],
        [
            vmem((parts, nodes, columns), BF16),
            vmem((parts,) + pos.shape + (width,), BF16),
            vmem((parts, rest_ids.shape[1], width), BF16),
            pltpu.SemaphoreType.DMA((parts, 1 + len(locals_) + len(others))),
        ],
    )[0]


def final_kernel(rows_ref, own_ref, above_ref, below_ref, out_ref, spread):
    slots = rows_ref.shape[1]
    nodes = own_ref.shape[1]
    k = pl.program_id(0)

    @pl.when(k == 0)
    def _():
        for b in range(2):
            ids = rows_ref[b : b + 1, :].astype(F32)
            spread[:, b * slots : (b + 1) * slots] = (
                (ids == iota((nodes, slots), 0).astype(F32)).astype(F32).astype(BF16)
            )

    back = jnp.concatenate([above_ref[k], below_ref[k]], axis=0)
    out_ref[0] = (own_ref[k] + dot(spread[...], back)).astype(BF16)


def finish(rows, own, above, below):
    parts, nodes, width = own.shape
    spec = pl.BlockSpec(memory_space=pltpu.VMEM)
    return pl.pallas_call(
        final_kernel,
        grid=(parts,),
        in_specs=[spec] * 4,
        out_specs=pl.BlockSpec((1, nodes, width), lambda i: (i, 0, 0)),
        out_shape=jax.ShapeDtypeStruct((parts, nodes, width), BF16),
        scratch_shapes=[vmem((nodes, 2 * rows.shape[1]), BF16)],
        compiler_params=pltpu.CompilerParams(vmem_limit_bytes=8 * MIB),
        name="finish",
    )(*[resident(a) for a in (rows, own, above, below)])


def per_device(residual, patch_inv, coarse_basis, coarse_inv, patch_slots, send_rows, coarse_block):
    waves, _, nodes, width = residual.shape
    patches = patch_inv.shape[0]
    size = coarse_basis.shape[3]
    slots = send_rows.shape[2]
    ext = nodes + 2 * slots
    owners = lax.axis_size(AXES)
    halves = width // LANES
    groups = owners // (waves * halves)
    per_group = size // groups
    assert groups * waves * halves == owners and per_group * groups == size
    blocks = coarse_inv.shape[0]
    share = -(-blocks // lax.axis_size("patch"))
    rows = patches * per_group
    padded = -(-(rows + patches + share) // 8) * 8
    half = patches // 2
    send = send_rows[0]
    basis_t = jnp.swapaxes(coarse_basis, 2, 3)

    x_all = residual.reshape(2 * waves, nodes, width)
    up, down, x4, slots_v = select_rows(x_all, send, patch_slots)
    below = passed_along(up, AXES, 1)
    above = passed_along(down, AXES, -1)
    crem, y, b_ext, pos, rest_ids, r_own, bt_rem = prepare(slots_v, basis_t, x4, ext)
    inv_rows = inverse_rows(coarse_inv, patches, per_group, padded - rows, share)
    sent = restrict(coarse_block, r_own, bt_rem, below, above, inv_rows, owners, per_group, padded)
    got = lax.all_to_all(sent, AXES, 0, 0, tiled=True)
    local_a, rest_a = local_products(pos, x_all, y, crem, below, above, patch_inv, 0, half)
    sums = owner_sums(got, patches, per_group, blocks, share)
    mine = lax.all_to_all(sums, AXES, 0, 0, tiled=True)
    local_b, rest_b = local_products(
        pos, x_all, y, crem, below, above, patch_inv, half, patches - half
    )
    coef, low, high = coefficients(
        mine, b_ext, rest_ids, [rest_a, rest_b], patches, slots, per_group
    )
    back_above = passed_along(low, AXES, -1)
    back_below = passed_along(high, AXES, 1)
    own = own_rows(b_ext, coef, rest_ids, pos, [local_a, local_b], [rest_a, rest_b], nodes)
    out = finish(send, own, back_above, back_below)
    return out.reshape(residual.shape)


def solution(mesh):
    placed = (
        P(None, None, AXES, None),
        P(AXES, None, None, None),
        P(AXES, None, None, None),
        P("coarse", None, None, None),
        P(AXES, None),
        P(AXES, None, None),
        P(AXES),
    )
    return jax.shard_map(
        per_device,
        mesh=mesh,
        in_specs=placed,
        out_specs=P(None, None, AXES, None),
        check_vma=False,
    )
```

time: 257 us -> 73 us (0.28)
  waiting for transfers between devices: 98.6 us -> 2.83 us
  matrix products: 84.9 us -> 0 us
  Pallas kernels: 0 us -> 42.4 us
  local copies, waits for them, and re-layouts: 42.4 us -> 0.21 us
  between operations: 13.5 us -> 0.12 us
  starting transfers between devices: 7.39 us -> 14.4 us
  blocking collectives: 9.23 us -> 12.7 us
    psum x1 -> x0, waiting for transfers between devices: 91.1 us -> none  [per_device(): totals = lax.psum(partial_sums, ('patch', 'coarse'))]
    dot_general x15 -> x0, matrix products: 84.9 us -> none  [the longest x3 23.4 us: spread_rows(): jnp.einsum(form, selector, upper_part, preferred_element_type=jnp.float32)]
    pallas_call x0 -> x9, Pallas kernels: none -> 42.4 us  [the longest x7 35.9 us: call(): pl.pallas_call(kernel, in_specs=[pl.BlockSpec(memory_space=m) for m in sp...]
    reshape x2 -> x0, local copies, waits for them, and re-layouts: 28.4 us -> none  [the longest x1 28 us: per_device(): patch_inv.reshape(patches, wave_count, 2, patch_nodes, 2, patch_nodes)]
    all_to_all x0 -> x1, blocking collectives: none -> 12.7 us  [per_device(): got = lax.all_to_all(sent, AXES, 0, 0, tiled=True)]
    all_gather x1 -> x0, blocking collectives: 9.23 us -> none  [per_device(): inverses = lax.all_gather(coarse_inv, 'coarse', axis=0, tiled=True)]
    unnamed x15 -> x7, local copies, waits for them, and re-layouts: 8.05 us -> 0.11 us
    ppermute x4, waiting for transfers between devices: 7.54 us -> 2.82 us  [passed_along(): return lax.ppermute(value, axis, pairs)]
  transfers between devices with their start and end apart: 5 -> 5, of which waited for: 4 -> 1; matrix products, arithmetic and copies ran while one was open for 21% -> 0% of each run, Pallas kernels for 0% -> 42%
where the time goes in v2:
time: 73 us; the launch traced here: 72.7 us
  Pallas kernels  42.4 us (58%)
  starting transfers between devices  14.4 us (20%)
  blocking collectives  12.7 us (17%)
  waiting for transfers between devices  2.83 us (4%)
    pallas_call x7, Pallas kernels, call(): pl.pallas_call(kernel, in_specs=[pl.BlockSpec(memory_space=m) for m in sp...  35.9 us
    all_to_all x1, blocking collectives, per_device(): got = lax.all_to_all(sent, AXES, 0, 0, tiled=True)  12.7 us
    ppermute x4, starting transfers between devices, passed_along(): return lax.ppermute(value, axis, pairs)  11.6 us
    pallas_call x1, Pallas kernels, select_rows(): pl.pallas_call(select_kernel, in_specs=[pl.BlockSpec(memory_space=pltpu.H...  3.42 us
    pallas_call x1, Pallas kernels, finish(): pl.pallas_call(final_kernel, grid=(parts,), in_specs=[spec] * 4, out_spec...  3.1 us
    ppermute x4, waiting for transfers between devices, passed_along(): return lax.ppermute(value, axis, pairs)  2.82 us
    all_to_all x1, starting transfers between devices, per_device(): mine = lax.all_to_all(sums, AXES, 0, 0, tiled=True)  2.8 us
  transfers between devices with their start and end apart: 5, of which 1 were waited for; matrix products, arithmetic and copies ran while one was open for 0% of the time, Pallas kernels for 42%

profile of v2, /device:TPU:0, one launch (start us, length us, event | category | flops | bytes accessed | tf_op | source)
XLA Modules:
  0.0 72.7 jit_solution(11851100762153724837)
XLA Ops:
  0.0 0.0 copy-start
  0.0 0.0 copy-start.2
  0.0 3.4 %select.2 = (bf16[4,128,256]{2,1,0:T(8,128)(2,1)}, bf16[4,128,256]{2,1,0:T(8,128)(2,1)}, bf16[4,1536,256]{2,1,0:T(8,128)(2,1)S(1)}, s32[4,512]{1,0:T(4,128)S(1)}) custom-call(bf16[4,1536,256]{2,1,0:T(8,128)(2,1)} %bitcast.11, s32[2,128]{1,0:T(2,128)} %bitcast.9, s32[4,512]{1,0:T(4,128)} %slots_hbm.1), custom_call_target="tpu_custom_call" | custom-call | tf_op jit(solution)/shard_map/select/pallas_call | solution.py:116
  3.4 0.5 collective-permute-start
  4.0 6.0 %collective-permute-start.1 = (bf16[4,128,256]{2,1,0:T(8,128)(2,1)}, bf16[4,128,256]{2,1,0:T(8,128)(2,1)}, u32[]{:S(2)}, u32[]{:S(2)}) collective-permute-start(bf16[4,128,256]{2,1,0:T(8,128)(2,1)} %get-tuple-element.29), channel_id=1, source_target_pairs={{0,31},{1,0},{2,1},{3,2},{4,3},{5,4},{6,5},{7,6},{8,7},{9,8},{10,9... | collective-permute-start | bytes 786440 | tf_op jit(solution)/shard_map/ppermute | solution.py:21
  10.0 0.0 copy-done
  10.0 0.1 copy.11
  10.1 0.1 reshape.14
  10.2 5.9 %shard_map.73 = (bf16[512,256]{1,0:T(8,128)(2,1)}, bf16[4,512,256]{2,1,0:T(8,128)(2,1)}, bf16[4,1792,128]{2,1,0:T(8,128)(2,1)}, f32[4,512]{1,0:T(4,128)S(1)}, f3...) custom-call(bf16[4,2,32,1024]{3,2,1,0:T(8,128)(2,1)} %bitcast.14, ...), custom_call_target="tpu_custom_call" | custom-call | tf_op jit(solution)/shard_map/pallas_call | solution.py:65
  16.1 0.0 collective-permute-done.below_hbm.below_ref
  16.1 0.0 collective-permute-done.1.above_hbm.above_ref
  16.1 0.0 copy-done.2
  16.1 1.7 %shard_map.76 = bf16[32,24,128]{2,1,0:T(8,128)(2,1)S(1)} custom-call(s32[4]{0:T(128)S(1)} %copy-done.2, f32[2,128,256]{2,1,0:T(8,128)S(1)} %get-tuple-element.36.r_ref, bf16[4,128,256]{2,1,0:T(8,128)(2,1)S(1)} %get-tuple-element.37.btrem_ref, bf16[4,128,256]{2,1,0:T(8,128)(2,1)} %collective-permute-done.below_hbm.below_ref, ...), custom_call_target="tpu_custom_call" | custom-call | tf_op jit(solution)/shard_map/pallas_call | solution.py:65
  17.9 12.7 %all_to_all.10.got_ref = bf16[32,24,128]{2,1,0:T(8,128)(2,1)S(1)} all-to-all(bf16[32,24,128]{2,1,0:T(8,128)(2,1)S(1)} %shard_map.76), channel_id=1, replica_groups=mesh['patch'=8,'coarse'=4] {'patch','coarse'}, dimensions={0} | all-to-all | bytes 393216 | tf_op jit(solution)/shard_map/all_to_all | solution.py:639
  30.5 1.3 %shard_map.77 = bf16[32,24,128]{2,1,0:T(8,128)(2,1)} custom-call(bf16[32,24,128]{2,1,0:T(8,128)(2,1)S(1)} %all_to_all.10.got_ref), custom_call_target="tpu_custom_call" | custom-call | tf_op jit(solution)/shard_map/pallas_call | solution.py:65
  31.8 2.8 %all-to-all-start.1 = ((bf16[32,24,128]{2,1,0:T(8,128)(2,1)}), bf16[32,24,128]{2,1,0:T(8,128)(2,1)S(1)}, u32[]{:S(2)}, u32[]{:S(2)}) async-start(bf16[32,24,128]{2,1,0:T(8,128)(2,1)} %shard_map.77), calls=%async_computation.1 | async-start | bytes 393216 | tf_op jit(solution)/shard_map/all_to_all | solution.py:642
  34.6 9.0 %shard_map.75 = (bf16[2,2,1024,256]{3,2,1,0:T(8,128)(2,1)}, bf16[4,256,256]{2,1,0:T(8,128)(2,1)}) custom-call(bf16[4,2,1024,1024]{3,2,1,0:T(8,128)(2,1)} %inv_hbm.3, bf16[4,1536,256]{2,1,0:T(8,128)(2,1)} %bitcast.12, bf16[4,512,256]{2,1,0:T(8,128)(2,1)} %get-tuple-element.26.y_hbm, bf16[512,256]{1,0:T(8,128)(2,1)} %get-tuple-element.27.crem_hbm, ...), custom_call_target="tpu_custom_call" | custom-call | tf_op jit(solution)/shard_map/pallas_call | solution.py:65
  43.7 9.0 %shard_map.74 = (bf16[2,2,1024,256]{3,2,1,0:T(8,128)(2,1)}, bf16[4,256,256]{2,1,0:T(8,128)(2,1)}) custom-call(bf16[4,2,1024,1024]{3,2,1,0:T(8,128)(2,1)} %inv_hbm.3, bf16[4,1536,256]{2,1,0:T(8,128)(2,1)} %bitcast.13, bf16[4,512,256]{2,1,0:T(8,128)(2,1)} %get-tuple-element.26.y_hbm, bf16[512,256]{1,0:T(8,128)(2,1)} %get-tuple-element.27.crem_hbm, ...), custom_call_target="tpu_custom_call" | custom-call | tf_op jit(solution)/shard_map/pallas_call | solution.py:65
  52.7 0.0 all-to-all-done.1.refs_2_
  52.7 2.3 %shard_map.78 = (bf16[2,128,256]{2,1,0:T(8,128)(2,1)S(1)}, bf16[4,128,256]{2,1,0:T(8,128)(2,1)S(1)}, bf16[4,128,256]{2,1,0:T(8,128)(2,1)S(1)}) custom-call(bf16[4,1792,128]{2,1,0:T(8,128)(2,1)} %get-tuple-element.25.bext_hbm, bf16[4,256,256]{2,1,0:T(8,128)(2,1)} %get-tuple-element.33.refs_0_.refs_2_, bf16[4,256,256]{2,1,0:T(8,128)(2,1)} %get-tuple-element.34.refs_1_.refs_3_, ...), custom_call_target="tpu_custom_call" | custom-call | tf_op jit(solution)/shard_map/pallas_call | solution.py:65
  55.1 5.1 %collective-permute-start.2 = (bf16[4,128,256]{2,1,0:T(8,128)(2,1)S(1)}, bf16[4,128,256]{2,1,0:T(8,128)(2,1)S(1)}, u32[]{:S(2)}, u32[]{:S(2)}) collective-permute-start(bf16[4,128,256]{2,1,0:T(8,128)(2,1)S(1)} %get-tuple-element.39), channel_id=1, source_target_pairs={{0,31},{1,0},{2,1},{3,2},{4,3},{5,4},{6,5},{7,6},{8,7},{9,8},{10,9... | collective-permute-start | bytes 786440 | tf_op jit(solution)/shard_map/ppermute | solution.py:21
  60.2 0.0 collective-permute-start.3
  60.2 0.0 copy-start.1
  60.2 6.6 %shard_map.79.own_ref = f32[4,1536,256]{2,1,0:T(8,128)S(1)} custom-call(bf16[4,1792,128]{2,1,0:T(8,128)(2,1)} %get-tuple-element.25.bext_hbm, bf16[2,2,1024,256]{3,2,1,0:T(8,128)(2,1)} %get-tuple-element.31.refs_0_, bf16[2,2,1024,256]{3,2,1,0:T(8,128)(2,1)} %get-tuple-element.32.refs_1_, bf16[4,256,256]{2,1,0:T(8,128)(2,1)} %get-tuple-element.33.refs_0_.refs_2_, ...), custom_call_target="tpu_custom_call" | custom-call | tf_op jit(solution)/shard_map/pallas_call | solution.py:65
  66.7 0.0 collective-permute-done.2.above_ref
  66.7 2.8 %collective-permute-done.3.below_ref = bf16[4,128,256]{2,1,0:T(8,128)(2,1)S(1)} collective-permute-done((bf16[4,128,256]{2,1,0:T(8,128)(2,1)S(1)}, bf16[4,128,256]{2,1,0:T(8,128)(2,1)S(1)}, u32[]{:S(2)}, u32[]{:S(2)}) %collective-permute-start.3) | collective-permute-done | bytes 262176 | tf_op jit(solution)/shard_map/ppermute | solution.py:21
  69.6 0.0 copy-done.1
  69.6 3.1 %finish.1 = bf16[4,1536,256]{2,1,0:T(8,128)(2,1)} custom-call(s32[2,128]{1,0:T(2,128)S(1)} %bitcast.10, f32[4,1536,256]{2,1,0:T(8,128)S(1)} %shard_map.79.own_ref, bf16[4,128,256]{2,1,0:T(8,128)(2,1)S(1)} %collective-permute-done.2.above_ref, bf16[4,128,256]{2,1,0:T(8,128)(2,1)S(1)} %collective-permute-done.3.below_ref), custom_call_target="tpu_custom_call" | custom-call | tf_op jit(solution)/shard_map/finish/pallas_call | solution.py:601
  (3 shorter events, 0.0 us)
Async XLA Ops:
  0.0 10.0 %copy-start = (bf16[16,2,32,32]{3,2,1,0:T(8,128)(2,1)S(1)}, bf16[16,2,32,32]{3,2,1,0:T(8,128)(2,1)}, u32[]{:S(2)}) copy-start(bf16[16,2,32,32]{3,2,1,0:T(8,128)(2,1)} %param.10) | copy-start | bytes 196612
  0.0 16.1 %copy-start.2 = (s32[4]{0:T(128)S(1)}, s32[4]{0:T(128)}, u32[]{:S(2)}) copy-start(s32[4]{0:T(128)} %block_ref.1) | copy-start | bytes 52
  3.4 12.6 %collective-permute-start = (bf16[4,128,256]{2,1,0:T(8,128)(2,1)}, bf16[4,128,256]{2,1,0:T(8,128)(2,1)}, u32[]{:S(2)}, u32[]{:S(2)}) collective-permute-start(bf16[4,128,256]{2,1,0:T(8,128)(2,1)} %get-tuple-element.28), channel_id=1, source_target_pairs={{0,1},{1,2},{2,3},{3,4},{4,5},{5,6},{6,7},{7,8},{8,9},{9,10},{10,1... | collective-permute-start | bytes 786440 | tf_op jit(solution)/shard_map/ppermute | solution.py:21
  4.0 12.1 %collective-permute-start.1 = (bf16[4,128,256]{2,1,0:T(8,128)(2,1)}, bf16[4,128,256]{2,1,0:T(8,128)(2,1)}, u32[]{:S(2)}, u32[]{:S(2)}) collective-permute-start(bf16[4,128,256]{2,1,0:T(8,128)(2,1)} %get-tuple-element.29), channel_id=1, source_target_pairs={{0,31},{1,0},{2,1},{3,2},{4,3},{5,4},{6,5},{7,6},{8,7},{9,8},{10,9... | collective-permute-start | bytes 786440 | tf_op jit(solution)/shard_map/ppermute | solution.py:21
  31.8 20.9 %all-to-all-start.1 = ((bf16[32,24,128]{2,1,0:T(8,128)(2,1)}), bf16[32,24,128]{2,1,0:T(8,128)(2,1)S(1)}, u32[]{:S(2)}, u32[]{:S(2)}) async-start(bf16[32,24,128]{2,1,0:T(8,128)(2,1)} %shard_map.77), calls=%async_computation.1 | async-start | bytes 393216 | tf_op jit(solution)/shard_map/all_to_all | solution.py:642
  55.1 11.6 %collective-permute-start.2 = (bf16[4,128,256]{2,1,0:T(8,128)(2,1)S(1)}, bf16[4,128,256]{2,1,0:T(8,128)(2,1)S(1)}, u32[]{:S(2)}, u32[]{:S(2)}) collective-permute-start(bf16[4,128,256]{2,1,0:T(8,128)(2,1)S(1)} %get-tuple-element.39), channel_id=1, source_target_pairs={{0,31},{1,0},{2,1},{3,2},{4,3},{5,4},{6,5},{7,6},{8,7},{9,8},{10,9... | collective-permute-start | bytes 786440 | tf_op jit(solution)/shard_map/ppermute | solution.py:21
  60.2 9.4 %collective-permute-start.3 = (bf16[4,128,256]{2,1,0:T(8,128)(2,1)S(1)}, bf16[4,128,256]{2,1,0:T(8,128)(2,1)S(1)}, u32[]{:S(2)}, u32[]{:S(2)}) collective-permute-start(bf16[4,128,256]{2,1,0:T(8,128)(2,1)S(1)} %get-tuple-element.40), channel_id=1, source_target_pairs={{0,1},{1,2},{2,3},{3,4},{4,5},{5,6},{6,7},{7,8},{8,9},{9,10},{10,1... | collective-permute-start | bytes 786440 | tf_op jit(solution)/shard_map/ppermute | solution.py:21
  60.2 9.4 %copy-start.1 = (s32[1,2,128]{2,1,0:T(2,128)S(1)}, s32[1,2,128]{2,1,0:T(2,128)}, u32[]{:S(2)}) copy-start(s32[1,2,128]{2,1,0:T(2,128)} %param.12) | copy-start | bytes 3076

commit v3 on v2

--- a/solution.py
+++ b/solution.py
@@ -76,9 +76,9 @@
     )
 
 
-def copy(source, target, sem):
+def copy(source, target, sem, priority=0):
     moved = pltpu.make_async_copy(source, target, sem)
-    moved.start()
+    moved.start(priority=priority)
     return moved
 
 
@@ -125,11 +125,13 @@
 
 
 def prep_kernel(
-    basis_hbm, slots_ref, x_ref,
-    crem_hbm, y_hbm, bext_hbm, pos_ref, rest_ref, r_ref, btrem_ref,
-    ccat, bt, basis_ref, y_ref, bext_ref, sems,
+    per_group, share, place_ref, basis_hbm, inv_hbm, slots_ref, x_ref,
+    crem_hbm, y_hbm, bext_hbm, pos_ref, rest_ref, r_ref, btrem_ref, lines_ref,
+    ccat, bt, basis_ref, y_ref, bext_ref, order_ref, inv_ref, square, sems,
 ):
     basis_in = copy(basis_hbm, basis_ref, sems.at[0])
+    held = jnp.minimum(place_ref[0] * share, inv_hbm.shape[0] - share)
+    inv_in = copy(inv_hbm.at[pl.ds(held, share)], inv_ref, sems.at[4])
     patches, patch_nodes = slots_ref.shape
     waves, width = basis_ref.shape[1], basis_ref.shape[2]
     parts, nodes, _ = x_ref.shape
@@ -144,11 +146,20 @@
     rank = dot(outside.astype(F32).astype(BF16), before.astype(F32).astype(BF16))
     pos = jnp.where(outside, rank + float(core), local)
     pos_ref[...] = pos
+    for p in range(patches):
+        prow = pos[p : p + 1, :]
+        order_ref[p] = one_hot_rows(as_column(prow), patch_nodes)
+        hit = prow == (iota((rest, patch_nodes), 0) + core).astype(F32)
+        ids = jnp.sum(
+            jnp.where(hit, jnp.broadcast_to(slots[p : p + 1, :], hit.shape), 0.0),
+            axis=1,
+            keepdims=True,
+        )
+        ids = jnp.broadcast_to(ids, (rest, LANES))
+        rest_ref[:, p * rest : (p + 1) * rest] = jnp.transpose(ids)[0:8]
+        ccat[p * rest : (p + 1) * rest, :] = one_hot_rows(ids, ext)
     basis_in.wait()
     for p in range(patches):
-        prow = pos[p : p + 1, :]
-        srow = slots[p : p + 1, :]
-        permute = one_hot_rows(as_column(prow), patch_nodes)
         basis = jnp.concatenate(
             [
                 basis_ref[p, w, :, q * patch_nodes : (q + 1) * patch_nodes]
@@ -157,16 +168,8 @@
             ],
             axis=0,
         )
-        moved = dot(basis, permute).astype(BF16)
-        hit = prow == (iota((rest, patch_nodes), 0) + core).astype(F32)
-        ids = jnp.sum(
-            jnp.where(hit, jnp.broadcast_to(srow, hit.shape), 0.0), axis=1, keepdims=True
-        )
-        ids = jnp.broadcast_to(ids, (rest, LANES))
-        rest_ref[:, p * rest : (p + 1) * rest] = jnp.transpose(ids)[0:8]
-        pick = one_hot_rows(ids, ext)
-        ccat[p * rest : (p + 1) * rest, :] = pick
-        spread = dot(moved[:, core:], pick).astype(BF16)
+        moved = dot(basis, order_ref[p]).astype(BF16)
+        spread = dot(moved[:, core:], ccat[p * rest : (p + 1) * rest, :]).astype(BF16)
         for k in range(parts):
             rows = slice(k * width, (k + 1) * width)
             here = slice(p * width, (p + 1) * width)
@@ -174,35 +177,47 @@
             bt[k, here, p * core : (p + 1) * core] = (
                 spread[rows, p * core : (p + 1) * core] + moved[rows, :core]
             )
-    sent = [copy(ccat.at[:, pl.ds(nodes, ext - nodes)], crem_hbm, sems.at[1])]
-    for k in range(parts):
-        btrem_ref[k] = bt[k, :, nodes:]
-        bext_ref[k] = jnp.transpose(bt[k])
-        sent.append(copy(bext_ref.at[k], bext_hbm.at[k], sems.at[3 + 2 * k]))
     for k in range(0, parts, 2):
         both = dot(ccat[:, :nodes], beside([x_ref[k], x_ref[k + 1]])).astype(BF16)
         for j in range(2):
             y_ref[k + j] = both[:, j * x_ref.shape[2] : (j + 1) * x_ref.shape[2]]
-    for k in range(parts):
-        sent.append(copy(y_ref.at[k], y_hbm.at[k], sems.at[2 + 2 * k]))
+            btrem_ref[k + j] = bt[k + j, :, nodes:]
+            bext_ref[k + j] = jnp.transpose(bt[k + j])
+    inv_in.wait()
+    lines_ref[...] = jnp.zeros(lines_ref.shape, F32)
+    for w in range(waves):
+        for t in range(share):
+            square[...] = inv_ref[t, w].astype(F32)
+            for c in range(per_group):
+                lines_ref[w * share + t, :, c * width : (c + 1) * width] = square[
+                    pl.ds(c, width // per_group, stride=per_group), :
+                ]
+    sent = [
+        copy(ccat.at[:, pl.ds(nodes, ext - nodes)], crem_hbm, sems.at[1]),
+        copy(y_ref, y_hbm, sems.at[2]),
+        copy(bext_ref, bext_hbm, sems.at[3]),
+    ]
     for w in range(waves):
         r_ref[w] = sum(dot(bt[k, :, :nodes], x_ref[k]) for k in (2 * w, 2 * w + 1))
     for moved in sent:
         moved.wait()
 
 
-def prepare(slots, basis_t, x4, ext):
+def prepare(slots, basis_t, coarse_inv, x4, ext, per_group, share):
     parts, nodes, width = x4.shape
     patches, patch_nodes = slots.shape
     rest = patch_nodes - nodes // patches
     columns = patches * basis_t.shape[2]
     y = ((parts, patches * rest, width), BF16)
     b_ext = ((parts, ext, columns), BF16)
+    size = coarse_inv.shape[3]
+    waves = coarse_inv.shape[1]
+    assert coarse_inv.shape[0] % share == 0
     return call(
-        prep_kernel,
-        12,
-        [],
-        [basis_t],
+        functools.partial(prep_kernel, per_group, share),
+        16,
+        [lax.axis_index("patch").astype(jnp.int32).reshape(1)],
+        [basis_t, coarse_inv],
         [slots, x4],
         [((patches * rest, ext - nodes), BF16), y, b_ext],
         [
@@ -210,6 +225,7 @@
             ((8, patches * rest), F32),
             ((parts // 2, columns, width), F32),
             ((parts, columns, ext - nodes), BF16),
+            ((waves * share, size // per_group, LANES), F32),
         ],
         [
             vmem((patches * rest, ext), BF16),
@@ -217,7 +233,10 @@
             vmem(basis_t.shape, BF16),
             vmem(*y),
             vmem(*b_ext),
-            pltpu.SemaphoreType.DMA((2 + 2 * parts,)),
+            vmem((patches, patch_nodes, patch_nodes), BF16),
+            vmem((share,) + coarse_inv.shape[1:], BF16),
+            vmem((size, size), F32),
+            pltpu.SemaphoreType.DMA((5,)),
         ],
     )
 
@@ -230,18 +249,26 @@
     return (source == j).astype(F32).astype(BF16)
 
 
-def restrict_kernel(per_group, block_ref, r_ref, btrem_ref, below_ref, above_ref, inv_ref, out_ref):
+def restrict_kernel(
+    per_group, block_ref, r_ref, btrem_ref, below_ref, above_ref, lines_ref,
+    far_hbm, out_hbm, out_ref, sems,
+):
     waves, columns, width = r_ref.shape
     patches = block_ref.shape[0]
     slots = below_ref.shape[1]
     rows = patches * per_group
     groups = columns // rows
     halves = width // LANES
+    sent = [
+        copy(below_ref, far_hbm.at[:, pl.ds(0, slots)], sems.at[0]),
+        copy(above_ref, far_hbm.at[:, pl.ds(slots, slots)], sems.at[1]),
+    ]
     order = owner_order(columns, patches, columns // patches, per_group)
     tail = out_ref.shape[1] - rows
     keys = jnp.zeros((tail, LANES), F32)
     for p in range(patches):
         keys = jnp.where(iota((tail, LANES), 0) == p, block_ref[p].astype(F32), keys)
+    share = lines_ref.shape[0] // waves
     for w in range(waves):
         total = r_ref[w]
         for q in range(2):
@@ -250,35 +277,34 @@
             total = total + dot(btrem_ref[k, :, slots:], above_ref[k])
         moved = dot(order, total.astype(BF16)).astype(BF16)
         for g in range(groups):
-            last = (keys + inv_ref[w * groups + g]).astype(BF16)
+            last = keys
+            for t in range(share):
+                line = jnp.broadcast_to(lines_ref[w * share + t, g : g + 1, :], keys.shape)
+                last = jnp.where(iota((tail, LANES), 0) == patches + t, line, last)
+            last = last.astype(BF16)
             for h in range(halves):
                 owner = (w * groups + g) * halves + h
                 out_ref[owner, :rows, :] = moved[g * rows : (g + 1) * rows, h * LANES : (h + 1) * LANES]
                 out_ref[owner, rows:, :] = last
-
-
-def restrict(block, r_own, bt_rem, below, above, inv_rows, owners, per_group, padded):
+        part = pl.ds(w * groups * halves, groups * halves)
+        sent.append(copy(out_ref.at[part], out_hbm.at[part], sems.at[2 + w], 1))
+    for copied in sent:
+        copied.wait()
+
+
+def restrict(block, r_own, bt_rem, below, above, lines, owners, per_group, padded):
+    parts, slots, width = below.shape
     out = ((owners, padded, LANES), BF16)
     return call(
         functools.partial(restrict_kernel, per_group),
         3,
         [block],
         [],
-        [r_own, bt_rem, below, above, inv_rows],
-        [],
-        [out],
-    )[0]
-
-
-def inverse_rows(coarse_inv, patches, per_group, tail, share):
-    blocks, waves, size, _ = coarse_inv.shape
-    count = lax.axis_size("patch")
-    padded = jnp.pad(coarse_inv, ((0, count * share - blocks), (0, 0), (0, 0), (0, 0)))
-    mine = lax.dynamic_slice_in_dim(padded, lax.axis_index("patch") * share, share, 0)
-    mine = mine.reshape(share, waves, size, size // per_group, per_group)
-    mine = mine.transpose(1, 3, 0, 4, 2).reshape(waves * (size // per_group), share, per_group * size)
-    edges = ((0, 0), (patches, tail - patches - share), (0, LANES - per_group * size))
-    return jnp.pad(mine.astype(F32), edges)
+        [r_own, bt_rem, below, above, lines],
+        [((parts, 2 * slots, width), BF16), out],
+        [],
+        [vmem(*out), pltpu.SemaphoreType.DMA((2 + r_own.shape[0],))],
+    )
 
 
 def sums_kernel(per_group, patches, coarse_count, blocks, share, got_ref, out_ref, data, tags):
@@ -343,7 +369,7 @@
 
 
 def local_kernel(
-    first, inv_hbm, x_hbm, y_hbm, crem_hbm, below_hbm, above_hbm, pos_ref,
+    first, inv_hbm, x_hbm, y_hbm, crem_hbm, far_hbm, pos_ref,
     local_hbm, rest_hbm,
     g, inv_ref, x_ref, y_ref, crem_ref, far_ref, local_ref, rest_ref, order_ref, back_ref,
     sems, inv_sems, out_sems,
@@ -353,17 +379,15 @@
     patch_nodes = pos_ref.shape[1]
     core = rows // count
     rest = patch_nodes - core
-    slots = below_hbm.shape[1]
     mine = pl.ds(first * rest, count * rest)
     small = [
         copy(crem_hbm.at[mine], crem_ref, sems.at[0]),
-        copy(below_hbm, far_ref.at[:, pl.ds(0, slots)], sems.at[1]),
-        copy(above_hbm, far_ref.at[:, pl.ds(slots, slots)], sems.at[2]),
-        copy(y_hbm.at[:, mine], y_ref, sems.at[3]),
-        copy(x_hbm.at[:, pl.ds(first * core, rows)], x_ref, sems.at[4]),
+        copy(far_hbm, far_ref, sems.at[1]),
+        copy(y_hbm.at[:, mine], y_ref, sems.at[2]),
+        copy(x_hbm.at[:, pl.ds(first * core, rows)], x_ref, sems.at[3]),
     ]
     inverses = {
-        (i, w): copy(inv_hbm.at[first + i, w], inv_ref.at[i, w], inv_sems.at[i * waves + w])
+        (i, w): copy(inv_hbm.at[first + i, w], inv_ref.at[i, w], inv_sems.at[i * waves + w], 1)
         for i in range(count)
         for w in range(waves)
     }
@@ -374,7 +398,6 @@
         back_ref[i] = (prow == places).astype(F32).astype(BF16)
     for moved in small:
         moved.wait()
-    sent = []
     for i in range(count):
         here = slice(i * rest, (i + 1) * rest)
         for k in range(0, parts, 2):
@@ -385,24 +408,27 @@
             moved = dot(order_ref[i], jnp.concatenate([mine, other], axis=0)).astype(BF16)
             for j in range(2):
                 at = (k + j) * patch_nodes
-                g[at : at + patch_nodes, :] = moved[:, j * width : (j + 1) * width]
+                g[i, at : at + patch_nodes, :] = moved[:, j * width : (j + 1) * width]
+    sent = []
+    for i in range(count):
+        here = slice(i * rest, (i + 1) * rest)
         for w in range(waves):
             inverses[i, w].wait()
         for w in range(waves):
-            terms = g[2 * w * patch_nodes : 2 * (w + 1) * patch_nodes, :]
+            terms = g[i, 2 * w * patch_nodes : 2 * (w + 1) * patch_nodes, :]
             local_ref[i, w] = dot_in_halves(inv_ref.at[i, w], terms).astype(BF16)
+        sent.append(copy(local_ref.at[i], local_hbm.at[i], out_sems.at[i]))
         for w in range(waves):
             pair = beside([local_ref[i, w, :patch_nodes, :], local_ref[i, w, patch_nodes:, :]])
             got = dot(back_ref[i], pair).astype(BF16)
             for j in range(2):
                 rest_ref[2 * w + j, here, :] = got[:, j * width : (j + 1) * width]
-            sent.append(copy(local_ref.at[i, w], local_hbm.at[i, w], out_sems.at[i, w]))
     sent.append(copy(rest_ref, rest_hbm, sems.at[0]))
     for moved in sent:
         moved.wait()
 
 
-def local_products(pos, x4, y, crem, below, above, patch_inv, first, count):
+def local_products(pos, x4, y, crem, far, patch_inv, first, count):
     parts, nodes, width = x4.shape
     patches, patch_nodes = pos.shape
     core = nodes // patches
@@ -414,12 +440,12 @@
         functools.partial(local_kernel, first),
         24,
         [],
-        [patch_inv, x4, y, crem, below, above],
+        [patch_inv, x4, y, crem, far],
         [pos],
         [local, others],
         [],
         [
-            vmem((parts * patch_nodes, width), BF16),
+            vmem((count, parts * patch_nodes, width), BF16),
             vmem((count,) + patch_inv.shape[1:], BF16),
             vmem((parts, count * core, width), BF16),
             vmem(*others),
@@ -429,9 +455,9 @@
             vmem(*others),
             vmem((count, patch_nodes, patch_nodes), BF16),
             vmem((count, rest, patch_nodes), BF16),
-            pltpu.SemaphoreType.DMA((5,)),
+            pltpu.SemaphoreType.DMA((4,)),
             pltpu.SemaphoreType.DMA((count * waves,)),
-            pltpu.SemaphoreType.DMA((count, waves)),
+            pltpu.SemaphoreType.DMA((count,)),
         ],
     )
 
@@ -457,15 +483,14 @@
     held = groups * patches
     i = iota((columns, held), 0)
     j = iota((columns, held), 1)
-    grow = ((i // rows) * patches + (i % rows) // per_group == j).astype(F32).astype(BF16)
-    i = iota((columns, LANES), 0)
-    j = iota((columns, LANES), 1)
-    in_lanes = j // size == i % per_group
-    fold = (iota((LANES, columns), 0) % size == iota((LANES, columns), 1) % size)
-    fold = fold.astype(F32).astype(BF16)
+    grow = ((i % size) // per_group * patches + i // size == j).astype(F32).astype(BF16)
+    in_lanes = iota((columns, LANES), 1) // size == iota((columns, LANES), 0) % per_group
+    i = iota((LANES, columns), 0)
+    j = iota((LANES, columns), 1)
+    fold = (i % size == (j // rows) * per_group + j % per_group).astype(F32).astype(BF16)
     i = iota((columns, columns), 0)
     j = iota((columns, columns), 1)
-    in_patch = j // size == (i % rows) // per_group
+    in_patch = (j % rows) // per_group == i // size
     ids = rest_ref[0:1, :]
     reach = (2 * slots, ids.shape[1])
     spread = (ids == (iota(reach, 0) + nodes).astype(F32)).astype(F32).astype(BF16)
@@ -481,7 +506,7 @@
             ].astype(F32)
         grown = dot(grow, inverses[...].astype(BF16))
         folded = dot(jnp.where(in_lanes, grown, 0.0).astype(BF16), fold)
-        inverse = jnp.transpose(jnp.where(in_patch, folded, 0.0)).astype(BF16)
+        inverse = jnp.where(in_patch, folded, 0.0).astype(BF16)
         coef = dot(inverse, gathered[...].astype(BF16)).astype(BF16)
         coef_ref[w] = coef
         if w == 0:
@@ -518,7 +543,7 @@
 
 
 def own_kernel(bext_hbm, *refs):
-    *pairs, rest_ref, pos_ref, coef_ref, out_ref, bown_ref, local_ref, other_ref, sems = refs
+    *pairs, rows_ref, rest_ref, pos_ref, coef_ref, out_ref, back_ref, bown_ref, local_ref, other_ref, sems = refs
     half = len(pairs) // 2
     parts, nodes, _ = out_ref.shape
     patches, patch_nodes = pos_ref.shape
@@ -534,9 +559,15 @@
         terms = pl.ds((k % 2) * patch_nodes, patch_nodes)
         for a in pairs[:half]:
             here = pl.ds(start, a.shape[0])
-            moves.append((a.at[:, k // 2, terms], local_ref.at[k, here]))
+            moves.append((a.at[:, k // 2, terms], local_ref.at[k, here], 1))
             start += a.shape[0]
-        arriving.append([copy(a, b, sems.at[k, i]) for i, (a, b) in enumerate(moves)])
+        arriving.append([copy(m[0], m[1], sems.at[k, i], *m[2:]) for i, m in enumerate(moves)])
+    slots = rows_ref.shape[1]
+    for b in range(2):
+        ids = rows_ref[b : b + 1, :].astype(F32)
+        back_ref[:, b * slots : (b + 1) * slots] = (
+            (ids == iota((nodes, slots), 0).astype(F32)).astype(F32).astype(BF16)
+        )
     ids = rest_ref[0:1, :]
     shape = (nodes, ids.shape[1])
     spread = (ids == iota(shape, 0).astype(F32)).astype(F32).astype(BF16)
@@ -558,7 +589,7 @@
             out_ref[k + j] = total[:, j * width : (j + 1) * width] + coarse
 
 
-def own_rows(b_ext, coef, rest_ids, pos, locals_, others, nodes):
+def own_rows(b_ext, coef, rows, rest_ids, pos, locals_, others, nodes):
     parts, _, columns = b_ext.shape
     width = coef.shape[2]
     return call(
@@ -566,48 +597,45 @@
         20,
         [],
         [b_ext] + locals_ + others,
-        [rest_ids, pos, coef],
-        [],
-        [((parts, nodes, width), F32)],
+        [rows, rest_ids, pos, coef],
+        [],
+        [((parts, nodes, width), F32), ((nodes, 2 * rows.shape[1]), BF16)],
         [
             vmem((parts, nodes, columns), BF16),
             vmem((parts,) + pos.shape + (width,), BF16),
             vmem((parts, rest_ids.shape[1], width), BF16),
             pltpu.SemaphoreType.DMA((parts, 1 + len(locals_) + len(others))),
         ],
+    )
+
+
+def final_kernel(own_ref, spread_ref, above_ref, below_ref, out_hbm, out_ref, sems):
+    parts, _, width = own_ref.shape
+    sent = []
+    for k in range(0, parts, 2):
+        back = jnp.concatenate(
+            [beside([a[k], a[k + 1]]) for a in (above_ref, below_ref)], axis=0
+        )
+        total = dot(spread_ref[...], back)
+        for j in range(2):
+            mine = total[:, j * width : (j + 1) * width]
+            out_ref[k + j] = (own_ref[k + j] + mine).astype(BF16)
+            sent.append(copy(out_ref.at[k + j], out_hbm.at[k + j], sems.at[k + j]))
+    for moved in sent:
+        moved.wait()
+
+
+def finish(own, spread, above, below):
+    return call(
+        final_kernel,
+        12,
+        [],
+        [],
+        [own, spread, above, below],
+        [(own.shape, BF16)],
+        [],
+        [vmem(own.shape, BF16), pltpu.SemaphoreType.DMA((own.shape[0],))],
     )[0]
-
-
-def final_kernel(rows_ref, own_ref, above_ref, below_ref, out_ref, spread):
-    slots = rows_ref.shape[1]
-    nodes = own_ref.shape[1]
-    k = pl.program_id(0)
-
-    @pl.when(k == 0)
-    def _():
-        for b in range(2):
-            ids = rows_ref[b : b + 1, :].astype(F32)
-            spread[:, b * slots : (b + 1) * slots] = (
-                (ids == iota((nodes, slots), 0).astype(F32)).astype(F32).astype(BF16)
-            )
-
-    back = jnp.concatenate([above_ref[k], below_ref[k]], axis=0)
-    out_ref[0] = (own_ref[k] + dot(spread[...], back)).astype(BF16)
-
-
-def finish(rows, own, above, below):
-    parts, nodes, width = own.shape
-    spec = pl.BlockSpec(memory_space=pltpu.VMEM)
-    return pl.pallas_call(
-        final_kernel,
-        grid=(parts,),
-        in_specs=[spec] * 4,
-        out_specs=pl.BlockSpec((1, nodes, width), lambda i: (i, 0, 0)),
-        out_shape=jax.ShapeDtypeStruct((parts, nodes, width), BF16),
-        scratch_shapes=[vmem((nodes, 2 * rows.shape[1]), BF16)],
-        compiler_params=pltpu.CompilerParams(vmem_limit_bytes=8 * MIB),
-        name="finish",
-    )(*[resident(a) for a in (rows, own, above, below)])
 
 
 def per_device(residual, patch_inv, coarse_basis, coarse_inv, patch_slots, send_rows, coarse_block):
@@ -633,23 +661,24 @@
     up, down, x4, slots_v = select_rows(x_all, send, patch_slots)
     below = passed_along(up, AXES, 1)
     above = passed_along(down, AXES, -1)
-    crem, y, b_ext, pos, rest_ids, r_own, bt_rem = prepare(slots_v, basis_t, x4, ext)
-    inv_rows = inverse_rows(coarse_inv, patches, per_group, padded - rows, share)
-    sent = restrict(coarse_block, r_own, bt_rem, below, above, inv_rows, owners, per_group, padded)
+    crem, y, b_ext, pos, rest_ids, r_own, bt_rem, lines = prepare(
+        slots_v, basis_t, coarse_inv, x4, ext, per_group, share
+    )
+    far, sent = restrict(
+        coarse_block, r_own, bt_rem, below, above, lines, owners, per_group, padded
+    )
     got = lax.all_to_all(sent, AXES, 0, 0, tiled=True)
-    local_a, rest_a = local_products(pos, x_all, y, crem, below, above, patch_inv, 0, half)
+    local_a, rest_a = local_products(pos, x_all, y, crem, far, patch_inv, 0, half)
     sums = owner_sums(got, patches, per_group, blocks, share)
     mine = lax.all_to_all(sums, AXES, 0, 0, tiled=True)
-    local_b, rest_b = local_products(
-        pos, x_all, y, crem, below, above, patch_inv, half, patches - half
-    )
+    local_b, rest_b = local_products(pos, x_all, y, crem, far, patch_inv, half, patches - half)
     coef, low, high = coefficients(
         mine, b_ext, rest_ids, [rest_a, rest_b], patches, slots, per_group
     )
     back_above = passed_along(low, AXES, -1)
     back_below = passed_along(high, AXES, 1)
-    own = own_rows(b_ext, coef, rest_ids, pos, [local_a, local_b], [rest_a, rest_b], nodes)
-    out = finish(send, own, back_above, back_below)
+    own, spread = own_rows(b_ext, coef, send, rest_ids, pos, [local_a, local_b], [rest_a, rest_b], nodes)
+    out = finish(own, spread, back_above, back_below)
     return out.reshape(residual.shape)
 
 

time: 73 us -> 69.5 us (0.952)
  Pallas kernels: 42.4 us -> 38.9 us
    pallas_call x1 -> x0, Pallas kernels: 3.1 us -> none  [finish(): pl.pallas_call(final_kernel, grid=(parts,), in_specs=[spec] * 4, out_spec...]
    pallas_call x7 -> x8, Pallas kernels: 35.9 us -> 35.5 us  [call(): pl.pallas_call(kernel, in_specs=[pl.BlockSpec(memory_space=m) for m in sp...]
  transfers between devices with their start and end apart: 5 -> 5, of which waited for: 1 -> 1; matrix products, arithmetic and copies ran while one was open for 0% -> 0% of each run, Pallas kernels for 42% -> 39%
where the time goes in v3:
time: 69.5 us; the launch traced here: 69.2 us
  Pallas kernels  38.9 us (56%)
  starting transfers between devices  14.4 us (21%)
  blocking collectives  13.2 us (19%)
  waiting for transfers between devices  2.45 us (4%)
    pallas_call x8, Pallas kernels, call(): pl.pallas_call(kernel, in_specs=[pl.BlockSpec(memory_space=m) for m in sp...  35.5 us
    all_to_all x1, blocking collectives, per_device(): got = lax.all_to_all(sent, AXES, 0, 0, tiled=True)  13.2 us
    ppermute x4, starting transfers between devices, passed_along(): return lax.ppermute(value, axis, pairs)  11.6 us
    pallas_call x1, Pallas kernels, select_rows(): pl.pallas_call(select_kernel, in_specs=[pl.BlockSpec(memory_space=pltpu.H...  3.4 us
    all_to_all x1, starting transfers between devices, per_device(): mine = lax.all_to_all(sums, AXES, 0, 0, tiled=True)  2.8 us
    ppermute x4, waiting for transfers between devices, passed_along(): return lax.ppermute(value, axis, pairs)  2.45 us
  transfers between devices with their start and end apart: 5, of which 1 were waited for; matrix products, arithmetic and copies ran while one was open for 0% of the time, Pallas kernels for 39%

profile of v3, /device:TPU:0, one launch (start us, length us, event | category | flops | bytes accessed | tf_op | source)
XLA Modules:
  0.0 69.2 jit_solution(74334522053105770)
XLA Ops:
  0.0 0.0 copy-start.1
  0.0 3.4 %select.1 = (bf16[4,128,256]{2,1,0:T(8,128)(2,1)}, bf16[4,128,256]{2,1,0:T(8,128)(2,1)}, bf16[4,1536,256]{2,1,0:T(8,128)(2,1)S(1)}, s32[4,512]{1,0:T(4,128)S(1)}) custom-call(bf16[4,1536,256]{2,1,0:T(8,128)(2,1)} %bitcast.7, s32[2,128]{1,0:T(2,128)} %bitcast.5, s32[4,512]{1,0:T(4,128)} %slots_hbm.1), custom_call_target="tpu_custom_call" | custom-call | tf_op jit(solution)/shard_map/select/pallas_call | solution.py:116
  3.4 0.5 collective-permute-start
  4.0 6.0 %collective-permute-start.1 = (bf16[4,128,256]{2,1,0:T(8,128)(2,1)}, bf16[4,128,256]{2,1,0:T(8,128)(2,1)}, u32[]{:S(2)}, u32[]{:S(2)}) collective-permute-start(bf16[4,128,256]{2,1,0:T(8,128)(2,1)} %get-tuple-element.36), channel_id=1, source_target_pairs={{0,31},{1,0},{2,1},{3,2},{4,3},{5,4},{6,5},{7,6},{8,7},{9,8},{10,9... | collective-permute-start | bytes 786440 | tf_op jit(solution)/shard_map/ppermute | solution.py:21
  9.9 5.8 %shard_map.73 = (bf16[512,256]{1,0:T(8,128)(2,1)}, bf16[4,512,256]{2,1,0:T(8,128)(2,1)}, bf16[4,1792,128]{2,1,0:T(8,128)(2,1)}, f32[4,512]{1,0:T(4,128)S(1)}, f3...) custom-call(s32[1]{0:T(128)} %bitcast.place_ref, ...), custom_call_target="tpu_custom_call" | custom-call | tf_op jit(solution)/shard_map/pallas_call | solution.py:65
  15.8 0.0 collective-permute-done.below_ref
  15.8 0.0 collective-permute-done.1.above_ref
  15.8 0.0 copy-done.1
  15.8 2.3 %shard_map.74 = (bf16[4,256,256]{2,1,0:T(8,128)(2,1)}, bf16[32,24,128]{2,1,0:T(8,128)(2,1)}) custom-call(s32[4]{0:T(128)S(1)} %copy-done.1, f32[2,128,256]{2,1,0:T(8,128)S(1)} %get-tuple-element.33.r_ref, bf16[4,128,256]{2,1,0:T(8,128)(2,1)S(1)} %get-tuple-element.34.btrem_ref, bf16[4,128,256]{2,1,0:T(8,128)(2,1)S(1)} %collective-permute-done.below_ref, ...), custom_call_target="tpu_custom_call" | custom-call | tf_op jit(solution)/shard_map/pallas_call | solution.py:65
  18.2 13.2 %all_to_all.10.got_ref = bf16[32,24,128]{2,1,0:T(8,128)(2,1)S(1)} all-to-all(bf16[32,24,128]{2,1,0:T(8,128)(2,1)} %get-tuple-element.45), channel_id=1, replica_groups=mesh['patch'=8,'coarse'=4] {'patch','coarse'}, dimensions={0} | all-to-all | bytes 393216 | tf_op jit(solution)/shard_map/all_to_all | solution.py:670
  31.3 1.3 %shard_map.77 = bf16[32,24,128]{2,1,0:T(8,128)(2,1)} custom-call(bf16[32,24,128]{2,1,0:T(8,128)(2,1)S(1)} %all_to_all.10.got_ref), custom_call_target="tpu_custom_call" | custom-call | tf_op jit(solution)/shard_map/pallas_call | solution.py:65
  32.6 2.8 %all-to-all-start.1 = ((bf16[32,24,128]{2,1,0:T(8,128)(2,1)}), bf16[32,24,128]{2,1,0:T(8,128)(2,1)S(1)}, u32[]{:S(2)}, u32[]{:S(2)}) async-start(bf16[32,24,128]{2,1,0:T(8,128)(2,1)} %shard_map.77), calls=%async_computation.1 | async-start | bytes 393216 | tf_op jit(solution)/shard_map/all_to_all | solution.py:673
  35.4 7.3 %shard_map.76 = (bf16[2,2,1024,256]{3,2,1,0:T(8,128)(2,1)}, bf16[4,256,256]{2,1,0:T(8,128)(2,1)}) custom-call(bf16[4,2,1024,1024]{3,2,1,0:T(8,128)(2,1)} %inv_hbm.5, bf16[4,1536,256]{2,1,0:T(8,128)(2,1)} %bitcast.8, bf16[4,512,256]{2,1,0:T(8,128)(2,1)} %get-tuple-element.31.y_hbm, bf16[512,256]{1,0:T(8,128)(2,1)} %get-tuple-element.32.crem_hbm, ...), custom_call_target="tpu_custom_call" | custom-call | tf_op jit(solution)/shard_map/pallas_call | solution.py:65
  42.7 0.0 copy-start
  42.7 7.2 %shard_map.75 = (bf16[2,2,1024,256]{3,2,1,0:T(8,128)(2,1)}, bf16[4,256,256]{2,1,0:T(8,128)(2,1)}) custom-call(bf16[4,2,1024,1024]{3,2,1,0:T(8,128)(2,1)} %inv_hbm.5, bf16[4,1536,256]{2,1,0:T(8,128)(2,1)} %bitcast.9, bf16[4,512,256]{2,1,0:T(8,128)(2,1)} %get-tuple-element.31.y_hbm, bf16[512,256]{1,0:T(8,128)(2,1)} %get-tuple-element.32.crem_hbm, ...), custom_call_target="tpu_custom_call" | custom-call | tf_op jit(solution)/shard_map/pallas_call | solution.py:65
  50.0 0.0 all-to-all-done.1.refs_2_
  50.0 2.3 %shard_map.78 = (bf16[2,128,256]{2,1,0:T(8,128)(2,1)S(1)}, bf16[4,128,256]{2,1,0:T(8,128)(2,1)S(1)}, bf16[4,128,256]{2,1,0:T(8,128)(2,1)S(1)}) custom-call(bf16[4,1792,128]{2,1,0:T(8,128)(2,1)} %get-tuple-element.30.bext_hbm, bf16[4,256,256]{2,1,0:T(8,128)(2,1)} %get-tuple-element.42.refs_0_.refs_2_, bf16[4,256,256]{2,1,0:T(8,128)(2,1)} %get-tuple-element.43.refs_1_.refs_3_, ...), custom_call_target="tpu_custom_call" | custom-call | tf_op jit(solution)/shard_map/pallas_call | solution.py:65
  52.3 5.1 %collective-permute-start.2 = (bf16[4,128,256]{2,1,0:T(8,128)(2,1)S(1)}, bf16[4,128,256]{2,1,0:T(8,128)(2,1)S(1)}, u32[]{:S(2)}, u32[]{:S(2)}) collective-permute-start(bf16[4,128,256]{2,1,0:T(8,128)(2,1)S(1)} %get-tuple-element.49), channel_id=1, source_target_pairs={{0,31},{1,0},{2,1},{3,2},{4,3},{5,4},{6,5},{7,6},{8,7},{9,8},{10,9... | collective-permute-start | bytes 786440 | tf_op jit(solution)/shard_map/ppermute | solution.py:21
  57.4 0.0 collective-permute-start.3
  57.4 0.0 copy-done
  57.4 6.9 %shard_map.79 = (f32[4,1536,256]{2,1,0:T(8,128)S(1)}, bf16[1536,256]{1,0:T(8,128)(2,1)S(1)}) custom-call(bf16[4,1792,128]{2,1,0:T(8,128)(2,1)} %get-tuple-element.30.bext_hbm, bf16[2,2,1024,256]{3,2,1,0:T(8,128)(2,1)} %get-tuple-element.40.refs_0_, bf16[2,2,1024,256]{3,2,1,0:T(8,128)(2,1)} %get-tuple-element.41.refs_1_, ...), custom_call_target="tpu_custom_call" | custom-call | tf_op jit(solution)/shard_map/pallas_call | solution.py:65
  64.3 0.0 collective-permute-done.2.above_ref
  64.3 2.4 %collective-permute-done.3.below_ref = bf16[4,128,256]{2,1,0:T(8,128)(2,1)S(1)} collective-permute-done((bf16[4,128,256]{2,1,0:T(8,128)(2,1)S(1)}, bf16[4,128,256]{2,1,0:T(8,128)(2,1)S(1)}, u32[]{:S(2)}, u32[]{:S(2)}) %collective-permute-start.3) | collective-permute-done | bytes 262176 | tf_op jit(solution)/shard_map/ppermute | solution.py:21
  66.7 2.3 %shard_map.80 = bf16[4,1536,256]{2,1,0:T(8,128)(2,1)} custom-call(f32[4,1536,256]{2,1,0:T(8,128)S(1)} %get-tuple-element.47.own_ref, bf16[1536,256]{1,0:T(8,128)(2,1)S(1)} %get-tuple-element.48.spread_ref, bf16[4,128,256]{2,1,0:T(8,128)(2,1)S(1)} %collective-permute-done.2.above_ref, bf16[4,128,256]{2,1,0:T(8,128)(2,1)S(1)} %collective-permute-done.3.below_ref), custom_call_target="tpu_custom_call" | custom-call | tf_op jit(solution)/shard_map/pallas_call | solution.py:65
Async XLA Ops:
  0.0 15.8 %copy-start.1 = (s32[4]{0:T(128)S(1)}, s32[4]{0:T(128)}, u32[]{:S(2)}) copy-start(s32[4]{0:T(128)} %block_ref.1) | copy-start | bytes 52
  3.4 12.4 %collective-permute-start = (bf16[4,128,256]{2,1,0:T(8,128)(2,1)}, bf16[4,128,256]{2,1,0:T(8,128)(2,1)S(1)}, u32[]{:S(2)}, u32[]{:S(2)}) collective-permute-start(bf16[4,128,256]{2,1,0:T(8,128)(2,1)} %get-tuple-element.35), channel_id=1, source_target_pairs={{0,1},{1,2},{2,3},{3,4},{4,5},{5,6},{6,7},{7,8},{8,9},{9,10},{10,1... | collective-permute-start | bytes 786440 | tf_op jit(solution)/shard_map/ppermute | solution.py:21
  4.0 11.8 %collective-permute-start.1 = (bf16[4,128,256]{2,1,0:T(8,128)(2,1)}, bf16[4,128,256]{2,1,0:T(8,128)(2,1)}, u32[]{:S(2)}, u32[]{:S(2)}) collective-permute-start(bf16[4,128,256]{2,1,0:T(8,128)(2,1)} %get-tuple-element.36), channel_id=1, source_target_pairs={{0,31},{1,0},{2,1},{3,2},{4,3},{5,4},{6,5},{7,6},{8,7},{9,8},{10,9... | collective-permute-start | bytes 786440 | tf_op jit(solution)/shard_map/ppermute | solution.py:21
  32.6 17.3 %all-to-all-start.1 = ((bf16[32,24,128]{2,1,0:T(8,128)(2,1)}), bf16[32,24,128]{2,1,0:T(8,128)(2,1)S(1)}, u32[]{:S(2)}, u32[]{:S(2)}) async-start(bf16[32,24,128]{2,1,0:T(8,128)(2,1)} %shard_map.77), calls=%async_computation.1 | async-start | bytes 393216 | tf_op jit(solution)/shard_map/all_to_all | solution.py:673
  42.7 14.6 %copy-start = (s32[1,2,128]{2,1,0:T(2,128)S(1)}, s32[1,2,128]{2,1,0:T(2,128)}, u32[]{:S(2)}) copy-start(s32[1,2,128]{2,1,0:T(2,128)} %param.12) | copy-start | bytes 3076
  52.3 12.0 %collective-permute-start.2 = (bf16[4,128,256]{2,1,0:T(8,128)(2,1)S(1)}, bf16[4,128,256]{2,1,0:T(8,128)(2,1)S(1)}, u32[]{:S(2)}, u32[]{:S(2)}) collective-permute-start(bf16[4,128,256]{2,1,0:T(8,128)(2,1)S(1)} %get-tuple-element.49), channel_id=1, source_target_pairs={{0,31},{1,0},{2,1},{3,2},{4,3},{5,4},{6,5},{7,6},{8,7},{9,8},{10,9... | collective-permute-start | bytes 786440 | tf_op jit(solution)/shard_map/ppermute | solution.py:21
  57.4 9.4 %collective-permute-start.3 = (bf16[4,128,256]{2,1,0:T(8,128)(2,1)S(1)}, bf16[4,128,256]{2,1,0:T(8,128)(2,1)S(1)}, u32[]{:S(2)}, u32[]{:S(2)}) collective-permute-start(bf16[4,128,256]{2,1,0:T(8,128)(2,1)S(1)} %get-tuple-element.50), channel_id=1, source_target_pairs={{0,1},{1,2},{2,3},{3,4},{4,5},{5,6},{6,7},{7,8},{8,9},{9,10},{10,1... | collective-permute-start | bytes 786440 | tf_op jit(solution)/shard_map/ppermute | solution.py:21

commit v4 on v3

--- a/solution.py
+++ b/solution.py
@@ -15,10 +15,11 @@
 BF16 = jnp.bfloat16
 
 
-def passed_along(value, axis, steps):
+def swapped(value, axis, odd_first):
     count = lax.axis_size(axis)
-    pairs = [(source, (source + steps) % count) for source in range(count)]
-    return lax.ppermute(value, axis, pairs)
+    shift = int(odd_first)
+    partner = {(i + shift) % count: ((i ^ 1) + shift) % count for i in range(count)}
+    return lax.ppermute(value, axis, sorted(partner.items()))
 
 
 def dot(a, b):
@@ -82,9 +83,14 @@
     return moved
 
 
+def partner_rows(rows_ref, odd):
+    up, down = (rows_ref[b : b + 1, :].astype(F32) for b in range(2))
+    return jnp.where(odd == 0, up, down), jnp.where(odd == 0, down, up)
+
+
 def select_kernel(
-    x_hbm, rows_hbm, slots_hbm, up_ref, down_ref, x_ref, slots_ref,
-    rows_ref, arrived,
+    odd_ref, x_hbm, rows_hbm, slots_hbm, near_ref, far_ref, slots_ref,
+    x_ref, rows_ref, arrived,
 ):
     slots = rows_ref.shape[1]
     parts, nodes, _ = x_ref.shape
@@ -95,7 +101,7 @@
         copy.start()
     small.wait()
     pick = jnp.concatenate(
-        [one_hot_rows(as_column(rows_ref[b : b + 1, :].astype(F32)), nodes) for b in range(2)], axis=0
+        [one_hot_rows(as_column(ids), nodes) for ids in partner_rows(rows_ref, odd_ref[0])], axis=0
     )
     width = x_ref.shape[2]
     for k in range(0, parts, 2):
@@ -103,35 +109,35 @@
         copies[k + 1].wait()
         got = dot(pick, beside([x_ref[k], x_ref[k + 1]])).astype(BF16)
         for j in range(2):
-            up_ref[k + j] = got[:slots, j * width : (j + 1) * width]
-            down_ref[k + j] = got[slots:, j * width : (j + 1) * width]
+            near_ref[k + j] = got[:slots, j * width : (j + 1) * width]
+            far_ref[k + j] = got[slots:, j * width : (j + 1) * width]
     later.wait()
 
 
-def select_rows(x4, rows, patch_slots):
+def select_rows(x4, rows, patch_slots, odd):
     parts, _, width = x4.shape
-    slots = rows.shape[1]
-    margin = vmem((parts, slots, width), BF16)
-    kept = [vmem(a.shape, a.dtype) for a in (x4, patch_slots)]
-    return pl.pallas_call(
+    margin = ((parts, rows.shape[1], width), BF16)
+    return call(
         select_kernel,
-        in_specs=[pl.BlockSpec(memory_space=pltpu.HBM)] * 3,
-        out_specs=[pl.BlockSpec(memory_space=pltpu.VMEM)] * 4,
-        out_shape=[margin, margin] + kept,
-        scratch_shapes=[vmem(rows.shape, rows.dtype), pltpu.SemaphoreType.DMA((parts + 2,))],
-        compiler_params=pltpu.CompilerParams(vmem_limit_bytes=6 * MIB),
-        name="select",
-    )(*[pltpu.with_memory_space_constraint(a, pltpu.HBM) for a in (x4, rows, patch_slots)])
+        10,
+        [odd],
+        [x4, rows, patch_slots],
+        [],
+        [],
+        [margin, margin, (patch_slots.shape, patch_slots.dtype)],
+        [vmem(x4.shape, BF16), vmem(rows.shape, rows.dtype), pltpu.SemaphoreType.DMA((parts + 2,))],
+    )
 
 
 def prep_kernel(
-    per_group, share, place_ref, basis_hbm, inv_hbm, slots_ref, x_ref,
+    per_group, share, place_ref, basis_hbm, inv_hbm, x_hbm, slots_ref,
     crem_hbm, y_hbm, bext_hbm, pos_ref, rest_ref, r_ref, btrem_ref, lines_ref,
-    ccat, bt, basis_ref, y_ref, bext_ref, order_ref, inv_ref, square, sems,
+    ccat, bt, basis_ref, y_ref, bext_ref, order_ref, inv_ref, square, x_ref, sems,
 ):
     basis_in = copy(basis_hbm, basis_ref, sems.at[0])
     held = jnp.minimum(place_ref[0] * share, inv_hbm.shape[0] - share)
     inv_in = copy(inv_hbm.at[pl.ds(held, share)], inv_ref, sems.at[4])
+    x_in = copy(x_hbm, x_ref, sems.at[5], 1)
     patches, patch_nodes = slots_ref.shape
     waves, width = basis_ref.shape[1], basis_ref.shape[2]
     parts, nodes, _ = x_ref.shape
@@ -177,6 +183,7 @@
             bt[k, here, p * core : (p + 1) * core] = (
                 spread[rows, p * core : (p + 1) * core] + moved[rows, :core]
             )
+    x_in.wait()
     for k in range(0, parts, 2):
         both = dot(ccat[:, :nodes], beside([x_ref[k], x_ref[k + 1]])).astype(BF16)
         for j in range(2):
@@ -215,10 +222,10 @@
     assert coarse_inv.shape[0] % share == 0
     return call(
         functools.partial(prep_kernel, per_group, share),
-        16,
+        20,
         [lax.axis_index("patch").astype(jnp.int32).reshape(1)],
-        [basis_t, coarse_inv],
-        [slots, x4],
+        [basis_t, coarse_inv, x4],
+        [slots],
         [((patches * rest, ext - nodes), BF16), y, b_ext],
         [
             ((patches, patch_nodes), F32),
@@ -236,7 +243,8 @@
             vmem((patches, patch_nodes, patch_nodes), BF16),
             vmem((share,) + coarse_inv.shape[1:], BF16),
             vmem((size, size), F32),
-            pltpu.SemaphoreType.DMA((5,)),
+            vmem(x4.shape, BF16),
+            pltpu.SemaphoreType.DMA((6,)),
         ],
     )
 
@@ -250,18 +258,19 @@
 
 
 def restrict_kernel(
-    per_group, block_ref, r_ref, btrem_ref, below_ref, above_ref, lines_ref,
+    per_group, block_ref, odd_ref, r_ref, btrem_ref, near_ref, other_ref, lines_ref,
     far_hbm, out_hbm, out_ref, sems,
 ):
     waves, columns, width = r_ref.shape
     patches = block_ref.shape[0]
-    slots = below_ref.shape[1]
+    slots = near_ref.shape[1]
     rows = patches * per_group
     groups = columns // rows
     halves = width // LANES
+    odd = odd_ref[0]
     sent = [
-        copy(below_ref, far_hbm.at[:, pl.ds(0, slots)], sems.at[0]),
-        copy(above_ref, far_hbm.at[:, pl.ds(slots, slots)], sems.at[1]),
+        copy(near_ref, far_hbm.at[:, pl.ds(pl.multiple_of((1 - odd) * slots, slots), slots)], sems.at[0]),
+        copy(other_ref, far_hbm.at[:, pl.ds(pl.multiple_of(odd * slots, slots), slots)], sems.at[1]),
     ]
     order = owner_order(columns, patches, columns // patches, per_group)
     tail = out_ref.shape[1] - rows
@@ -273,8 +282,9 @@
         total = r_ref[w]
         for q in range(2):
             k = 2 * w + q
-            total = total + dot(btrem_ref[k, :, :slots], below_ref[k])
-            total = total + dot(btrem_ref[k, :, slots:], above_ref[k])
+            near, other = near_ref[k], other_ref[k]
+            total = total + dot(btrem_ref[k, :, :slots], jnp.where(odd == 0, other, near))
+            total = total + dot(btrem_ref[k, :, slots:], jnp.where(odd == 0, near, other))
         moved = dot(order, total.astype(BF16)).astype(BF16)
         for g in range(groups):
             last = keys
@@ -292,15 +302,15 @@
         copied.wait()
 
 
-def restrict(block, r_own, bt_rem, below, above, lines, owners, per_group, padded):
-    parts, slots, width = below.shape
+def restrict(block, odd, r_own, bt_rem, near, other, lines, owners, per_group, padded):
+    parts, slots, width = near.shape
     out = ((owners, padded, LANES), BF16)
     return call(
         functools.partial(restrict_kernel, per_group),
         3,
-        [block],
-        [],
-        [r_own, bt_rem, below, above, lines],
+        [block, odd],
+        [],
+        [r_own, bt_rem, near, other, lines],
         [((parts, 2 * slots, width), BF16), out],
         [],
         [vmem(*out), pltpu.SemaphoreType.DMA((2 + r_own.shape[0],))],
@@ -463,17 +473,26 @@
 
 
 def coef_kernel(
-    per_group, patches, bext_hbm, *refs
+    per_group, patches, odd_ref, bext_hbm, *refs
 ):
-    *other_hbm, sums_ref, rest_ref, coef_ref, low_ref, high_ref = refs[:-5]
+    *other_hbm, sums_ref, rest_ref, coef_ref, near_ref, far_ref = refs[:-5]
     gathered, inverses, brem_ref, other_ref, sems = refs[-5:]
-    slots = low_ref.shape[1]
+    slots = near_ref.shape[1]
     nodes = bext_hbm.shape[1] - 2 * slots
-    arriving = [copy(bext_hbm.at[:, pl.ds(nodes, 2 * slots)], brem_ref, sems.at[0])]
+    odd = odd_ref[0]
+    starts = [pl.multiple_of(nodes + h * slots, slots) for h in (1 - odd, odd)]
+    arriving = [
+        copy(
+            bext_hbm.at[:, pl.ds(start, slots)],
+            brem_ref.at[:, pl.ds(h * slots, slots)],
+            sems.at[h],
+        )
+        for h, start in enumerate(starts)
+    ]
     start = 0
     for i, other in enumerate(other_hbm):
         place = pl.ds(start, other.shape[1])
-        arriving.append(copy(other, other_ref.at[:, place], sems.at[1 + i]))
+        arriving.append(copy(other, other_ref.at[:, place], sems.at[2 + i]))
         start += other.shape[1]
     waves, columns, width = coef_ref.shape
     size = columns // patches
@@ -493,7 +512,10 @@
     in_patch = (j % rows) // per_group == i // size
     ids = rest_ref[0:1, :]
     reach = (2 * slots, ids.shape[1])
-    spread = (ids == (iota(reach, 0) + nodes).astype(F32)).astype(F32).astype(BF16)
+    row = iota(reach, 0)
+    swap = jnp.where(odd == 0, slots, 0)
+    place = jnp.where(row < slots, row + swap, row - swap) + nodes
+    spread = (ids == place.astype(F32)).astype(F32).astype(BF16)
     for w in range(waves):
         for g in range(groups):
             for h in range(halves):
@@ -515,11 +537,11 @@
         for q in range(2):
             k = 2 * w + q
             margin = (dot(spread, other_ref[k]) + dot(brem_ref[k], coef)).astype(BF16)
-            low_ref[k] = margin[:slots]
-            high_ref[k] = margin[slots:]
-
-
-def coefficients(sums, b_ext, rest_ids, others, patches, slots, per_group):
+            near_ref[k] = margin[:slots]
+            far_ref[k] = margin[slots:]
+
+
+def coefficients(odd, sums, b_ext, rest_ids, others, patches, slots, per_group):
     parts, _, columns = b_ext.shape
     width = others[0].shape[2]
     groups = columns // (patches * per_group)
@@ -527,7 +549,7 @@
     return call(
         functools.partial(coef_kernel, per_group, patches),
         6,
-        [],
+        [odd],
         [b_ext] + others,
         [sums, rest_ids],
         [],
@@ -537,12 +559,12 @@
             vmem((groups * patches, LANES), F32),
             vmem((parts, 2 * slots, columns), BF16),
             vmem((parts, rest_ids.shape[1], width), BF16),
-            pltpu.SemaphoreType.DMA((1 + len(others),)),
+            pltpu.SemaphoreType.DMA((2 + len(others),)),
         ],
     )
 
 
-def own_kernel(bext_hbm, *refs):
+def own_kernel(odd_ref, bext_hbm, *refs):
     *pairs, rows_ref, rest_ref, pos_ref, coef_ref, out_ref, back_ref, bown_ref, local_ref, other_ref, sems = refs
     half = len(pairs) // 2
     parts, nodes, _ = out_ref.shape
@@ -559,12 +581,11 @@
         terms = pl.ds((k % 2) * patch_nodes, patch_nodes)
         for a in pairs[:half]:
             here = pl.ds(start, a.shape[0])
-            moves.append((a.at[:, k // 2, terms], local_ref.at[k, here], 1))
+            moves.append((a.at[:, k // 2, terms], local_ref.at[k, here]))
             start += a.shape[0]
-        arriving.append([copy(m[0], m[1], sems.at[k, i], *m[2:]) for i, m in enumerate(moves)])
+        arriving.append([copy(m[0], m[1], sems.at[k, i], int(k > 1)) for i, m in enumerate(moves)])
     slots = rows_ref.shape[1]
-    for b in range(2):
-        ids = rows_ref[b : b + 1, :].astype(F32)
+    for b, ids in enumerate(partner_rows(rows_ref, odd_ref[0])):
         back_ref[:, b * slots : (b + 1) * slots] = (
             (ids == iota((nodes, slots), 0).astype(F32)).astype(F32).astype(BF16)
         )
@@ -589,13 +610,13 @@
             out_ref[k + j] = total[:, j * width : (j + 1) * width] + coarse
 
 
-def own_rows(b_ext, coef, rows, rest_ids, pos, locals_, others, nodes):
+def own_rows(odd, b_ext, coef, rows, rest_ids, pos, locals_, others, nodes):
     parts, _, columns = b_ext.shape
     width = coef.shape[2]
     return call(
         own_kernel,
         20,
-        [],
+        [odd],
         [b_ext] + locals_ + others,
         [rows, rest_ids, pos, coef],
         [],
@@ -609,12 +630,12 @@
     )
 
 
-def final_kernel(own_ref, spread_ref, above_ref, below_ref, out_hbm, out_ref, sems):
+def final_kernel(own_ref, spread_ref, near_ref, other_ref, out_hbm, out_ref, sems):
     parts, _, width = own_ref.shape
     sent = []
     for k in range(0, parts, 2):
         back = jnp.concatenate(
-            [beside([a[k], a[k + 1]]) for a in (above_ref, below_ref)], axis=0
+            [beside([a[k], a[k + 1]]) for a in (near_ref, other_ref)], axis=0
         )
         total = dot(spread_ref[...], back)
         for j in range(2):
@@ -625,13 +646,13 @@
         moved.wait()
 
 
-def finish(own, spread, above, below):
+def finish(own, spread, near, other):
     return call(
         final_kernel,
         12,
         [],
         [],
-        [own, spread, above, below],
+        [own, spread, near, other],
         [(own.shape, BF16)],
         [],
         [vmem(own.shape, BF16), pltpu.SemaphoreType.DMA((own.shape[0],))],
@@ -648,37 +669,39 @@
     halves = width // LANES
     groups = owners // (waves * halves)
     per_group = size // groups
-    assert groups * waves * halves == owners and per_group * groups == size
+    assert owners % 2 == 0 and groups * waves * halves == owners and per_group * groups == size
     blocks = coarse_inv.shape[0]
     share = -(-blocks // lax.axis_size("patch"))
     rows = patches * per_group
     padded = -(-(rows + patches + share) // 8) * 8
     half = patches // 2
     send = send_rows[0]
+    odd = (lax.axis_index(AXES) % 2).astype(jnp.int32).reshape(1)
     basis_t = jnp.swapaxes(coarse_basis, 2, 3)
 
     x_all = residual.reshape(2 * waves, nodes, width)
-    up, down, x4, slots_v = select_rows(x_all, send, patch_slots)
-    below = passed_along(up, AXES, 1)
-    above = passed_along(down, AXES, -1)
+    to_first, to_second, slots_v = select_rows(x_all, send, patch_slots, odd)
+    first_rows = swapped(to_first, AXES, False)
+    second_rows = swapped(to_second, AXES, True)
     crem, y, b_ext, pos, rest_ids, r_own, bt_rem, lines = prepare(
-        slots_v, basis_t, coarse_inv, x4, ext, per_group, share
+        slots_v, basis_t, coarse_inv, x_all, ext, per_group, share
     )
     far, sent = restrict(
-        coarse_block, r_own, bt_rem, below, above, lines, owners, per_group, padded
+        coarse_block, odd, r_own, bt_rem, first_rows, second_rows, lines,
+        owners, per_group, padded,
     )
     got = lax.all_to_all(sent, AXES, 0, 0, tiled=True)
     local_a, rest_a = local_products(pos, x_all, y, crem, far, patch_inv, 0, half)
     sums = owner_sums(got, patches, per_group, blocks, share)
     mine = lax.all_to_all(sums, AXES, 0, 0, tiled=True)
     local_b, rest_b = local_products(pos, x_all, y, crem, far, patch_inv, half, patches - half)
-    coef, low, high = coefficients(
-        mine, b_ext, rest_ids, [rest_a, rest_b], patches, slots, per_group
-    )
-    back_above = passed_along(low, AXES, -1)
-    back_below = passed_along(high, AXES, 1)
-    own, spread = own_rows(b_ext, coef, send, rest_ids, pos, [local_a, local_b], [rest_a, rest_b], nodes)
-    out = finish(own, spread, back_above, back_below)
+    coef, to_first, to_second = coefficients(
+        odd, mine, b_ext, rest_ids, [rest_a, rest_b], patches, slots, per_group
+    )
+    first_back = swapped(to_first, AXES, False)
+    second_back = swapped(to_second, AXES, True)
+    own, spread = own_rows(odd, b_ext, coef, send, rest_ids, pos, [local_a, local_b], [rest_a, rest_b], nodes)
+    out = finish(own, spread, first_back, second_back)
     return out.reshape(residual.shape)
 
 

time: 69.5 us -> 66.4 us (0.955)
  waiting for transfers between devices: 2.45 us -> 0.01 us
  Pallas kernels: 38.9 us -> 37.6 us
  starting transfers between devices: 14.4 us -> 15.6 us
    pallas_call x1 -> x0, Pallas kernels: 3.4 us -> none  [select_rows(): pl.pallas_call(select_kernel, in_specs=[pl.BlockSpec(memory_space=pltpu.H...]
    ppermute x4, waiting for transfers between devices: 2.45 us -> 0.01 us  [swapped(): return lax.ppermute(value, axis, sorted(partner.items()))]
    pallas_call x8 -> x9, Pallas kernels: 35.5 us -> 37.6 us  [call(): pl.pallas_call(kernel, in_specs=[pl.BlockSpec(memory_space=m) for m in sp...]
    ppermute x4, starting transfers between devices: 11.6 us -> 12.8 us  [swapped(): return lax.ppermute(value, axis, sorted(partner.items()))]
  transfers between devices with their start and end apart: 5 -> 5, of which waited for: 1 -> 0; matrix products, arithmetic and copies ran while one was open for 0% -> 0% of each run, Pallas kernels for 39% -> 41%
where the time goes in v4:
time: 66.4 us; the launch traced here: 66.1 us
  Pallas kernels  37.6 us (57%)
  starting transfers between devices  15.6 us (23%)
  blocking collectives  12.6 us (19%)
    pallas_call x9, Pallas kernels, call(): pl.pallas_call(kernel, in_specs=[pl.BlockSpec(memory_space=m) for m in sp...  37.6 us
    ppermute x4, starting transfers between devices, swapped(): return lax.ppermute(value, axis, sorted(partner.items()))  12.8 us
    all_to_all x1, blocking collectives, per_device(): got = lax.all_to_all(sent, AXES, 0, 0, tiled=True)  12.6 us
    all_to_all x1, starting transfers between devices, per_device(): mine = lax.all_to_all(sums, AXES, 0, 0, tiled=True)  2.8 us
  transfers between devices with their start and end apart: 5, of which 0 were waited for; matrix products, arithmetic and copies ran while one was open for 0% of the time, Pallas kernels for 41%

profile of v4, /device:TPU:0, one launch (start us, length us, event | category | flops | bytes accessed | tf_op | source)
XLA Modules:
  0.0 66.1 jit_solution(12774183786266128643)
XLA Ops:
  0.0 0.0 copy-start.1
  0.0 2.6 %shard_map.73 = (bf16[4,128,256]{2,1,0:T(8,128)(2,1)S(1)}, bf16[4,128,256]{2,1,0:T(8,128)(2,1)S(1)}, s32[4,512]{1,0:T(4,128)S(1)}) custom-call(s32[1]{0:T(128)} %bitcast.odd_ref, bf16[4,1536,256]{2,1,0:T(8,128)(2,1)} %bitcast.8, s32[2,128]{1,0:T(2,128)} %bitcast.6, s32[4,512]{1,0:T(4,128)} %slots_hbm.1), custom_call_target="tpu_custom_call" | custom-call | tf_op jit(solution)/shard_map/pallas_call | solution.py:66
  2.6 0.6 collective-permute-start
  3.2 6.6 %collective-permute-start.1 = (bf16[4,128,256]{2,1,0:T(8,128)(2,1)S(1)}, bf16[4,128,256]{2,1,0:T(8,128)(2,1)S(1)}, u32[]{:S(2)}, u32[]{:S(2)}) collective-permute-start(bf16[4,128,256]{2,1,0:T(8,128)(2,1)S(1)} %get-tuple-element.34), channel_id=1, source_target_pairs={{0,31},{1,2},{2,1},{3,4},{4,3},{5,6},{6,5},{7,8},{8,7},{9,10},{10,... | collective-permute-start | bytes 786440 | tf_op jit(solution)/shard_map/ppermute | solution.py:22
  9.8 6.0 %shard_map.74 = (bf16[512,256]{1,0:T(8,128)(2,1)}, bf16[4,512,256]{2,1,0:T(8,128)(2,1)}, bf16[4,1792,128]{2,1,0:T(8,128)(2,1)}, f32[4,512]{1,0:T(4,128)S(1)}, f3...) custom-call(s32[1]{0:T(128)} %bitcast.1.place_ref, ...), custom_call_target="tpu_custom_call" | custom-call | tf_op jit(solution)/shard_map/pallas_call | solution.py:66
  15.8 0.0 collective-permute-done.near_ref
  15.8 0.0 collective-permute-done.1.other_ref
  15.8 0.0 copy-done.1
  15.8 1.9 %shard_map.75 = (bf16[4,256,256]{2,1,0:T(8,128)(2,1)}, bf16[32,24,128]{2,1,0:T(8,128)(2,1)}) custom-call(s32[4]{0:T(128)S(1)} %copy-done.1, s32[1]{0:T(128)} %bitcast.odd_ref, f32[2,128,256]{2,1,0:T(8,128)S(1)} %get-tuple-element.31.r_ref, bf16[4,128,256]{2,1,0:T(8,128)(2,1)S(1)} %get-tuple-element.32.btrem_ref, ...), custom_call_target="tpu_custom_call" | custom-call | tf_op jit(solution)/shard_map/pallas_call | solution.py:66
  17.8 12.6 %all_to_all.10.got_ref = bf16[32,24,128]{2,1,0:T(8,128)(2,1)S(1)} all-to-all(bf16[32,24,128]{2,1,0:T(8,128)(2,1)} %get-tuple-element.43), channel_id=1, replica_groups=mesh['patch'=8,'coarse'=4] {'patch','coarse'}, dimensions={0} | all-to-all | bytes 393216 | tf_op jit(solution)/shard_map/all_to_all | solution.py:693
  30.4 1.3 %shard_map.78 = bf16[32,24,128]{2,1,0:T(8,128)(2,1)} custom-call(bf16[32,24,128]{2,1,0:T(8,128)(2,1)S(1)} %all_to_all.10.got_ref), custom_call_target="tpu_custom_call" | custom-call | tf_op jit(solution)/shard_map/pallas_call | solution.py:66
  31.7 2.8 %all-to-all-start.1 = ((bf16[32,24,128]{2,1,0:T(8,128)(2,1)}), bf16[32,24,128]{2,1,0:T(8,128)(2,1)S(1)}, u32[]{:S(2)}, u32[]{:S(2)}) async-start(bf16[32,24,128]{2,1,0:T(8,128)(2,1)} %shard_map.78), calls=%async_computation.1 | async-start | bytes 393216 | tf_op jit(solution)/shard_map/all_to_all | solution.py:696
  34.5 7.2 %shard_map.77 = (bf16[2,2,1024,256]{3,2,1,0:T(8,128)(2,1)}, bf16[4,256,256]{2,1,0:T(8,128)(2,1)}) custom-call(bf16[4,2,1024,1024]{3,2,1,0:T(8,128)(2,1)} %inv_hbm.5, bf16[4,1536,256]{2,1,0:T(8,128)(2,1)} %bitcast.10, bf16[4,512,256]{2,1,0:T(8,128)(2,1)} %get-tuple-element.29.y_hbm, bf16[512,256]{1,0:T(8,128)(2,1)} %get-tuple-element.30.crem_hbm, ...), custom_call_target="tpu_custom_call" | custom-call | tf_op jit(solution)/shard_map/pallas_call | solution.py:66
  41.8 0.0 copy-start
  41.8 7.3 %shard_map.76 = (bf16[2,2,1024,256]{3,2,1,0:T(8,128)(2,1)}, bf16[4,256,256]{2,1,0:T(8,128)(2,1)}) custom-call(bf16[4,2,1024,1024]{3,2,1,0:T(8,128)(2,1)} %inv_hbm.5, bf16[4,1536,256]{2,1,0:T(8,128)(2,1)} %bitcast.11, bf16[4,512,256]{2,1,0:T(8,128)(2,1)} %get-tuple-element.29.y_hbm, bf16[512,256]{1,0:T(8,128)(2,1)} %get-tuple-element.30.crem_hbm, ...), custom_call_target="tpu_custom_call" | custom-call | tf_op jit(solution)/shard_map/pallas_call | solution.py:66
  49.1 0.0 all-to-all-done.1.refs_2_
  49.1 2.4 %shard_map.79 = (bf16[2,128,256]{2,1,0:T(8,128)(2,1)S(1)}, bf16[4,128,256]{2,1,0:T(8,128)(2,1)S(1)}, bf16[4,128,256]{2,1,0:T(8,128)(2,1)S(1)}) custom-call(s32[1]{0:T(128)} %bitcast.odd_ref, bf16[4,1792,128]{2,1,0:T(8,128)(2,1)} %get-tuple-element.28.bext_hbm, bf16[4,256,256]{2,1,0:T(8,128)(2,1)} %get-tuple-element.40.refs_0_.refs_2_, ...), custom_call_target="tpu_custom_call" | custom-call | tf_op jit(solution)/shard_map/pallas_call | solution.py:66
  51.4 0.3 collective-permute-start.2
  51.8 5.3 %collective-permute-start.3 = (bf16[4,128,256]{2,1,0:T(8,128)(2,1)S(1)}, bf16[4,128,256]{2,1,0:T(8,128)(2,1)S(1)}, u32[]{:S(2)}, u32[]{:S(2)}) collective-permute-start(bf16[4,128,256]{2,1,0:T(8,128)(2,1)S(1)} %get-tuple-element.48), channel_id=1, source_target_pairs={{0,31},{1,2},{2,1},{3,4},{4,3},{5,6},{6,5},{7,8},{8,7},{9,10},{10,... | collective-permute-start | bytes 786440 | tf_op jit(solution)/shard_map/ppermute | solution.py:22
  57.1 0.0 copy-done
  57.1 6.5 %shard_map.80 = (f32[4,1536,256]{2,1,0:T(8,128)S(1)}, bf16[1536,256]{1,0:T(8,128)(2,1)S(1)}) custom-call(s32[1]{0:T(128)} %bitcast.odd_ref, bf16[4,1792,128]{2,1,0:T(8,128)(2,1)} %get-tuple-element.28.bext_hbm, bf16[2,2,1024,256]{3,2,1,0:T(8,128)(2,1)} %get-tuple-element.38.refs_0_, bf16[2,2,1024,256]{3,2,1,0:T(8,128)(2,1)} %get-tuple-element.39.refs_1_, ...), custom_call_target="tpu_custom_call" | custom-call | tf_op jit(solution)/shard_map/pallas_call | solution.py:66
  63.6 0.0 collective-permute-done.2.near_ref
  63.7 0.0 collective-permute-done.3.other_ref
  63.7 2.3 %shard_map.81 = bf16[4,1536,256]{2,1,0:T(8,128)(2,1)} custom-call(f32[4,1536,256]{2,1,0:T(8,128)S(1)} %get-tuple-element.45.own_ref, bf16[1536,256]{1,0:T(8,128)(2,1)S(1)} %get-tuple-element.46.spread_ref, bf16[4,128,256]{2,1,0:T(8,128)(2,1)S(1)} %collective-permute-done.2.near_ref, bf16[4,128,256]{2,1,0:T(8,128)(2,1)S(1)} %collective-permute-done.3.other_ref), custom_call_target="tpu_custom_call" | custom-call | tf_op jit(solution)/shard_map/pallas_call | solution.py:66
Async XLA Ops:
  0.0 15.8 %copy-start.1 = (s32[4]{0:T(128)S(1)}, s32[4]{0:T(128)}, u32[]{:S(2)}) copy-start(s32[4]{0:T(128)} %block_ref.1) | copy-start | bytes 52
  2.6 13.2 %collective-permute-start = (bf16[4,128,256]{2,1,0:T(8,128)(2,1)S(1)}, bf16[4,128,256]{2,1,0:T(8,128)(2,1)S(1)}, u32[]{:S(2)}, u32[]{:S(2)}) collective-permute-start(bf16[4,128,256]{2,1,0:T(8,128)(2,1)S(1)} %get-tuple-element.33), channel_id=1, source_target_pairs={{0,1},{1,0},{2,3},{3,2},{4,5},{5,4},{6,7},{7,6},{8,9},{9,8},{10,11... | collective-permute-start | bytes 786440 | tf_op jit(solution)/shard_map/ppermute | solution.py:22
  3.2 12.6 %collective-permute-start.1 = (bf16[4,128,256]{2,1,0:T(8,128)(2,1)S(1)}, bf16[4,128,256]{2,1,0:T(8,128)(2,1)S(1)}, u32[]{:S(2)}, u32[]{:S(2)}) collective-permute-start(bf16[4,128,256]{2,1,0:T(8,128)(2,1)S(1)} %get-tuple-element.34), channel_id=1, source_target_pairs={{0,31},{1,2},{2,1},{3,4},{4,3},{5,6},{6,5},{7,8},{8,7},{9,10},{10,... | collective-permute-start | bytes 786440 | tf_op jit(solution)/shard_map/ppermute | solution.py:22
  31.7 17.3 %all-to-all-start.1 = ((bf16[32,24,128]{2,1,0:T(8,128)(2,1)}), bf16[32,24,128]{2,1,0:T(8,128)(2,1)S(1)}, u32[]{:S(2)}, u32[]{:S(2)}) async-start(bf16[32,24,128]{2,1,0:T(8,128)(2,1)} %shard_map.78), calls=%async_computation.1 | async-start | bytes 393216 | tf_op jit(solution)/shard_map/all_to_all | solution.py:696
  41.8 15.3 %copy-start = (s32[1,2,128]{2,1,0:T(2,128)S(1)}, s32[1,2,128]{2,1,0:T(2,128)}, u32[]{:S(2)}) copy-start(s32[1,2,128]{2,1,0:T(2,128)} %param.12) | copy-start | bytes 3076
  51.4 12.2 %collective-permute-start.2 = (bf16[4,128,256]{2,1,0:T(8,128)(2,1)S(1)}, bf16[4,128,256]{2,1,0:T(8,128)(2,1)S(1)}, u32[]{:S(2)}, u32[]{:S(2)}) collective-permute-start(bf16[4,128,256]{2,1,0:T(8,128)(2,1)S(1)} %get-tuple-element.47), channel_id=1, source_target_pairs={{0,1},{1,0},{2,3},{3,2},{4,5},{5,4},{6,7},{7,6},{8,9},{9,8},{10,11... | collective-permute-start | bytes 786440 | tf_op jit(solution)/shard_map/ppermute | solution.py:22
  51.8 11.9 %collective-permute-start.3 = (bf16[4,128,256]{2,1,0:T(8,128)(2,1)S(1)}, bf16[4,128,256]{2,1,0:T(8,128)(2,1)S(1)}, u32[]{:S(2)}, u32[]{:S(2)}) collective-permute-start(bf16[4,128,256]{2,1,0:T(8,128)(2,1)S(1)} %get-tuple-element.48), channel_id=1, source_target_pairs={{0,31},{1,2},{2,1},{3,4},{4,3},{5,6},{6,5},{7,8},{8,7},{9,10},{10,... | collective-permute-start | bytes 786440 | tf_op jit(solution)/shard_map/ppermute | solution.py:22

commit v5 on v4

--- a/solution.py
+++ b/solution.py
@@ -183,13 +183,18 @@
             bt[k, here, p * core : (p + 1) * core] = (
                 spread[rows, p * core : (p + 1) * core] + moved[rows, :core]
             )
+    for k in range(parts):
+        btrem_ref[k] = bt[k, :, nodes:]
+        bext_ref[k] = jnp.transpose(bt[k])
+    sent = [
+        copy(ccat.at[:, pl.ds(nodes, ext - nodes)], crem_hbm, sems.at[1]),
+        copy(bext_ref, bext_hbm, sems.at[3], 1),
+    ]
     x_in.wait()
     for k in range(0, parts, 2):
         both = dot(ccat[:, :nodes], beside([x_ref[k], x_ref[k + 1]])).astype(BF16)
         for j in range(2):
             y_ref[k + j] = both[:, j * x_ref.shape[2] : (j + 1) * x_ref.shape[2]]
-            btrem_ref[k + j] = bt[k + j, :, nodes:]
-            bext_ref[k + j] = jnp.transpose(bt[k + j])
     inv_in.wait()
     lines_ref[...] = jnp.zeros(lines_ref.shape, F32)
     for w in range(waves):
@@ -199,11 +204,7 @@
                 lines_ref[w * share + t, :, c * width : (c + 1) * width] = square[
                     pl.ds(c, width // per_group, stride=per_group), :
                 ]
-    sent = [
-        copy(ccat.at[:, pl.ds(nodes, ext - nodes)], crem_hbm, sems.at[1]),
-        copy(y_ref, y_hbm, sems.at[2]),
-        copy(bext_ref, bext_hbm, sems.at[3]),
-    ]
+    sent.append(copy(y_ref, y_hbm, sems.at[2]))
     for w in range(waves):
         r_ref[w] = sum(dot(bt[k, :, :nodes], x_ref[k]) for k in (2 * w, 2 * w + 1))
     for moved in sent:
@@ -492,7 +493,7 @@
     start = 0
     for i, other in enumerate(other_hbm):
         place = pl.ds(start, other.shape[1])
-        arriving.append(copy(other, other_ref.at[:, place], sems.at[2 + i]))
+        arriving.append(copy(other, other_ref.at[:, place], sems.at[2 + i], 1))
         start += other.shape[1]
     waves, columns, width = coef_ref.shape
     size = columns // patches
@@ -570,8 +571,7 @@
     parts, nodes, _ = out_ref.shape
     patches, patch_nodes = pos_ref.shape
     core = nodes // patches
-    arriving = []
-    for k in range(parts):
+    def load(k):
         moves = [(bext_hbm.at[k, pl.ds(0, nodes)], bown_ref.at[k])]
         start = 0
         for a in pairs[half:]:
@@ -583,7 +583,9 @@
             here = pl.ds(start, a.shape[0])
             moves.append((a.at[:, k // 2, terms], local_ref.at[k, here]))
             start += a.shape[0]
-        arriving.append([copy(m[0], m[1], sems.at[k, i], int(k > 1)) for i, m in enumerate(moves)])
+        return [copy(m[0], m[1], sems.at[k, i], i % 2) for i, m in enumerate(moves)]
+
+    arriving = {k: load(k) for k in range(2)}
     slots = rows_ref.shape[1]
     for b, ids in enumerate(partner_rows(rows_ref, odd_ref[0])):
         back_ref[:, b * slots : (b + 1) * slots] = (
@@ -600,6 +602,8 @@
     for k in range(0, parts, 2):
         for moved in arriving[k] + arriving[k + 1]:
             moved.wait()
+        for later in range(k + 2, min(k + 4, parts)):
+            arriving[later] = load(later)
         total = dot(spread, beside([other_ref[k], other_ref[k + 1]]))
         cores = [
             dot(backs[p], beside([local_ref[k, p], local_ref[k + 1, p]])) for p in range(patches)
@@ -641,7 +645,7 @@
         for j in range(2):
             mine = total[:, j * width : (j + 1) * width]
             out_ref[k + j] = (own_ref[k + j] + mine).astype(BF16)
-            sent.append(copy(out_ref.at[k + j], out_hbm.at[k + j], sems.at[k + j]))
+            sent.append(copy(out_ref.at[k + j], out_hbm.at[k + j], sems.at[k + j], j))
     for moved in sent:
         moved.wait()
 

time: 66.4 us -> 66.4 us (level)
  no operation moved by 1% of the time
where the time goes in v5:
time: 66.4 us; the launch traced here: 66.1 us
  Pallas kernels  37.2 us (56%)
  starting transfers between devices  15.6 us (23%)
  blocking collectives  13 us (20%)
    pallas_call x9, Pallas kernels, call(): pl.pallas_call(kernel, in_specs=[pl.BlockSpec(memory_space=m) for m in sp...  37.2 us
    all_to_all x1, blocking collectives, per_device(): got = lax.all_to_all(sent, AXES, 0, 0, tiled=True)  13 us
    ppermute x4, starting transfers between devices, swapped(): return lax.ppermute(value, axis, sorted(partner.items()))  12.8 us
    all_to_all x1, starting transfers between devices, per_device(): mine = lax.all_to_all(sums, AXES, 0, 0, tiled=True)  2.8 us
  transfers between devices with their start and end apart: 5, of which 0 were waited for; matrix products, arithmetic and copies ran while one was open for 0% of the time, Pallas kernels for 41%

profile of v5, /device:TPU:0, one launch (start us, length us, event | category | flops | bytes accessed | tf_op | source)
XLA Modules:
  0.0 66.1 jit_solution(4239527097117144830)
XLA Ops:
  0.0 0.0 copy-start.1
  0.0 2.6 %shard_map.73 = (bf16[4,128,256]{2,1,0:T(8,128)(2,1)S(1)}, bf16[4,128,256]{2,1,0:T(8,128)(2,1)S(1)}, s32[4,512]{1,0:T(4,128)S(1)}) custom-call(s32[1]{0:T(128)} %bitcast.odd_ref, bf16[4,1536,256]{2,1,0:T(8,128)(2,1)} %bitcast.8, s32[2,128]{1,0:T(2,128)} %bitcast.6, s32[4,512]{1,0:T(4,128)} %slots_hbm.1), custom_call_target="tpu_custom_call" | custom-call | tf_op jit(solution)/shard_map/pallas_call | solution.py:66
  2.6 0.6 collective-permute-start
  3.2 6.6 %collective-permute-start.1 = (bf16[4,128,256]{2,1,0:T(8,128)(2,1)S(1)}, bf16[4,128,256]{2,1,0:T(8,128)(2,1)S(1)}, u32[]{:S(2)}, u32[]{:S(2)}) collective-permute-start(bf16[4,128,256]{2,1,0:T(8,128)(2,1)S(1)} %get-tuple-element.34), channel_id=1, source_target_pairs={{0,31},{1,2},{2,1},{3,4},{4,3},{5,6},{6,5},{7,8},{8,7},{9,10},{10,... | collective-permute-start | bytes 786440 | tf_op jit(solution)/shard_map/ppermute | solution.py:22
  9.8 5.7 %shard_map.74 = (bf16[512,256]{1,0:T(8,128)(2,1)}, bf16[4,512,256]{2,1,0:T(8,128)(2,1)}, bf16[4,1792,128]{2,1,0:T(8,128)(2,1)}, f32[4,512]{1,0:T(4,128)S(1)}, f3...) custom-call(s32[1]{0:T(128)} %bitcast.1.place_ref, ...), custom_call_target="tpu_custom_call" | custom-call | tf_op jit(solution)/shard_map/pallas_call | solution.py:66
  15.5 0.0 collective-permute-done.near_ref
  15.5 0.0 collective-permute-done.1.other_ref
  15.5 0.0 copy-done.1
  15.5 1.9 %shard_map.75 = (bf16[4,256,256]{2,1,0:T(8,128)(2,1)}, bf16[32,24,128]{2,1,0:T(8,128)(2,1)}) custom-call(s32[4]{0:T(128)S(1)} %copy-done.1, s32[1]{0:T(128)} %bitcast.odd_ref, f32[2,128,256]{2,1,0:T(8,128)S(1)} %get-tuple-element.31.r_ref, bf16[4,128,256]{2,1,0:T(8,128)(2,1)S(1)} %get-tuple-element.32.btrem_ref, ...), custom_call_target="tpu_custom_call" | custom-call | tf_op jit(solution)/shard_map/pallas_call | solution.py:66
  17.4 13.0 %all_to_all.10.got_ref = bf16[32,24,128]{2,1,0:T(8,128)(2,1)S(1)} all-to-all(bf16[32,24,128]{2,1,0:T(8,128)(2,1)} %get-tuple-element.43), channel_id=1, replica_groups=mesh['patch'=8,'coarse'=4] {'patch','coarse'}, dimensions={0} | all-to-all | bytes 393216 | tf_op jit(solution)/shard_map/all_to_all | solution.py:697
  30.4 1.3 %shard_map.78 = bf16[32,24,128]{2,1,0:T(8,128)(2,1)} custom-call(bf16[32,24,128]{2,1,0:T(8,128)(2,1)S(1)} %all_to_all.10.got_ref), custom_call_target="tpu_custom_call" | custom-call | tf_op jit(solution)/shard_map/pallas_call | solution.py:66
  31.7 2.8 %all-to-all-start.1 = ((bf16[32,24,128]{2,1,0:T(8,128)(2,1)}), bf16[32,24,128]{2,1,0:T(8,128)(2,1)S(1)}, u32[]{:S(2)}, u32[]{:S(2)}) async-start(bf16[32,24,128]{2,1,0:T(8,128)(2,1)} %shard_map.78), calls=%async_computation.1 | async-start | bytes 393216 | tf_op jit(solution)/shard_map/all_to_all | solution.py:700
  34.5 7.2 %shard_map.77 = (bf16[2,2,1024,256]{3,2,1,0:T(8,128)(2,1)}, bf16[4,256,256]{2,1,0:T(8,128)(2,1)}) custom-call(bf16[4,2,1024,1024]{3,2,1,0:T(8,128)(2,1)} %inv_hbm.5, bf16[4,1536,256]{2,1,0:T(8,128)(2,1)} %bitcast.10, bf16[4,512,256]{2,1,0:T(8,128)(2,1)} %get-tuple-element.29.y_hbm, bf16[512,256]{1,0:T(8,128)(2,1)} %get-tuple-element.30.crem_hbm, ...), custom_call_target="tpu_custom_call" | custom-call | tf_op jit(solution)/shard_map/pallas_call | solution.py:66
  41.8 0.0 copy-start
  41.8 7.3 %shard_map.76 = (bf16[2,2,1024,256]{3,2,1,0:T(8,128)(2,1)}, bf16[4,256,256]{2,1,0:T(8,128)(2,1)}) custom-call(bf16[4,2,1024,1024]{3,2,1,0:T(8,128)(2,1)} %inv_hbm.5, bf16[4,1536,256]{2,1,0:T(8,128)(2,1)} %bitcast.11, bf16[4,512,256]{2,1,0:T(8,128)(2,1)} %get-tuple-element.29.y_hbm, bf16[512,256]{1,0:T(8,128)(2,1)} %get-tuple-element.30.crem_hbm, ...), custom_call_target="tpu_custom_call" | custom-call | tf_op jit(solution)/shard_map/pallas_call | solution.py:66
  49.1 0.0 all-to-all-done.1.refs_2_
  49.1 2.3 %shard_map.79 = (bf16[2,128,256]{2,1,0:T(8,128)(2,1)S(1)}, bf16[4,128,256]{2,1,0:T(8,128)(2,1)S(1)}, bf16[4,128,256]{2,1,0:T(8,128)(2,1)S(1)}) custom-call(s32[1]{0:T(128)} %bitcast.odd_ref, bf16[4,1792,128]{2,1,0:T(8,128)(2,1)} %get-tuple-element.28.bext_hbm, bf16[4,256,256]{2,1,0:T(8,128)(2,1)} %get-tuple-element.40.refs_0_.refs_2_, ...), custom_call_target="tpu_custom_call" | custom-call | tf_op jit(solution)/shard_map/pallas_call | solution.py:66
  51.4 0.3 collective-permute-start.2
  51.7 5.3 %collective-permute-start.3 = (bf16[4,128,256]{2,1,0:T(8,128)(2,1)S(1)}, bf16[4,128,256]{2,1,0:T(8,128)(2,1)S(1)}, u32[]{:S(2)}, u32[]{:S(2)}) collective-permute-start(bf16[4,128,256]{2,1,0:T(8,128)(2,1)S(1)} %get-tuple-element.48), channel_id=1, source_target_pairs={{0,31},{1,2},{2,1},{3,4},{4,3},{5,6},{6,5},{7,8},{8,7},{9,10},{10,... | collective-permute-start | bytes 786440 | tf_op jit(solution)/shard_map/ppermute | solution.py:22
  57.1 0.0 copy-done
  57.1 6.6 %shard_map.80 = (f32[4,1536,256]{2,1,0:T(8,128)S(1)}, bf16[1536,256]{1,0:T(8,128)(2,1)S(1)}) custom-call(s32[1]{0:T(128)} %bitcast.odd_ref, bf16[4,1792,128]{2,1,0:T(8,128)(2,1)} %get-tuple-element.28.bext_hbm, bf16[2,2,1024,256]{3,2,1,0:T(8,128)(2,1)} %get-tuple-element.38.refs_0_, bf16[2,2,1024,256]{3,2,1,0:T(8,128)(2,1)} %get-tuple-element.39.refs_1_, ...), custom_call_target="tpu_custom_call" | custom-call | tf_op jit(solution)/shard_map/pallas_call | solution.py:66
  63.6 0.0 collective-permute-done.2.near_ref
  63.7 0.0 collective-permute-done.3.other_ref
  63.7 2.3 %shard_map.81 = bf16[4,1536,256]{2,1,0:T(8,128)(2,1)} custom-call(f32[4,1536,256]{2,1,0:T(8,128)S(1)} %get-tuple-element.45.own_ref, bf16[1536,256]{1,0:T(8,128)(2,1)S(1)} %get-tuple-element.46.spread_ref, bf16[4,128,256]{2,1,0:T(8,128)(2,1)S(1)} %collective-permute-done.2.near_ref, bf16[4,128,256]{2,1,0:T(8,128)(2,1)S(1)} %collective-permute-done.3.other_ref), custom_call_target="tpu_custom_call" | custom-call | tf_op jit(solution)/shard_map/pallas_call | solution.py:66
Async XLA Ops:
  0.0 15.5 %copy-start.1 = (s32[4]{0:T(128)S(1)}, s32[4]{0:T(128)}, u32[]{:S(2)}) copy-start(s32[4]{0:T(128)} %block_ref.1) | copy-start | bytes 52
  2.6 12.9 %collective-permute-start = (bf16[4,128,256]{2,1,0:T(8,128)(2,1)S(1)}, bf16[4,128,256]{2,1,0:T(8,128)(2,1)S(1)}, u32[]{:S(2)}, u32[]{:S(2)}) collective-permute-start(bf16[4,128,256]{2,1,0:T(8,128)(2,1)S(1)} %get-tuple-element.33), channel_id=1, source_target_pairs={{0,1},{1,0},{2,3},{3,2},{4,5},{5,4},{6,7},{7,6},{8,9},{9,8},{10,11... | collective-permute-start | bytes 786440 | tf_op jit(solution)/shard_map/ppermute | solution.py:22
  3.2 12.3 %collective-permute-start.1 = (bf16[4,128,256]{2,1,0:T(8,128)(2,1)S(1)}, bf16[4,128,256]{2,1,0:T(8,128)(2,1)S(1)}, u32[]{:S(2)}, u32[]{:S(2)}) collective-permute-start(bf16[4,128,256]{2,1,0:T(8,128)(2,1)S(1)} %get-tuple-element.34), channel_id=1, source_target_pairs={{0,31},{1,2},{2,1},{3,4},{4,3},{5,6},{6,5},{7,8},{8,7},{9,10},{10,... | collective-permute-start | bytes 786440 | tf_op jit(solution)/shard_map/ppermute | solution.py:22
  31.7 17.3 %all-to-all-start.1 = ((bf16[32,24,128]{2,1,0:T(8,128)(2,1)}), bf16[32,24,128]{2,1,0:T(8,128)(2,1)S(1)}, u32[]{:S(2)}, u32[]{:S(2)}) async-start(bf16[32,24,128]{2,1,0:T(8,128)(2,1)} %shard_map.78), calls=%async_computation.1 | async-start | bytes 393216 | tf_op jit(solution)/shard_map/all_to_all | solution.py:700
  41.8 15.3 %copy-start = (s32[1,2,128]{2,1,0:T(2,128)S(1)}, s32[1,2,128]{2,1,0:T(2,128)}, u32[]{:S(2)}) copy-start(s32[1,2,128]{2,1,0:T(2,128)} %param.12) | copy-start | bytes 3076
  51.4 12.2 %collective-permute-start.2 = (bf16[4,128,256]{2,1,0:T(8,128)(2,1)S(1)}, bf16[4,128,256]{2,1,0:T(8,128)(2,1)S(1)}, u32[]{:S(2)}, u32[]{:S(2)}) collective-permute-start(bf16[4,128,256]{2,1,0:T(8,128)(2,1)S(1)} %get-tuple-element.47), channel_id=1, source_target_pairs={{0,1},{1,0},{2,3},{3,2},{4,5},{5,4},{6,7},{7,6},{8,9},{9,8},{10,11... | collective-permute-start | bytes 786440 | tf_op jit(solution)/shard_map/ppermute | solution.py:22
  51.7 11.9 %collective-permute-start.3 = (bf16[4,128,256]{2,1,0:T(8,128)(2,1)S(1)}, bf16[4,128,256]{2,1,0:T(8,128)(2,1)S(1)}, u32[]{:S(2)}, u32[]{:S(2)}) collective-permute-start(bf16[4,128,256]{2,1,0:T(8,128)(2,1)S(1)} %get-tuple-element.48), channel_id=1, source_target_pairs={{0,31},{1,2},{2,1},{3,4},{4,3},{5,6},{6,5},{7,8},{8,7},{9,10},{10,... | collective-permute-start | bytes 786440 | tf_op jit(solution)/shard_map/ppermute | solution.py:22

commit v6 on v5

--- a/solution.py
+++ b/solution.py
@@ -97,8 +97,8 @@
     small = pltpu.make_async_copy(rows_hbm, rows_ref, arrived.at[parts])
     copies = [pltpu.make_async_copy(x_hbm.at[k], x_ref.at[k], arrived.at[k]) for k in range(parts)]
     later = pltpu.make_async_copy(slots_hbm, slots_ref, arrived.at[parts + 1])
-    for copy in [small] + copies + [later]:
-        copy.start()
+    for i, moved in enumerate([small] + copies + [later]):
+        moved.start(priority=i % 2)
     small.wait()
     pick = jnp.concatenate(
         [one_hot_rows(as_column(ids), nodes) for ids in partner_rows(rows_ref, odd_ref[0])], axis=0
@@ -571,7 +571,8 @@
     parts, nodes, _ = out_ref.shape
     patches, patch_nodes = pos_ref.shape
     core = nodes // patches
-    def load(k):
+    arriving = []
+    for k in range(parts):
         moves = [(bext_hbm.at[k, pl.ds(0, nodes)], bown_ref.at[k])]
         start = 0
         for a in pairs[half:]:
@@ -583,9 +584,7 @@
             here = pl.ds(start, a.shape[0])
             moves.append((a.at[:, k // 2, terms], local_ref.at[k, here]))
             start += a.shape[0]
-        return [copy(m[0], m[1], sems.at[k, i], i % 2) for i, m in enumerate(moves)]
-
-    arriving = {k: load(k) for k in range(2)}
+        arriving.append([copy(m[0], m[1], sems.at[k, i], int(k > 1)) for i, m in enumerate(moves)])
     slots = rows_ref.shape[1]
     for b, ids in enumerate(partner_rows(rows_ref, odd_ref[0])):
         back_ref[:, b * slots : (b + 1) * slots] = (
@@ -602,8 +601,6 @@
     for k in range(0, parts, 2):
         for moved in arriving[k] + arriving[k + 1]:
             moved.wait()
-        for later in range(k + 2, min(k + 4, parts)):
-            arriving[later] = load(later)
         total = dot(spread, beside([other_ref[k], other_ref[k + 1]]))
         cores = [
             dot(backs[p], beside([local_ref[k, p], local_ref[k + 1, p]])) for p in range(patches)

time: 66.4 us -> 66.6 us (level)
  transfers between devices with their start and end apart: 5 -> 5, of which waited for: 0 -> 0; matrix products, arithmetic and copies ran while one was open for 0% -> 0% of each run, Pallas kernels for 41% -> 40%
where the time goes in v6:
time: 66.6 us; the launch traced here: 66.3 us
  Pallas kernels  37.4 us (56%)
  starting transfers between devices  15.6 us (23%)
  blocking collectives  13 us (20%)
    pallas_call x9, Pallas kernels, call(): pl.pallas_call(kernel, in_specs=[pl.BlockSpec(memory_space=m) for m in sp...  37.4 us
    all_to_all x1, blocking collectives, per_device(): got = lax.all_to_all(sent, AXES, 0, 0, tiled=True)  13 us
    ppermute x4, starting transfers between devices, swapped(): return lax.ppermute(value, axis, sorted(partner.items()))  12.8 us
    all_to_all x1, starting transfers between devices, per_device(): mine = lax.all_to_all(sums, AXES, 0, 0, tiled=True)  2.8 us
  transfers between devices with their start and end apart: 5, of which 0 were waited for; matrix products, arithmetic and copies ran while one was open for 0% of the time, Pallas kernels for 40%

profile of v6, /device:TPU:0, one launch (start us, length us, event | category | flops | bytes accessed | tf_op | source)
XLA Modules:
  0.0 66.3 jit_solution(6038440226016622566)
XLA Ops:
  0.0 0.0 copy-start.1
  0.0 2.8 %shard_map.73 = (bf16[4,128,256]{2,1,0:T(8,128)(2,1)S(1)}, bf16[4,128,256]{2,1,0:T(8,128)(2,1)S(1)}, s32[4,512]{1,0:T(4,128)S(1)}) custom-call(s32[1]{0:T(128)} %bitcast.odd_ref, bf16[4,1536,256]{2,1,0:T(8,128)(2,1)} %bitcast.8, s32[2,128]{1,0:T(2,128)} %bitcast.6, s32[4,512]{1,0:T(4,128)} %slots_hbm.1), custom_call_target="tpu_custom_call" | custom-call | tf_op jit(solution)/shard_map/pallas_call | solution.py:66
  2.9 0.6 collective-permute-start
  3.4 6.6 %collective-permute-start.1 = (bf16[4,128,256]{2,1,0:T(8,128)(2,1)S(1)}, bf16[4,128,256]{2,1,0:T(8,128)(2,1)S(1)}, u32[]{:S(2)}, u32[]{:S(2)}) collective-permute-start(bf16[4,128,256]{2,1,0:T(8,128)(2,1)S(1)} %get-tuple-element.34), channel_id=1, source_target_pairs={{0,31},{1,2},{2,1},{3,4},{4,3},{5,6},{6,5},{7,8},{8,7},{9,10},{10,... | collective-permute-start | bytes 786440 | tf_op jit(solution)/shard_map/ppermute | solution.py:22
  10.0 5.7 %shard_map.74 = (bf16[512,256]{1,0:T(8,128)(2,1)}, bf16[4,512,256]{2,1,0:T(8,128)(2,1)}, bf16[4,1792,128]{2,1,0:T(8,128)(2,1)}, f32[4,512]{1,0:T(4,128)S(1)}, f3...) custom-call(s32[1]{0:T(128)} %bitcast.1.place_ref, ...), custom_call_target="tpu_custom_call" | custom-call | tf_op jit(solution)/shard_map/pallas_call | solution.py:66
  15.7 0.0 collective-permute-done.near_ref
  15.7 0.0 collective-permute-done.1.other_ref
  15.7 0.0 copy-done.1
  15.7 1.9 %shard_map.75 = (bf16[4,256,256]{2,1,0:T(8,128)(2,1)}, bf16[32,24,128]{2,1,0:T(8,128)(2,1)}) custom-call(s32[4]{0:T(128)S(1)} %copy-done.1, s32[1]{0:T(128)} %bitcast.odd_ref, f32[2,128,256]{2,1,0:T(8,128)S(1)} %get-tuple-element.31.r_ref, bf16[4,128,256]{2,1,0:T(8,128)(2,1)S(1)} %get-tuple-element.32.btrem_ref, ...), custom_call_target="tpu_custom_call" | custom-call | tf_op jit(solution)/shard_map/pallas_call | solution.py:66
  17.7 13.0 %all_to_all.10.got_ref = bf16[32,24,128]{2,1,0:T(8,128)(2,1)S(1)} all-to-all(bf16[32,24,128]{2,1,0:T(8,128)(2,1)} %get-tuple-element.43), channel_id=1, replica_groups=mesh['patch'=8,'coarse'=4] {'patch','coarse'}, dimensions={0} | all-to-all | bytes 393216 | tf_op jit(solution)/shard_map/all_to_all | solution.py:694
  30.7 1.3 %shard_map.78 = bf16[32,24,128]{2,1,0:T(8,128)(2,1)} custom-call(bf16[32,24,128]{2,1,0:T(8,128)(2,1)S(1)} %all_to_all.10.got_ref), custom_call_target="tpu_custom_call" | custom-call | tf_op jit(solution)/shard_map/pallas_call | solution.py:66
  32.0 2.8 %all-to-all-start.1 = ((bf16[32,24,128]{2,1,0:T(8,128)(2,1)}), bf16[32,24,128]{2,1,0:T(8,128)(2,1)S(1)}, u32[]{:S(2)}, u32[]{:S(2)}) async-start(bf16[32,24,128]{2,1,0:T(8,128)(2,1)} %shard_map.78), calls=%async_computation.1 | async-start | bytes 393216 | tf_op jit(solution)/shard_map/all_to_all | solution.py:697
  34.8 7.2 %shard_map.77 = (bf16[2,2,1024,256]{3,2,1,0:T(8,128)(2,1)}, bf16[4,256,256]{2,1,0:T(8,128)(2,1)}) custom-call(bf16[4,2,1024,1024]{3,2,1,0:T(8,128)(2,1)} %inv_hbm.5, bf16[4,1536,256]{2,1,0:T(8,128)(2,1)} %bitcast.10, bf16[4,512,256]{2,1,0:T(8,128)(2,1)} %get-tuple-element.29.y_hbm, bf16[512,256]{1,0:T(8,128)(2,1)} %get-tuple-element.30.crem_hbm, ...), custom_call_target="tpu_custom_call" | custom-call | tf_op jit(solution)/shard_map/pallas_call | solution.py:66
  42.0 0.0 copy-start
  42.0 7.3 %shard_map.76 = (bf16[2,2,1024,256]{3,2,1,0:T(8,128)(2,1)}, bf16[4,256,256]{2,1,0:T(8,128)(2,1)}) custom-call(bf16[4,2,1024,1024]{3,2,1,0:T(8,128)(2,1)} %inv_hbm.5, bf16[4,1536,256]{2,1,0:T(8,128)(2,1)} %bitcast.11, bf16[4,512,256]{2,1,0:T(8,128)(2,1)} %get-tuple-element.29.y_hbm, bf16[512,256]{1,0:T(8,128)(2,1)} %get-tuple-element.30.crem_hbm, ...), custom_call_target="tpu_custom_call" | custom-call | tf_op jit(solution)/shard_map/pallas_call | solution.py:66
  49.3 0.0 all-to-all-done.1.refs_2_
  49.3 2.3 %shard_map.79 = (bf16[2,128,256]{2,1,0:T(8,128)(2,1)S(1)}, bf16[4,128,256]{2,1,0:T(8,128)(2,1)S(1)}, bf16[4,128,256]{2,1,0:T(8,128)(2,1)S(1)}) custom-call(s32[1]{0:T(128)} %bitcast.odd_ref, bf16[4,1792,128]{2,1,0:T(8,128)(2,1)} %get-tuple-element.28.bext_hbm, bf16[4,256,256]{2,1,0:T(8,128)(2,1)} %get-tuple-element.40.refs_0_.refs_2_, ...), custom_call_target="tpu_custom_call" | custom-call | tf_op jit(solution)/shard_map/pallas_call | solution.py:66
  51.7 0.3 collective-permute-start.2
  52.0 5.3 %collective-permute-start.3 = (bf16[4,128,256]{2,1,0:T(8,128)(2,1)S(1)}, bf16[4,128,256]{2,1,0:T(8,128)(2,1)S(1)}, u32[]{:S(2)}, u32[]{:S(2)}) collective-permute-start(bf16[4,128,256]{2,1,0:T(8,128)(2,1)S(1)} %get-tuple-element.48), channel_id=1, source_target_pairs={{0,31},{1,2},{2,1},{3,4},{4,3},{5,6},{6,5},{7,8},{8,7},{9,10},{10,... | collective-permute-start | bytes 786440 | tf_op jit(solution)/shard_map/ppermute | solution.py:22
  57.3 0.0 copy-done
  57.3 6.5 %shard_map.80 = (f32[4,1536,256]{2,1,0:T(8,128)S(1)}, bf16[1536,256]{1,0:T(8,128)(2,1)S(1)}) custom-call(s32[1]{0:T(128)} %bitcast.odd_ref, bf16[4,1792,128]{2,1,0:T(8,128)(2,1)} %get-tuple-element.28.bext_hbm, bf16[2,2,1024,256]{3,2,1,0:T(8,128)(2,1)} %get-tuple-element.38.refs_0_, bf16[2,2,1024,256]{3,2,1,0:T(8,128)(2,1)} %get-tuple-element.39.refs_1_, ...), custom_call_target="tpu_custom_call" | custom-call | tf_op jit(solution)/shard_map/pallas_call | solution.py:66
  63.9 0.0 collective-permute-done.2.near_ref
  63.9 0.0 collective-permute-done.3.other_ref
  63.9 2.3 %shard_map.81 = bf16[4,1536,256]{2,1,0:T(8,128)(2,1)} custom-call(f32[4,1536,256]{2,1,0:T(8,128)S(1)} %get-tuple-element.45.own_ref, bf16[1536,256]{1,0:T(8,128)(2,1)S(1)} %get-tuple-element.46.spread_ref, bf16[4,128,256]{2,1,0:T(8,128)(2,1)S(1)} %collective-permute-done.2.near_ref, bf16[4,128,256]{2,1,0:T(8,128)(2,1)S(1)} %collective-permute-done.3.other_ref), custom_call_target="tpu_custom_call" | custom-call | tf_op jit(solution)/shard_map/pallas_call | solution.py:66
Async XLA Ops:
  0.0 15.7 %copy-start.1 = (s32[4]{0:T(128)S(1)}, s32[4]{0:T(128)}, u32[]{:S(2)}) copy-start(s32[4]{0:T(128)} %block_ref.1) | copy-start | bytes 52
  2.9 12.8 %collective-permute-start = (bf16[4,128,256]{2,1,0:T(8,128)(2,1)S(1)}, bf16[4,128,256]{2,1,0:T(8,128)(2,1)S(1)}, u32[]{:S(2)}, u32[]{:S(2)}) collective-permute-start(bf16[4,128,256]{2,1,0:T(8,128)(2,1)S(1)} %get-tuple-element.33), channel_id=1, source_target_pairs={{0,1},{1,0},{2,3},{3,2},{4,5},{5,4},{6,7},{7,6},{8,9},{9,8},{10,11... | collective-permute-start | bytes 786440 | tf_op jit(solution)/shard_map/ppermute | solution.py:22
  3.4 12.3 %collective-permute-start.1 = (bf16[4,128,256]{2,1,0:T(8,128)(2,1)S(1)}, bf16[4,128,256]{2,1,0:T(8,128)(2,1)S(1)}, u32[]{:S(2)}, u32[]{:S(2)}) collective-permute-start(bf16[4,128,256]{2,1,0:T(8,128)(2,1)S(1)} %get-tuple-element.34), channel_id=1, source_target_pairs={{0,31},{1,2},{2,1},{3,4},{4,3},{5,6},{6,5},{7,8},{8,7},{9,10},{10,... | collective-permute-start | bytes 786440 | tf_op jit(solution)/shard_map/ppermute | solution.py:22
  32.0 17.3 %all-to-all-start.1 = ((bf16[32,24,128]{2,1,0:T(8,128)(2,1)}), bf16[32,24,128]{2,1,0:T(8,128)(2,1)S(1)}, u32[]{:S(2)}, u32[]{:S(2)}) async-start(bf16[32,24,128]{2,1,0:T(8,128)(2,1)} %shard_map.78), calls=%async_computation.1 | async-start | bytes 393216 | tf_op jit(solution)/shard_map/all_to_all | solution.py:697
  42.0 15.3 %copy-start = (s32[1,2,128]{2,1,0:T(2,128)S(1)}, s32[1,2,128]{2,1,0:T(2,128)}, u32[]{:S(2)}) copy-start(s32[1,2,128]{2,1,0:T(2,128)} %param.12) | copy-start | bytes 3076
  51.7 12.2 %collective-permute-start.2 = (bf16[4,128,256]{2,1,0:T(8,128)(2,1)S(1)}, bf16[4,128,256]{2,1,0:T(8,128)(2,1)S(1)}, u32[]{:S(2)}, u32[]{:S(2)}) collective-permute-start(bf16[4,128,256]{2,1,0:T(8,128)(2,1)S(1)} %get-tuple-element.47), channel_id=1, source_target_pairs={{0,1},{1,0},{2,3},{3,2},{4,5},{5,4},{6,7},{7,6},{8,9},{9,8},{10,11... | collective-permute-start | bytes 786440 | tf_op jit(solution)/shard_map/ppermute | solution.py:22
  52.0 11.9 %collective-permute-start.3 = (bf16[4,128,256]{2,1,0:T(8,128)(2,1)S(1)}, bf16[4,128,256]{2,1,0:T(8,128)(2,1)S(1)}, u32[]{:S(2)}, u32[]{:S(2)}) collective-permute-start(bf16[4,128,256]{2,1,0:T(8,128)(2,1)S(1)} %get-tuple-element.48), channel_id=1, source_target_pairs={{0,31},{1,2},{2,1},{3,4},{4,3},{5,6},{6,5},{7,8},{8,7},{9,10},{10,... | collective-permute-start | bytes 786440 | tf_op jit(solution)/shard_map/ppermute | solution.py:22
